TPU v7x, 32 devices: a whole 2x2x4 slice. The times are simulated.
32 devices in a mesh: rep: 8 (over y, x, core), fsdp: 4 (over z).
Axes of the slice: x: 2, y: 2, z: 4, core: 2. Of those that a mesh axis runs over, the one named last changes fastest.
Arguments:
- inputs: bfloat16 [24576, 768], P(('rep', 'fsdp')), may hold values from -6 to 6
- first_values: bfloat16 [24576, 384], P(('rep', 'fsdp')), may hold values from -6 to 6
- cotangent: bfloat16 [24576, 768], P(('rep', 'fsdp')), may hold values from -6 to 6
- tree_ids: int32 [24576], P('rep'), may hold values from 0 to 2, as said below
- segment_ids: int32 [24576], P('rep'), may hold values from 0 to 12, as said below
- path_table: int32 [24, 13, 3], P('rep'), may hold values from 0 to 12, as said below
- attn_gain: bfloat16 [768], P('fsdp'), may hold values from 0.5 to 1.5
- attn_shift: bfloat16 [768], P('fsdp'), may hold values from -3 to 3
- w_query: bfloat16 [768, 768], P('fsdp'), may hold values from -0.21875 to 0.21875
- w_key: bfloat16 [768, 768], P('fsdp'), may hold values from -0.21875 to 0.21875
- w_value: bfloat16 [768, 384], P('fsdp'), may hold values from -0.21875 to 0.21875
- w_out: bfloat16 [768, 768], P('fsdp'), may hold values from -1.75 to 1.75
- mlp_gain: bfloat16 [768], P('fsdp'), may hold values from 0.5 to 1.5
- mlp_shift: bfloat16 [768], P('fsdp'), may hold values from -3 to 3
- w_in: bfloat16 [768, 3072], P('fsdp'), may hold values from -0.21875 to 0.21875
- w_down: bfloat16 [3072, 768], P('fsdp'), may hold values from -0.109375 to 0.109375
Outputs:
- outputs: bfloat16 [24576, 768], P(('rep', 'fsdp'))
- input_grad: float32 [24576, 768], P(('rep', 'fsdp'))
- first_values_grad: float32 [24576, 384], P(('rep', 'fsdp'))
- attn_gain_grad: float32 [768], P('fsdp')
- attn_shift_grad: float32 [768], P('fsdp')
- w_query_grad: float32 [768, 768], P('fsdp')
- w_key_grad: float32 [768, 768], P('fsdp')
- w_value_grad: float32 [768, 384], P('fsdp')
- w_out_grad: float32 [768, 768], P('fsdp')
- mlp_gain_grad: float32 [768], P('fsdp')
- mlp_shift_grad: float32 [768], P('fsdp')
- w_in_grad: float32 [768, 3072], P('fsdp')
- w_down_grad: float32 [3072, 768], P('fsdp')
Inputs may be any that keep to these rules, and one draw needn't show every extreme that they name: `tree_ids`: within each aligned block of 3072 tokens every tree number 0 to 2 covers exactly one aligned run of 1024 consecutive tokens. `segment_ids`: each tree's tokens are its trunk (segment 0, 512 tokens), then 4 branches of 64 tokens numbered 1 to 4 in some order, then 4 * 2 leaves of 32 tokens numbered 4 + 1 and up in some order. `path_table`: row t, s lists the trunk, the branch and the leaf on the path to segment s of tree t, repeating the segment itself where it is shallower; every branch is the parent of 2 leaves. Tree t of group r is row r * 3 + t.
All inputs are finite; a program needn't handle non-finite values.
Results may differ from a plain program's by a relative error of at most 0.013.
Values may be sent and summed in bfloat16 or wider, within the bound.
A program may use at most 192 MiB of HBM per device.

v0:
```python
import jax
import jax.numpy as jnp
from jax import lax
from jax.sharding import PartitionSpec as P

HEAD = 64
TREE_LEN = 1024


epsilon = 1e-05
far_below = -1e30


def shifted(block, axis, distance):
    devices = range(lax.axis_size(axis))
    route = [(i - distance, i) for i in devices if i - distance in devices]
    return lax.ppermute(block, axis, route)


def affine_norm(values_in, gain_vec, shift_vec):
    center = values_in - jnp.mean(values_in, axis=1, keepdims=True)
    spread = jnp.mean(center * center, axis=1, keepdims=True)
    return center * lax.rsqrt(spread + epsilon) * gain_vec + shift_vec


def gelu_tanh(values_in):
    return jax.nn.gelu(values_in, approximate=True)


def path_rows(tree_ids, segment_ids, path_table):
    seg_count = path_table.shape[1]
    flat_table = path_table.reshape(-1, 3)
    lookup = tree_ids * seg_count + segment_ids
    onehot = (lookup[:, None] == jnp.arange(flat_table.shape[0], dtype=jnp.int32)[None, :]).astype(
        jnp.int32
    )
    return jnp.sum(onehot[:, :, None] * flat_table[None, :, :], axis=1)


def visible_mask(tree_ids, segment_ids, path_table, row_start, row_count, key_start, window_len):
    paths = path_rows(tree_ids, segment_ids, path_table)
    query_tree = lax.dynamic_slice_in_dim(tree_ids, row_start, row_count, 0)
    query_path = lax.dynamic_slice_in_dim(paths, row_start, row_count, 0)
    query_pos = row_start + jnp.arange(row_count, dtype=jnp.int32)
    key_pos = key_start + jnp.arange(window_len, dtype=jnp.int32)
    inside = key_pos >= 0
    safe_pos = jnp.clip(key_pos, 0, tree_ids.shape[0] - 1)
    key_tree = jnp.take(tree_ids, safe_pos)
    key_seg = jnp.take(segment_ids, safe_pos)
    same_tree = query_tree[:, None] == key_tree[None, :]
    earlier = key_pos[None, :] <= query_pos[:, None]
    on_path = (
        (key_seg[None, :] == query_path[:, 0:1])
        | (key_seg[None, :] == query_path[:, 1:2])
        | (key_seg[None, :] == query_path[:, 2:3])
    )
    return inside[None, :] & same_tree & earlier & on_path


def pair_slice(block, pair_index):
    return lax.dynamic_slice_in_dim(block, pair_index * 2 * HEAD, 2 * HEAD, 1).reshape(
        block.shape[0], 2, HEAD
    )


def pair_scores(query_pair, key_pair, visible):
    scores = jnp.einsum(
        "qhd,khd->hqk", query_pair, key_pair, preferred_element_type=jnp.float32
    ) * HEAD ** (-0.5)
    return jnp.where(visible[None, :, :], scores, far_below)


def reorder_rows(grad_block, fsdp_count, rep_count):
    return grad_block.reshape(fsdp_count, rep_count, -1).transpose(1, 0, 2).reshape(-1)


def fetch_earlier(both_rows, distance):
    return shifted(both_rows, "fsdp", distance)


def return_earlier(grad_rows, distance):
    return shifted(grad_rows.astype(jnp.bfloat16), "fsdp", -distance).astype(grad_rows.dtype)


def on_device(
    inputs,
    first_values,
    cotangent,
    tree_ids,
    segment_ids,
    path_table,
    attn_gain,
    attn_shift,
    w_query,
    w_key,
    w_value,
    w_out,
    mlp_gain,
    mlp_shift,
    w_in,
    w_down,
):
    row_count, feat_width = inputs.shape
    scale = HEAD ** (-0.5)
    fsdp_count = lax.axis_size("fsdp")
    reach = 0
    for device_pos in range(fsdp_count):
        offset = device_pos * row_count % TREE_LEN
        reach = max(reach, (offset + row_count - 1) // row_count)
    window_len = (reach + 1) * row_count
    row_start = lax.axis_index("fsdp") * row_count
    gain1, shift1, query_w, key_w, value_w, out_w = (
        lax.all_gather(attn_gain, "fsdp", axis=0, tiled=True),
        lax.all_gather(attn_shift, "fsdp", axis=0, tiled=True),
        lax.all_gather(w_query, "fsdp", axis=0, tiled=True),
        lax.all_gather(w_key, "fsdp", axis=0, tiled=True),
        lax.all_gather(w_value, "fsdp", axis=0, tiled=True),
        lax.all_gather(w_out, "fsdp", axis=0, tiled=True),
    )
    resid_in = inputs.astype(jnp.float32)
    normed1_f, norm1_back = jax.vjp(
        affine_norm, resid_in, gain1.astype(jnp.float32), shift1.astype(jnp.float32)
    )
    normed1 = normed1_f.astype(jnp.bfloat16)
    queries = jnp.dot(normed1, query_w, preferred_element_type=jnp.float32).astype(jnp.bfloat16)
    key_rows = jnp.dot(normed1, key_w, preferred_element_type=jnp.float32).astype(jnp.bfloat16)
    fresh = jnp.dot(normed1, value_w, preferred_element_type=jnp.float32).astype(jnp.bfloat16)
    value_rows = jnp.concatenate([fresh, first_values], axis=1)
    both_rows = jnp.concatenate([key_rows, value_rows], axis=1)
    near_parts = []
    for distance in range(reach, 0, -1):
        near_parts.append(fetch_earlier(both_rows, distance))
    near_parts.append(both_rows)
    window_rows = jnp.concatenate(near_parts, axis=0)
    win_keys = window_rows[:, :feat_width]
    win_values = window_rows[:, feat_width:]
    key_start = row_start - reach * row_count
    visible = visible_mask(
        tree_ids, segment_ids, path_table, row_start, row_count, key_start, window_len
    )
    head_count = feat_width // HEAD
    pair_count = head_count // 2

    def forward_pair(pair_index, carry):
        mixed_acc, lse_acc = carry
        query_pair = pair_slice(queries, pair_index)
        key_pair = pair_slice(win_keys, pair_index)
        value_pair = pair_slice(win_values, pair_index)
        scores = pair_scores(query_pair, key_pair, visible)
        row_max = jnp.max(scores, axis=2, keepdims=True)
        expo = jnp.exp(scores - row_max)
        denom_sum = jnp.sum(expo, axis=2, keepdims=True)
        probs = expo / denom_sum
        lse_pair = (row_max + jnp.log(denom_sum))[:, :, 0]
        weights_b = probs.astype(jnp.bfloat16)
        pair_out = jnp.einsum(
            "hqk,khd->qhd", weights_b, value_pair, preferred_element_type=jnp.float32
        )
        pair_out = pair_out.reshape(row_count, 2 * HEAD).astype(jnp.bfloat16)
        mixed_acc = lax.dynamic_update_slice_in_dim(mixed_acc, pair_out, pair_index * 2 * HEAD, 1)
        lse_acc = lax.dynamic_update_slice_in_dim(lse_acc, lse_pair, pair_index * 2, 0)
        return (mixed_acc, lse_acc)

    mixed, lse_all = lax.fori_loop(
        0,
        pair_count,
        forward_pair,
        (
            jnp.zeros((row_count, feat_width), jnp.bfloat16),
            jnp.zeros((head_count, row_count), jnp.float32),
        ),
    )
    resid = resid_in + jnp.dot(mixed, out_w, preferred_element_type=jnp.float32)
    gain2, shift2, inner_w, down_w = (
        lax.all_gather(mlp_gain, "fsdp", axis=0, tiled=True),
        lax.all_gather(mlp_shift, "fsdp", axis=0, tiled=True),
        lax.all_gather(w_in, "fsdp", axis=0, tiled=True),
        lax.all_gather(w_down, "fsdp", axis=0, tiled=True),
    )
    normed2_f, norm2_back = jax.vjp(
        affine_norm, resid, gain2.astype(jnp.float32), shift2.astype(jnp.float32)
    )
    normed2 = normed2_f.astype(jnp.bfloat16)
    act = jnp.dot(normed2, inner_w, preferred_element_type=jnp.float32)
    hidden_f, gelu_back = jax.vjp(gelu_tanh, act)
    hidden = hidden_f.astype(jnp.bfloat16)
    outputs = (resid + jnp.dot(hidden, down_w, preferred_element_type=jnp.float32)).astype(
        jnp.bfloat16
    )
    grad_hidden = jnp.dot(cotangent, down_w.T, preferred_element_type=jnp.float32)
    down_grad = jnp.dot(hidden.T, cotangent, preferred_element_type=jnp.float32)
    grad_act = gelu_back(grad_hidden)[0].astype(jnp.bfloat16)
    inner_grad = jnp.dot(normed2.T, grad_act, preferred_element_type=jnp.float32)
    grad_normed2 = jnp.dot(grad_act, inner_w.T, preferred_element_type=jnp.float32)
    grad_ln2, gain2_grad, shift2_grad = norm2_back(grad_normed2)
    grad_resid = cotangent.astype(jnp.float32) + grad_ln2
    grad_branch = grad_resid.astype(jnp.bfloat16)
    out_grad = jnp.dot(mixed.T, grad_branch, preferred_element_type=jnp.float32)
    grad_mixed = jnp.dot(grad_branch, out_w.T, preferred_element_type=jnp.float32).astype(
        jnp.bfloat16
    )

    def backward_pair(pair_index, carry):
        query_acc, key_acc, value_acc = carry
        query_pair = pair_slice(queries, pair_index)
        key_pair = pair_slice(win_keys, pair_index)
        value_pair = pair_slice(win_values, pair_index)
        grad_pair = pair_slice(grad_mixed, pair_index)
        scores = pair_scores(query_pair, key_pair, visible)
        lse_pair = lax.dynamic_slice_in_dim(lse_all, pair_index * 2, 2, 0)
        probs = jnp.exp(scores - lse_pair[:, :, None])
        weights_b = probs.astype(jnp.bfloat16)
        grad_weights = jnp.einsum(
            "qhd,khd->hqk", grad_pair, value_pair, preferred_element_type=jnp.float32
        )
        inner_sum = jnp.sum(probs * grad_weights, axis=2, keepdims=True)
        grad_scores = (probs * (grad_weights - inner_sum)).astype(jnp.bfloat16)
        query_part = (
            jnp.einsum("hqk,khd->qhd", grad_scores, key_pair, preferred_element_type=jnp.float32)
            * scale
        )
        key_part = (
            jnp.einsum("hqk,qhd->khd", grad_scores, query_pair, preferred_element_type=jnp.float32)
            * scale
        )
        value_part = jnp.einsum(
            "hqk,qhd->khd", weights_b, grad_pair, preferred_element_type=jnp.float32
        )
        query_acc = lax.dynamic_update_slice_in_dim(
            query_acc, query_part.reshape(row_count, 2 * HEAD), pair_index * 2 * HEAD, 1
        )
        key_acc = lax.dynamic_update_slice_in_dim(
            key_acc, key_part.reshape(window_len, 2 * HEAD), pair_index * 2 * HEAD, 1
        )
        value_acc = lax.dynamic_update_slice_in_dim(
            value_acc, value_part.reshape(window_len, 2 * HEAD), pair_index * 2 * HEAD, 1
        )
        return (query_acc, key_acc, value_acc)

    query_full, key_win, value_win = lax.fori_loop(
        0,
        pair_count,
        backward_pair,
        (
            jnp.zeros((row_count, feat_width), jnp.float32),
            jnp.zeros((window_len, feat_width), jnp.float32),
            jnp.zeros((window_len, feat_width), jnp.float32),
        ),
    )
    grad_window = jnp.concatenate([key_win, value_win], axis=1).reshape(
        reach + 1, row_count, 2 * feat_width
    )
    own_grad = grad_window[reach]
    for distance in range(1, reach + 1):
        own_grad = own_grad + return_earlier(grad_window[reach - distance], distance)
    key_total = own_grad[:, :feat_width]
    value_total = own_grad[:, feat_width:]
    half_width = feat_width // 2
    grad_queries = query_full.astype(jnp.bfloat16)
    grad_keys = key_total.astype(jnp.bfloat16)
    grad_fresh = value_total[:, :half_width].astype(jnp.bfloat16)
    first_grad = value_total[:, half_width:]
    query_grad = jnp.dot(normed1.T, grad_queries, preferred_element_type=jnp.float32)
    key_grad = jnp.dot(normed1.T, grad_keys, preferred_element_type=jnp.float32)
    value_grad = jnp.dot(normed1.T, grad_fresh, preferred_element_type=jnp.float32)
    grad_normed1 = (
        jnp.dot(grad_queries, query_w.T, preferred_element_type=jnp.float32)
        + jnp.dot(grad_keys, key_w.T, preferred_element_type=jnp.float32)
        + jnp.dot(grad_fresh, value_w.T, preferred_element_type=jnp.float32)
    )
    grad_ln1, gain1_grad, shift1_grad = norm1_back(grad_normed1)
    input_grad = grad_resid + grad_ln1
    norm_grads = jnp.stack([gain1_grad, shift1_grad, gain2_grad, shift2_grad], axis=1)
    partial_list = (norm_grads, query_grad, key_grad, value_grad, out_grad, inner_grad, down_grad)
    rep_count = lax.axis_size("rep")
    pieces = (
        lax.psum_scatter(
            reorder_rows(norm_grads, fsdp_count, rep_count),
            ("rep", "fsdp"),
            scatter_dimension=0,
            tiled=True,
        ),
        lax.psum_scatter(
            reorder_rows(query_grad, fsdp_count, rep_count),
            ("rep", "fsdp"),
            scatter_dimension=0,
            tiled=True,
        ),
        lax.psum_scatter(
            reorder_rows(key_grad, fsdp_count, rep_count),
            ("rep", "fsdp"),
            scatter_dimension=0,
            tiled=True,
        ),
        lax.psum_scatter(
            reorder_rows(value_grad, fsdp_count, rep_count),
            ("rep", "fsdp"),
            scatter_dimension=0,
            tiled=True,
        ),
        lax.psum_scatter(
            reorder_rows(out_grad, fsdp_count, rep_count),
            ("rep", "fsdp"),
            scatter_dimension=0,
            tiled=True,
        ),
        lax.psum_scatter(
            reorder_rows(inner_grad, fsdp_count, rep_count),
            ("rep", "fsdp"),
            scatter_dimension=0,
            tiled=True,
        ),
        lax.psum_scatter(
            reorder_rows(down_grad, fsdp_count, rep_count),
            ("rep", "fsdp"),
            scatter_dimension=0,
            tiled=True,
        ),
    )
    spread = (
        lax.all_gather(pieces[0].astype(jnp.bfloat16), "rep", axis=0, tiled=True).astype(
            jnp.float32
        ),
        lax.all_gather(pieces[1].astype(jnp.bfloat16), "rep", axis=0, tiled=True).astype(
            jnp.float32
        ),
        lax.all_gather(pieces[2].astype(jnp.bfloat16), "rep", axis=0, tiled=True).astype(
            jnp.float32
        ),
        lax.all_gather(pieces[3].astype(jnp.bfloat16), "rep", axis=0, tiled=True).astype(
            jnp.float32
        ),
        lax.all_gather(pieces[4].astype(jnp.bfloat16), "rep", axis=0, tiled=True).astype(
            jnp.float32
        ),
        lax.all_gather(pieces[5].astype(jnp.bfloat16), "rep", axis=0, tiled=True).astype(
            jnp.float32
        ),
        lax.all_gather(pieces[6].astype(jnp.bfloat16), "rep", axis=0, tiled=True).astype(
            jnp.float32
        ),
    )
    summed = tuple(
        (
            piece_sum.reshape((whole.shape[0] // fsdp_count,) + whole.shape[1:])
            for piece_sum, whole in zip(spread, partial_list)
        )
    )
    norm_shard = summed[0]
    return (
        outputs,
        input_grad,
        first_grad,
        norm_shard[:, 0],
        norm_shard[:, 1],
        summed[1],
        summed[2],
        summed[3],
        summed[4],
        norm_shard[:, 2],
        norm_shard[:, 3],
        summed[5],
        summed[6],
    )


def solution(mesh):
    placed = (
        P(("rep", "fsdp"), None),
        P(("rep", "fsdp"), None),
        P(("rep", "fsdp"), None),
        P("rep"),
        P("rep"),
        P("rep", None, None),
        P("fsdp"),
        P("fsdp"),
        P("fsdp", None),
        P("fsdp", None),
        P("fsdp", None),
        P("fsdp", None),
        P("fsdp"),
        P("fsdp"),
        P("fsdp", None),
        P("fsdp", None),
    )
    return jax.shard_map(
        on_device,
        mesh=mesh,
        in_specs=placed,
        out_specs=(
            P(("rep", "fsdp"), None),
            P(("rep", "fsdp"), None),
            P(("rep", "fsdp"), None),
            P("fsdp"),
            P("fsdp"),
            P("fsdp", None),
            P("fsdp", None),
            P("fsdp", None),
            P("fsdp", None),
            P("fsdp"),
            P("fsdp"),
            P("fsdp", None),
            P("fsdp", None),
        ),
        check_vma=False,
    )
```

profile of v0, /device:TPU:0, one launch (start us, length us, event | category | flops | bytes accessed | tf_op | source)
XLA Modules:
  0.0 1321.9 jit_solution(18333137715302261885)
XLA Ops:
  13.4 14.0 %all-reduce.13 = (bf16[768]{0:T(1024)(128)(2,1)S(1)}, bf16[768]{0:T(1024)(128)(2,1)S(1)}, bf16[768]{0:T(1024)(128)(2,1)S(1)}, bf16[768]{0:T(1024)(128)(2,1)S(1)}) all-reduce(bf16[768]{0:T(1024)(128)(2,1)S(1)} %dynamic-update-slice.1, bf16[768]{0:T(1024)(128)(2,1)S(1)} %dynamic-update-slice, ...), channel_id=1, replica_groups=mesh['rep'=8,'fsdp'=4] {'fsdp'}, use_global_device_ids=true, to_apply=%add.1 | all-reduce | flops 3072 | bytes 12288
  28.0 23.2 %all_gather.54 = bf16[768,384]{1,0:T(8,128)(2,1)S(1)} all-gather(bf16[192,384]{1,0:T(8,128)(2,1)S(1)} %copy-done.27), channel_id=1, replica_groups=mesh['rep'=8,'fsdp'=4] {'fsdp'}, dimensions={0}, use_global_device_ids=true | all-gather | bytes 737280 | tf_op jit(solution)/shard_map/all_gather | solution.py:117
  85.4 13.9 %all-gather.10.cloned.1.call-done = bf16[768,768]{1,0:T(8,128)(2,1)} async-done(((bf16[192,768]{1,0:T(8,128)(2,1)}), bf16[768,768]{1,0:T(8,128)(2,1)}) %all-gather.10.cloned.1.call-update) | async-done | bytes 1179664 | tf_op jit(solution)/shard_map/all_gather | solution.py:115
  104.5 43.7 %collective-permute-done = bf16[768,1536]{0,1:T(8,128)(2,1)} collective-permute-done((bf16[768,1536]{0,1:T(8,128)(2,1)}, bf16[768,1536]{0,1:T(8,128)(2,1)}, u32[]{:S(2)}, u32[]{:S(2)}) %collective-permute-start) | collective-permute-done | bytes 2359328 | tf_op jit(solution)/shard_map/ppermute | solution.py:17
  148.2 11.2 maximum_maximum_fusion
  162.6 87.1 %while.38 = (s32[]{:T(128)}, bf16[768,768]{0,1:T(8,128)(2,1)S(1)}, f32[12,768]{1,0:T(8,128)}, bf16[1536,768]{0,1:T(8,128)(2,1)}, bf16[768,768]{0,1:T(8,128)(2,1)...) while((s32[]{:T(128)}, bf16[768,768]{0,1:T(8,128)(2,1)S(1)}, ...), condition=%wide.region_6.8_spmd.clone, body=%wide.region_3.7_spmd.clone.sunk | while | flops 644184576 | bytes 36703076 | solution.py:164
  264.7 63.1 %all-gather.14.cloned.1.call-done = bf16[768,3072]{1,0:T(8,128)(2,1)} async-done(((bf16[192,3072]{1,0:T(8,128)(2,1)}), bf16[768,3072]{1,0:T(8,128)(2,1)}) %all-gather.14.cloned.1.call-update) | async-done | bytes 4718608 | tf_op jit(solution)/shard_map/all_gather | solution.py:177
  327.8 15.9 %fusion.18 = (bf16[768,3072]{1,0:T(8,128)(2,1)S(1)}, f32[768,3072]{1,0:T(8,128)}) fusion(f32[768,3072]{1,0:T(8,128)} %fusion.62, bf16[768,3072]{1,0:T(8,128)(2,1)} %all-gather.14.cloned.1.call-done, f32[768,768]{0,1:T(8,128)S(1)} %get-tuple-element.816, f32[768]{0:T(1024)} %convert_element_type.147, f32[768]{0:T(1024)} %convert_element_type.146, ...), kind=kOutput, calls=%fused_computation.43 | convolution fusion | flops 3674013696 | bytes 30683136 | tf_op jit(solution)/shard_map/dot_general | solution.py:184
  368.5 270.2 %while.39 = (s32[]{:T(128)}, bf16[768,768]{0,1:T(8,128)(2,1)S(1)}, f32[1536,768]{1,0:T(8,128)}, f32[1536,768]{1,0:T(8,128)}, bf16[1536,768]{0,1:T(8,128)(2,1)}, ...) while((s32[]{:T(128)}, bf16[768,768]{0,1:T(8,128)(2,1)S(1)}, ...), condition=%wide.region_13.15_spmd.clone, body=%wide.region_11.14_spmd.clone.sunk | while | flops 1543371264 | bytes 86377304 | solution.py:240
  390.3 9.5 multiply_convert_fusion.5
  435.4 9.5 multiply_convert_fusion.5
  480.3 9.5 multiply_convert_fusion.5
  525.3 9.5 multiply_convert_fusion.5
  570.3 9.5 multiply_convert_fusion.5
  615.2 9.5 multiply_convert_fusion.5
  665.0 8.8 fusion.47
  682.3 13.4 %copy.158 = f32[4,8,73728]{2,0,1:T(4,128)} copy(f32[4,8,73728]{2,1,0:T(8,128)} %reshape.364) | data formatting | bytes 18874368 | tf_op jit(solution)/shard_map/reshape | solution.py:74
  704.4 13.0 fusion.49
  725.5 13.4 %copy.157 = f32[4,8,73728]{2,0,1:T(4,128)} copy(f32[4,8,73728]{2,1,0:T(8,128)} %reshape.368) | data formatting | bytes 18874368 | tf_op jit(solution)/shard_map/reshape | solution.py:74
  784.9 437.1 %all-reduce.15 = (bf16[3072]{0:T(1024)(128)(2,1)}, bf16[589824]{0:T(1024)(128)(2,1)}, bf16[589824]{0:T(1024)(128)(2,1)}, bf16[294912]{0:T(1024)(128)(2,1)}, bf16...) all-reduce(f32[3072]{0:T(1024)} %reshape.345, ...), channel_id=2, replica_groups=mesh['rep'=8,'fsdp'=4] {'rep','fsdp'}, use_global_device_ids=true, to_apply=%region_20.22.clone | all-reduce | flops 6786048 | bytes 40716288
  1227.1 10.8 add_convert_fusion
  1251.9 11.9 all-reduce.4
  1264.7 10.3 all_gather.62
  1287.0 9.3 all_gather.64
  (438 shorter events, 534.1 us)
Async XLA Ops:
  7.2 45.3 %all-gather.8.cloned.1.call-start = ((), (), s32[]{:S(2)}) async-start(), calls=%async_computation | async-start | bytes 1474560 | tf_op jit(solution)/shard_map/all_gather | solution.py:116
  7.9 91.3 %all-gather.10.cloned.1.call-start = ((), (), s32[]{:S(2)}) async-start(), calls=%async_computation.1 | async-start | bytes 1474560 | tf_op jit(solution)/shard_map/all_gather | solution.py:115
  8.7 241.1 %all-gather.12.cloned.1.call-start = ((), (), s32[]{:S(2)}) async-start(), calls=%async_computation.2 | async-start | bytes 1474560 | tf_op jit(solution)/shard_map/all_gather | solution.py:118
  9.5 246.6 %all-gather.16.cloned.1.call-start = ((), (), s32[]{:S(2)}) async-start(), calls=%async_computation.4 | async-start | bytes 5898240 | tf_op jit(solution)/shard_map/all_gather | solution.py:178
  10.0 317.8 %all-gather.14.cloned.1.call-start = ((), (), s32[]{:S(2)}) async-start(), calls=%async_computation.3 | async-start | bytes 5898240 | tf_op jit(solution)/shard_map/all_gather | solution.py:177
  10.4 17.6 %copy-start.27 = (bf16[192,384]{1,0:T(8,128)(2,1)S(1)}, bf16[192,384]{1,0:T(8,128)(2,1)}, u32[]{:S(2)}) copy-start(bf16[192,384]{1,0:T(8,128)(2,1)} %param.32) | copy-start | bytes 442372
  11.0 240.1 %copy-start.2 = (bf16[768,768]{0,1:T(8,128)(2,1)}, bf16[768,768]{0,1:T(8,128)(2,1)S(1)}, u32[]{:S(2)}) copy-start(bf16[768,768]{0,1:T(8,128)(2,1)S(1)} %copy.99) | copy-start | bytes 3538948
  27.4 71.9 %copy-start.51 = (f32[768]{0:T(1024)}, f32[768]{0:T(1024)S(1)}, u32[]{:S(2)}) copy-start(f32[768]{0:T(1024)S(1)} %convert_element_type.140) | copy-start | bytes 9220
  27.4 71.9 %copy-start.30 = (f32[768]{0:T(1024)}, f32[768]{0:T(1024)S(1)}, u32[]{:S(2)}) copy-start(f32[768]{0:T(1024)S(1)} %convert_element_type.139) | copy-start | bytes 9220
  27.6 71.6 %copy-start.28 = (f32[768]{0:T(1024)}, f32[768]{0:T(1024)S(1)}, u32[]{:S(2)}) copy-start(f32[768]{0:T(1024)S(1)} %broadcast_multiply_fusion.1) | copy-start | bytes 9220
  28.0 24.1 %copy-start.35 = (f32[768]{0:T(1024)}, f32[768]{0:T(1024)S(1)}, u32[]{:S(2)}) copy-start(f32[768]{0:T(1024)S(1)} %fusion.28) | copy-start | bytes 9220
  51.2 48.1 %copy-start.39 = (f32[768]{0:T(1024)}, f32[768]{0:T(1024)S(1)}, u32[]{:S(2)}) copy-start(f32[768]{0:T(1024)S(1)} %fusion.45) | copy-start | bytes 9220
  56.9 91.3 %collective-permute-start = (bf16[768,1536]{0,1:T(8,128)(2,1)}, bf16[768,1536]{0,1:T(8,128)(2,1)}, u32[]{:S(2)}, u32[]{:S(2)}) collective-permute-start(bf16[768,1536]{0,1:T(8,128)(2,1)} %pad_maximum_fusion), channel_id=1, source_target_pairs={{0,1},{1,2},{2,3},{4,5},{5,6},{6,7},{8,9},{9,10},{10,11},{12,13},{... | collective-permute-start | bytes 7077896 | tf_op jit(solution)/shard_map/ppermute | solution.py:17
  61.1 1247.1 %all-gather.18.cloned.1.call-start = ((), (), s32[]{:S(2)}) async-start(), calls=%async_computation.5 | async-start | bytes 1327104 | tf_op jit(solution)/shard_map/all_gather | solution.py:336
  61.4 9.1 copy-start.1
  70.5 8.4 copy-start.49
  253.9 102.2 %copy-start.4 = (f32[768,768]{0,1:T(8,128)}, f32[768,768]{0,1:T(8,128)S(1)}, u32[]{:S(2)}) copy-start(f32[768,768]{0,1:T(8,128)S(1)} %get-tuple-element.816) | copy-start | bytes 7077892
  327.8 15.9 %copy-start.55 = (bf16[768,3072]{1,0:T(8,128)(2,1)S(1)}, bf16[768,3072]{1,0:T(8,128)(2,1)}, u32[]{:S(2)}) copy-start(bf16[768,3072]{1,0:T(8,128)(2,1)} %all-gather.14.cloned.1.call-done) | copy-start | bytes 14155780
  638.7 12.8 copy-start.20
  649.0 99.8 %collective-permute-start.1 = (bf16[768,1536]{1,0:T(8,128)(2,1)}, bf16[768,1536]{1,0:T(8,128)(2,1)}, u32[]{:S(2)}, u32[]{:S(2)}) collective-permute-start(bf16[768,1536]{1,0:T(8,128)(2,1)} %slice.93), channel_id=1, source_target_pairs={{1,0},{2,1},{3,2},{5,4},{6,5},{7,6},{9,8},{10,9},{11,10},{13,12},{... | collective-permute-start | bytes 7077896 | tf_op jit(solution)/shard_map/ppermute | solution.py:17
  695.7 8.7 copy-start.19
  738.9 8.8 copy-start.21
  738.9 8.8 copy-start.57
  1223.6 87.7 %all-gather.20.cloned.1.call-start = ((), (), s32[]{:S(2)}) async-start(), calls=%async_computation.6 | async-start | bytes 1327104 | tf_op jit(solution)/shard_map/all_gather | solution.py:339
  (60 other events, 171.6 us)
Sparse Core Ops, SparseCore 0:
  9.6 42.8 all-gather.7
  54.0 45.1 all-gather.9
  100.8 46.3 all-gather.11
  148.7 89.7 all-gather.15
  239.9 87.8 all-gather.13
  1223.7 22.1 all-gather.17
  1247.8 24.5 all-gather.19
where the time goes:
time: 1330 us; the launch traced here: 1320 us
  blocking collectives  522 us (39%)
  matrix products  271 us (20%)
  local copies, waits for them, and re-layouts  220 us (17%)
  other arithmetic  161 us (12%)
  waiting for transfers between devices  124 us (9%)
  between operations  16.8 us (1%)
    unnamed x3, blocking collectives  463 us
    reshape x14, local copies, waits for them, and re-layouts, reorder_rows(): grad_block.reshape(fsdp_count, rep_count, -1).transpose(1, 0, 2).reshape(-1)  63.8 us
    dot_general x12, matrix products, pair_scores(): jnp.einsum('qhd,khd->hqk', query_pair, key_pair, preferred_element_type=j...  63.7 us
    all_gather x1, waiting for transfers between devices, on_device(): lax.all_gather(w_in, 'fsdp', axis=0, tiled=True)  63.1 us
    unnamed x159, local copies, waits for them, and re-layouts  58.6 us
    convert_element_type x6, other arithmetic, backward_pair(): grad_scores = (probs * (grad_weights - inner_sum)).astype(jnp.bfloat16)  56.7 us
    ppermute x2, waiting for transfers between devices, shifted(): return lax.ppermute(block, axis, route)  43.7 us
    and x12, other arithmetic, visible_mask(): return inside[None, :] & same_tree & earlier & on_path  42.9 us
  transfers between devices with their start and end apart: 9, of which 4 were waited for; matrix products, arithmetic and copies ran while one was open for 22% of the time, Pallas kernels for 0%

commit v1 on v0

--- a/solution.py
+++ b/solution.py
@@ -1,7 +1,265 @@
+import functools
+
 import jax
 import jax.numpy as jnp
 from jax import lax
+from jax.experimental import pallas as pl
+from jax.experimental.pallas import tpu as pltpu
 from jax.sharding import PartitionSpec as P
+
+MESH = pl.DeviceIdType.MESH
+
+class Place:
+    def __init__(self, fsdp):
+        self.fsdp = fsdp
+        r = lax.axis_index("rep")
+        self.f = lax.axis_index("fsdp")
+        self.k = lax.rem(r, 2)
+        self.x = lax.rem(r // 2, 2)
+        self.y = r // 4
+        def rid(y, x, k): return (y * 2 + x) * 2 + k
+        self.core = (rid(self.y, self.x, 1 - self.k), self.f)
+        self.xn = (rid(self.y, 1 - self.x, self.k), self.f)
+        self.yn = (rid(1 - self.y, self.x, self.k), self.f)
+        self.r = r
+        self.others = [lax.rem(self.f + j, fsdp) for j in range(1, fsdp)]
+    def zdev(self, fo): return (self.r, fo)
+    def barrier(self):
+        bar = pltpu.get_barrier_semaphore()
+        devs = [self.core, self.xn, self.yn] + [self.zdev(o) for o in self.others]
+        for d in devs:
+            pl.semaphore_signal(bar, inc=1, device_id=d, device_id_type=MESH)
+        pl.semaphore_wait(bar, len(devs))
+
+def drain(view, sem):
+    pltpu.make_async_copy(view, view, sem).wait()
+
+class Gather:
+    def __init__(self, pc, buf, send, recv, xfirst):
+        self.pc, self.buf, self.s, self.r, self.xf = pc, buf, send, recv, xfirst
+        self.H = buf.shape[-1] // 2
+        self.cols = pl.ds(pl.multiple_of(pc.k * self.H, 128), self.H)
+    def push(self, view, stage, dev):
+        pltpu.make_async_remote_copy(src_ref=view, dst_ref=view, send_sem=self.s.at[stage], recv_sem=self.r.at[stage], device_id=dev, device_id_type=MESH).start()
+    def z_start(self):
+        pc = self.pc
+        v = self.buf.at[pc.f, pc.y, pc.x, :, self.cols]
+        for o in pc.others: self.push(v, 0, pc.zdev(o))
+    def three(self): return self.buf.at[pl.ds(0, self.pc.fsdp - 1), 0, 0, :, self.cols]
+    def z_wait(self): drain(self.three(), self.r.at[0])
+    def a_start(self):
+        pc = self.pc
+        for o in pc.others:
+            v = self.buf.at[o, pc.y, pc.x, :, self.cols]
+            self.push(v, 1, pc.xn); self.push(v, 2, pc.yn)
+    def a_wait(self):
+        drain(self.three(), self.r.at[1]); drain(self.three(), self.r.at[2])
+    def b_start(self):
+        pc = self.pc
+        for o in pc.others:
+            if self.xf: self.push(self.buf.at[o, 1 - pc.y, pc.x, :, self.cols], 3, pc.xn)
+            else: self.push(self.buf.at[o, pc.y, 1 - pc.x, :, self.cols], 3, pc.yn)
+    def b_wait(self): drain(self.three(), self.r.at[3])
+    def c_start(self):
+        pc = self.pc
+        for o in pc.others: self.push(self.buf.at[o, :, :, :, self.cols], 4, pc.core)
+    def big(self): return self.buf.at[pl.ds(0, self.pc.fsdp - 1), :, :, :, self.cols]
+    def c_wait(self): drain(self.big(), self.r.at[4])
+    def finish(self):
+        for st in range(4): drain(self.three(), self.s.at[st])
+        drain(self.big(), self.s.at[4])
+
+def run_pipeline(items, stages):
+    n, d = len(items), len(stages)
+    for t in range(n + d - 1):
+        for s in range(d):
+            i = t - s
+            if 0 <= i < n: stages[s](items[i])
+
+GST = [lambda g: (g.z_wait(), g.a_start()), lambda g: (g.a_wait(), g.b_start()), lambda g: (g.b_wait(), g.c_start()), lambda g: g.c_wait()]
+
+def gather_kernel(fsdp, n_ff, qkv, wo, win, wdn, vec, oqkv, oo, oin, odn, ovec, lsem, ssem, rsem):
+    pc = Place(fsdp)
+    f = pc.f
+    loc = []
+    def local(src, dst):
+        c = pltpu.make_async_copy(src, dst, lsem.at[len(loc)]); c.start(); loc.append(c)
+    for j in range(2): local(qkv.at[:, :, :, pl.ds(j * 1024, 1024)], oqkv.at[j, f])
+    local(wo, oo.at[f])
+    W = win.shape[-1] // fsdp
+    for c in range(n_ff):
+        for g in range(fsdp): local(win.at[:, :, :, pl.ds(g * W + c * 128, 128)], oin.at[c, f, :, :, :, pl.ds(g * 128, 128)])
+        local(wdn.at[c], odn.at[c, f])
+    local(vec, ovec.at[f])
+    pc.barrier()
+    items, lc = [], []
+    def item(buf, xf, locs):
+        i = len(items)
+        items.append(Gather(pc, buf, ssem.at[i], rsem.at[i], xf)); lc.append(locs)
+    item(oqkv.at[0], True, loc[0:1]); item(oqkv.at[1], False, loc[1:2]); item(oo, True, loc[2:3])
+    p = 3
+    for c in range(n_ff):
+        item(oin.at[c], True, loc[p:p + fsdp]); p += fsdp
+        item(odn.at[c], False, loc[p:p + 1]); p += 1
+    loc[p].wait()
+    nv = len(items)
+    for o in pc.others:
+        pltpu.make_async_remote_copy(src_ref=ovec.at[f], dst_ref=ovec.at[f], send_sem=ssem.at[nv, 0], recv_sem=rsem.at[nv, 0], device_id=pc.zdev(o), device_id_type=MESH).start()
+    for it, l in zip(items, lc):
+        for c in l: c.wait()
+        it.z_start()
+    run_pipeline(items, GST)
+    v3 = ovec.at[pl.ds(0, fsdp - 1)]
+    drain(v3, rsem.at[nv, 0]); drain(v3, ssem.at[nv, 0])
+    for it in items: it.finish()
+
+def gather_call(fsdp, qkv, wo, win, wdn, vec):
+    d = qkv.shape[0]; m = d // 4
+    n_ff = wdn.shape[0] // 128
+    sh = lambda a: a.reshape(2, 2, m, a.shape[1])
+    bf = jnp.bfloat16
+    outs = (jax.ShapeDtypeStruct((2, fsdp, 2, 2, m, 1024), bf), jax.ShapeDtypeStruct((fsdp, 2, 2, m, wo.shape[1]), bf),
+            jax.ShapeDtypeStruct((n_ff, fsdp, 2, 2, m, fsdp * 128), bf), jax.ShapeDtypeStruct((n_ff, fsdp, 2, 2, 32, wdn.shape[1]), bf),
+            jax.ShapeDtypeStruct((fsdp, 8, vec.shape[1]), jnp.float32))
+    nit = 3 + 2 * n_ff
+    nloc = 4 + n_ff * (fsdp + 1)
+    any_ = pl.BlockSpec(memory_space=pl.ANY)
+    return pl.pallas_call(functools.partial(gather_kernel, fsdp, n_ff), out_shape=outs, in_specs=[any_] * 5, out_specs=[any_] * 5,
+        scratch_shapes=[pltpu.SemaphoreType.DMA((nloc,)), pltpu.SemaphoreType.DMA((nit + 1, 5)), pltpu.SemaphoreType.DMA((nit + 1, 5))],
+        compiler_params=pltpu.CompilerParams(collective_id=1, has_side_effects=True))(
+        sh(qkv), sh(wo), sh(win), wdn.reshape(n_ff, 2, 2, 32, -1), vec)
+
+class Reduce:
+    def __init__(self, pc, buf, r1, r2, r3, r4, res, send, recv, xfirst):
+        self.pc, self.buf, self.r1, self.r2, self.r3, self.r4, self.res = pc, buf, r1, r2, r3, r4, res
+        self.s, self.r, self.xf = send, recv, xfirst
+        self.H = H = buf.shape[-1] // 2
+        self.cols = pl.ds(pl.multiple_of(pc.k * H, 128), H)
+        self.ocols = pl.ds(pl.multiple_of((1 - pc.k) * H, 128), H)
+        self.F = buf.shape[0]
+    def send(self, src, dst, stage, dev):
+        pltpu.make_async_remote_copy(src_ref=src, dst_ref=dst, send_sem=self.s.at[stage], recv_sem=self.r.at[stage], device_id=dev, device_id_type=MESH).start()
+    def p1(self):
+        self.send(self.buf.at[:, :, :, :, self.ocols], self.r1, 0, self.pc.core)
+    def p2(self):
+        pc = self.pc
+        drain(self.r1, self.r.at[0])
+        @pl.loop(0, self.F * 4)
+        def _(i):
+            a, b, c = i // 4, lax.rem(i // 2, 2), lax.rem(i, 2)
+            self.r1[a, b, c] = (self.r1[a, b, c].astype(jnp.float32) + self.buf[a, b, c, :, self.cols].astype(jnp.float32)).astype(jnp.bfloat16)
+        if self.xf: self.send(self.r1.at[:, :, 1 - pc.x], self.r2, 1, pc.xn)
+        else: self.send(self.r1.at[:, 1 - pc.y], self.r2, 1, pc.yn)
+    def p3(self):
+        pc = self.pc
+        drain(self.r2, self.r.at[1])
+        @pl.loop(0, self.F * 2)
+        def _(i):
+            a, b = i // 2, lax.rem(i, 2)
+            mine = self.r1[a, b, pc.x] if self.xf else self.r1[a, pc.y, b]
+            self.r2[a, b] = (self.r2[a, b].astype(jnp.float32) + mine.astype(jnp.float32)).astype(jnp.bfloat16)
+        if self.xf: self.send(self.r2.at[:, 1 - pc.y], self.r3, 2, pc.yn)
+        else: self.send(self.r2.at[:, 1 - pc.x], self.r3, 2, pc.xn)
+    def p4(self):
+        pc = self.pc
+        drain(self.r3, self.r.at[2])
+        q = pc.y if self.xf else pc.x
+        @pl.loop(0, self.F)
+        def _(a):
+            self.r3[a] = (self.r3[a].astype(jnp.float32) + self.r2[a, q].astype(jnp.float32)).astype(jnp.bfloat16)
+        for o in pc.others: self.send(self.r3.at[o], self.r4.at[pc.f], 3, pc.zdev(o))
+    def p5(self):
+        pc = self.pc
+        drain(self.r4.at[pl.ds(0, self.F - 1)], self.r.at[3])
+        tot = self.r3[pc.f].astype(jnp.float32)
+        for o in pc.others: tot = tot + self.r4[o].astype(jnp.float32)
+        self.res[pc.y, pc.x, :, self.cols] = tot.astype(jnp.bfloat16)
+        v = self.res.at[pc.y, pc.x, :, self.cols]
+        self.send(v, v, 4, pc.xn); self.send(v, v, 5, pc.yn)
+    def p6(self):
+        pc = self.pc
+        v = self.res.at[0, 0, :, self.cols]
+        drain(v, self.r.at[4]); drain(v, self.r.at[5])
+        if self.xf:
+            v = self.res.at[1 - pc.y, pc.x, :, self.cols]; self.send(v, v, 6, pc.xn)
+        else:
+            v = self.res.at[pc.y, 1 - pc.x, :, self.cols]; self.send(v, v, 6, pc.yn)
+    def p7(self):
+        drain(self.res.at[0, 0, :, self.cols], self.r.at[6])
+        v = self.res.at[:, :, :, self.cols]
+        self.send(v, v, 7, self.pc.core)
+    def p8(self):
+        drain(self.res.at[:, :, :, self.cols], self.r.at[7])
+    def finish(self):
+        drain(self.r1, self.s.at[0]); drain(self.r2, self.s.at[1]); drain(self.r3, self.s.at[2])
+        drain(self.r4.at[pl.ds(0, self.F - 1)], self.s.at[3])
+        v = self.res.at[0, 0, :, self.cols]
+        for i in (4, 5, 6): drain(v, self.s.at[i])
+        drain(self.res.at[:, :, :, self.cols], self.s.at[7])
+    STAGES = None
+
+Reduce.STAGES = [Reduce.p1, Reduce.p2, Reduce.p3, Reduce.p4, Reduce.p5, Reduce.p6, Reduce.p7, Reduce.p8]
+
+def red_scratch(shape):
+    F, _, _, m, C = shape; H = C // 2; bf = jnp.bfloat16
+    return [pltpu.VMEM((F, 2, 2, m, H), bf), pltpu.VMEM((F, 2, m, H), bf), pltpu.VMEM((F, m, H), bf), pltpu.VMEM((F, m, H), bf)]
+
+def reduce_kernel(fsdp, n_ff, gqkv, go, gin, gdn, gvec, oq, oo, oi, od, ov, *scr):
+    pc = Place(fsdp)
+    bq, bo, bi, bd, rq, ro, ri, rd, vr, vz, lsem, ssem, rsem, vs, vrs = scr
+    srcs = [(gqkv.at[j], bq.at[j]) for j in range(2)] + [(go, bo)]
+    for c in range(n_ff): srcs += [(gin.at[c], bi.at[c]), (gdn.at[c], bd.at[c])]
+    cps = []
+    for i, (a, b) in enumerate(srcs):
+        c = pltpu.make_async_copy(a, b, lsem.at[i]); c.start(); cps.append(c)
+    pc.barrier()
+    def ex(src, dst, i, dev):
+        c = pltpu.make_async_remote_copy(src_ref=src, dst_ref=dst, send_sem=vs.at[i], recv_sem=vrs.at[i], device_id=dev, device_id_type=MESH); c.start(); return c
+    items = []
+    def item(buf, r, res, xf):
+        i = len(items)
+        items.append(Reduce(pc, buf, *r, res, ssem.at[i], rsem.at[i], xf))
+    item(bq.at[0], [a.at[0] for a in rq], oq.at[0], True); item(bq.at[1], [a.at[1] for a in rq], oq.at[1], False); item(bo, ro, oo, True)
+    for c in range(n_ff):
+        item(bi.at[c], [a.at[c] for a in ri], oi.at[c], True); item(bd.at[c], [a.at[c] for a in rd], od.at[c], False)
+    order = list(range(3, len(items))) + [2, 0, 1]
+    def first(i):
+        cps[i].wait(); items[i].p1()
+    run_pipeline(order, [first] + [(lambda i, p=p: p(items[i])) for p in Reduce.STAGES[1:]])
+    cur = gvec
+    for i, dev in enumerate((pc.core, pc.xn, pc.yn)):
+        c = ex(cur, vr.at[i], i, dev); c.wait()
+        vr[i] = vr[i] + cur[...]
+        cur = vr.at[i]
+    for o in pc.others: ex(cur, vz.at[pc.f], 3, pc.zdev(o))
+    v3 = vz.at[pl.ds(0, fsdp - 1)]
+    drain(v3, vrs.at[3]); drain(v3, vs.at[3])
+    vz[pc.f] = cur[...]
+    tot = vz[0]
+    for j in range(1, fsdp): tot = tot + vz[j]
+    ov[...] = tot
+    for it in items: it.finish()
+
+def reduce_call(fsdp, gqkv, go, gin, gdn, gvec):
+    bf = jnp.bfloat16
+    n_ff = gin.shape[0]
+    def stack(shape, lead): return [pltpu.VMEM((lead,) + tuple(s.inner_aval.shape if hasattr(s, "inner_aval") else s.shape), bf) for s in red_scratch(shape)]
+    outs = tuple(jax.ShapeDtypeStruct(s, bf) for s in (gqkv.shape[:1] + gqkv.shape[2:], go.shape[1:], gin.shape[:1] + gin.shape[2:], gdn.shape[:1] + gdn.shape[2:])) + (jax.ShapeDtypeStruct(gvec.shape, jnp.float32),)
+    nit = 3 + 2 * n_ff
+    any_ = pl.BlockSpec(memory_space=pl.ANY); vm = pl.BlockSpec(memory_space=pltpu.VMEM)
+    scr = [pltpu.VMEM(a.shape, bf) for a in (gqkv, go, gin, gdn)]
+    flat = scr + []
+    groups = [stack(gqkv.shape[1:], 2), red_scratch(go.shape), stack(gin.shape[1:], n_ff), stack(gdn.shape[1:], n_ff)]
+    D = pltpu.SemaphoreType.DMA
+    tail = [pltpu.VMEM((3,) + gvec.shape, jnp.float32), pltpu.VMEM((fsdp,) + gvec.shape, jnp.float32), D((nit,)), D((nit, 8)), D((nit, 8)), D((4,)), D((4,))]
+    def body(a, b, c, d, e, o1, o2, o3, o4, o5, *s):
+        base, rest = list(s[:4]), list(s[4:])
+        g = [rest[i * 4:(i + 1) * 4] for i in range(4)]
+        reduce_kernel(fsdp, n_ff, a, b, c, d, e, o1, o2, o3, o4, o5, *base, *g, *rest[16:])
+    return pl.pallas_call(body, out_shape=outs, in_specs=[any_] * 4 + [vm], out_specs=[vm] * 5,
+        scratch_shapes=flat + [x for g in groups for x in g] + tail,
+        compiler_params=pltpu.CompilerParams(collective_id=2, has_side_effects=True, vmem_limit_bytes=56 << 20))(gqkv, go, gin, gdn, gvec)
+
 
 HEAD = 64
 TREE_LEN = 1024
@@ -80,6 +338,59 @@
 
 def return_earlier(grad_rows, distance):
     return shifted(grad_rows.astype(jnp.bfloat16), "fsdp", -distance).astype(grad_rows.dtype)
+
+
+def packed_qkv(query, key, value):
+    h, pad = query.shape[1] * 2 // 3, jnp.zeros_like(value[:, : value.shape[1] // 3])
+    n = value.shape[1] * 2 // 3
+    return jnp.concatenate([query[:, :h], key[:, :h], query[:, h:], value[:, :n], key[:, h:], value[:, n:], pad], axis=1)
+
+
+def unpacked_qkv(first, second):
+    h = first.shape[-1] // 2
+    q = h // 2
+    return (
+        jnp.concatenate([first[..., :h], second[..., :q]], axis=-1),
+        jnp.concatenate([first[..., h:], second[..., h : h + q]], axis=-1),
+        jnp.concatenate([second[..., q:h], second[..., h + q : h + q + q // 2]], axis=-1),
+    )
+
+
+def gathered(fsdp, gain1, shift1, gain2, shift2, w_query, w_key, w_value, w_out, w_in, w_down):
+    rows, width = w_query.shape
+    vec = jnp.stack([gain1, shift1, gain2, shift2]).astype(jnp.float32)
+    vec = jnp.zeros((8, width), jnp.float32).at[:4, :rows].set(vec)
+    vec = jnp.roll(vec, lax.axis_index("fsdp") * rows, axis=1)
+    oq, oo, oi, od, ov = gather_call(fsdp, packed_qkv(w_query, w_key, w_value), w_out, w_in, w_down, vec)
+    vecs = jnp.sum(ov, axis=0).astype(jnp.bfloat16)
+    qkv = oq.reshape(2, width, -1)
+    query_w, key_w, value_w = unpacked_qkv(qkv[0], qkv[1])
+    n_ff = oi.shape[0]
+    inner = oi.reshape(n_ff, width, fsdp, 128).transpose(1, 2, 0, 3).reshape(width, -1)
+    down = od.reshape(n_ff, fsdp, 128, width).transpose(1, 0, 2, 3).reshape(-1, width)
+    return (*vecs[:4], query_w, key_w, value_w, oo.reshape(width, width), inner, down)
+
+
+def reduced(fsdp, g1, b1, g2, b2, dq, dk, dv, do, din, ddn):
+    width = dq.shape[0]
+    rows = width // fsdp
+    n_ff = din.shape[1] // (fsdp * 128)
+    bf = jnp.bfloat16
+    vec = jnp.zeros((8, width), jnp.float32).at[:4].set(jnp.stack([g1, b1, g2, b2]))
+    qkv = packed_qkv(dq, dk, dv).astype(bf)
+    qkv = qkv.reshape(width, 2, -1).transpose(1, 0, 2).reshape(2, fsdp, 2, 2, rows // 4, -1)
+    gin = din.astype(bf).reshape(width, fsdp, n_ff, 128).transpose(2, 0, 1, 3).reshape(n_ff, fsdp, 2, 2, rows // 4, -1)
+    gdn = ddn.astype(bf).reshape(fsdp, n_ff, 128, width).transpose(1, 0, 2, 3).reshape(n_ff, fsdp, 2, 2, 32, width)
+    rq, ro, ri, rd, rv = reduce_call(fsdp, qkv, do.astype(bf).reshape(fsdp, 2, 2, rows // 4, width), gin, gdn, vec)
+    rv = lax.dynamic_slice_in_dim(rv, lax.axis_index("fsdp") * rows, rows, 1)
+    f32 = jnp.float32
+    rq = rq.reshape(2, rows, -1)
+    q, k, v = unpacked_qkv(rq[0], rq[1])
+    ri = ri.reshape(n_ff, rows, fsdp, 128).transpose(1, 2, 0, 3).reshape(rows, -1)
+    return (
+        *rv[:4], q.astype(f32), k.astype(f32), v.astype(f32), ro.reshape(rows, width).astype(f32),
+        ri.astype(f32), rd.reshape(-1, width).astype(f32),
+    )
 
 
 def on_device(
@@ -109,14 +420,17 @@
         reach = max(reach, (offset + row_count - 1) // row_count)
     window_len = (reach + 1) * row_count
     row_start = lax.axis_index("fsdp") * row_count
-    gain1, shift1, query_w, key_w, value_w, out_w = (
-        lax.all_gather(attn_gain, "fsdp", axis=0, tiled=True),
-        lax.all_gather(attn_shift, "fsdp", axis=0, tiled=True),
-        lax.all_gather(w_query, "fsdp", axis=0, tiled=True),
-        lax.all_gather(w_key, "fsdp", axis=0, tiled=True),
-        lax.all_gather(w_value, "fsdp", axis=0, tiled=True),
-        lax.all_gather(w_out, "fsdp", axis=0, tiled=True),
-    )
+    rep_count = lax.axis_size("rep")
+    fast = rep_count == 8 and attn_gain.shape[0] % 64 == 0
+    if fast:
+        gain1, shift1, gain2, shift2, query_w, key_w, value_w, out_w, inner_w, down_w = gathered(
+            fsdp_count, attn_gain, attn_shift, mlp_gain, mlp_shift, w_query, w_key, w_value, w_out, w_in, w_down
+        )
+    else:
+        gain1, shift1, query_w, key_w, value_w, out_w, gain2, shift2, inner_w, down_w = (
+            lax.all_gather(v, "fsdp", axis=0, tiled=True)
+            for v in (attn_gain, attn_shift, w_query, w_key, w_value, w_out, mlp_gain, mlp_shift, w_in, w_down)
+        )
     resid_in = inputs.astype(jnp.float32)
     normed1_f, norm1_back = jax.vjp(
         affine_norm, resid_in, gain1.astype(jnp.float32), shift1.astype(jnp.float32)
@@ -171,12 +485,6 @@
         ),
     )
     resid = resid_in + jnp.dot(mixed, out_w, preferred_element_type=jnp.float32)
-    gain2, shift2, inner_w, down_w = (
-        lax.all_gather(mlp_gain, "fsdp", axis=0, tiled=True),
-        lax.all_gather(mlp_shift, "fsdp", axis=0, tiled=True),
-        lax.all_gather(w_in, "fsdp", axis=0, tiled=True),
-        lax.all_gather(w_down, "fsdp", axis=0, tiled=True),
-    )
     normed2_f, norm2_back = jax.vjp(
         affine_norm, resid, gain2.astype(jnp.float32), shift2.astype(jnp.float32)
     )
@@ -270,9 +578,13 @@
     )
     grad_ln1, gain1_grad, shift1_grad = norm1_back(grad_normed1)
     input_grad = grad_resid + grad_ln1
+    if fast:
+        g1, b1, g2, b2, dq, dk, dv, do, din, ddn = reduced(
+            fsdp_count, gain1_grad, shift1_grad, gain2_grad, shift2_grad, query_grad, key_grad, value_grad, out_grad, inner_grad, down_grad
+        )
+        return (outputs, input_grad, first_grad, g1, b1, dq, dk, dv, do, g2, b2, din, ddn)
     norm_grads = jnp.stack([gain1_grad, shift1_grad, gain2_grad, shift2_grad], axis=1)
     partial_list = (norm_grads, query_grad, key_grad, value_grad, out_grad, inner_grad, down_grad)
-    rep_count = lax.axis_size("rep")
     pieces = (
         lax.psum_scatter(
             reorder_rows(norm_grads, fsdp_count, rep_count),

time: 1330 us -> 873 us (0.66)
  blocking collectives: 522 us -> 0 us
  Pallas kernels: 0 us -> 289 us
  waiting for transfers between devices: 124 us -> 36.1 us
  matrix products: 271 us -> 190 us
  local copies, waits for them, and re-layouts: 220 us -> 194 us
  other arithmetic: 161 us -> 144 us
  between operations: 16.8 us -> 1.8 us
    unnamed x3 -> x0, blocking collectives: 463 us -> none
    pallas_call x0 -> x2, Pallas kernels: none -> 289 us  [the longest x1 177 us: gather_call(): pl.pallas_call(functools.partial(gather_kernel, fsdp, n_ff), out_shape=ou...]
    all_gather x7 -> x0, waiting for transfers between devices: 77.4 us -> none  [the longest x1 63.1 us: on_device(): lax.all_gather(w_in, 'fsdp', axis=0, tiled=True)]
    all_gather x5 -> x0, blocking collectives: 59.5 us -> none  [the longest x1 23.2 us: on_device(): lax.all_gather(w_value, 'fsdp', axis=0, tiled=True)]
    reshape x21 -> x9, local copies, waits for them, and re-layouts: 74.3 us -> 35.3 us  [the longest x2 16.1 us: gathered(): oi.reshape(n_ff, width, fsdp, 128).transpose(1, 2, 0, 3).reshape(width, -1)]
    unnamed x159 -> x152, local copies, waits for them, and re-layouts: 58.6 us -> 32.2 us
    dot_general x6, matrix products: 30.5 us -> 8.57 us  [backward_pair(): jnp.einsum('qhd,khd->hqk', grad_pair, value_pair, preferred_element_type=...]
    convert_element_type x0 -> x5, local copies, waits for them, and re-layouts: none -> 17.9 us  [the longest x1 6.64 us: reduced(): din.astype(bf).reshape(width, fsdp, n_ff, 128).transpose(2, 0, 1, 3)]
  transfers between devices with their start and end apart: 9 -> 2, of which waited for: 4 -> 2; matrix products, arithmetic and copies ran while one was open for 22% -> 8% of each run, Pallas kernels for 0% -> 0%
where the time goes in v1:
time: 873 us; the launch traced here: 865 us
  Pallas kernels  289 us (33%)
  local copies, waits for them, and re-layouts  194 us (22%)
  matrix products  190 us (22%)
  other arithmetic  144 us (16%)
  waiting for transfers between devices  36.1 us (4%)
    pallas_call x1, Pallas kernels, gather_call(): pl.pallas_call(functools.partial(gather_kernel, fsdp, n_ff), out_shape=ou...  177 us
    pallas_call x1, Pallas kernels, reduce_call(): pl.pallas_call(body, out_shape=outs, in_specs=[any_] * 4 + [vm], out_spec...  112 us
    convert_element_type x6, other arithmetic, backward_pair(): grad_scores = (probs * (grad_weights - inner_sum)).astype(jnp.bfloat16)  56.3 us
    dot_general x12, matrix products, pair_scores(): jnp.einsum('qhd,khd->hqk', query_pair, key_pair, preferred_element_type=j...  52.6 us
    dynamic_slice x42, local copies, waits for them, and re-layouts, pair_slice(): lax.dynamic_slice_in_dim(block, pair_index * 2 * HEAD, 2 * HEAD, 1)  37.2 us
    ppermute x2, waiting for transfers between devices, shifted(): return lax.ppermute(block, axis, route)  36.1 us
    and x12, other arithmetic, visible_mask(): return inside[None, :] & same_tree & earlier & on_path  32.3 us
    unnamed x152, local copies, waits for them, and re-layouts  32.2 us
  transfers between devices with their start and end apart: 2, of which 2 were waited for; matrix products, arithmetic and copies ran while one was open for 8% of the time, Pallas kernels for 0%

profile of v1, /device:TPU:0, one launch (start us, length us, event | category | flops | bytes accessed | tf_op | source)
XLA Modules:
  0.0 864.7 jit_solution(6585448004719851476)
XLA Ops:
  9.6 177.0 %shard_map.255 = (bf16[2,4,2,2,48,1024]{5,4,3,2,1,0:T(8,128)(2,1)}, bf16[4,2,2,48,768]{4,3,2,1,0:T(8,128)(2,1)}, bf16[6,4,2,2,48,512]{5,4,3,2,1,0:T(8,128)(2,1)}...) custom-call(bf16[2,2,48,2048]{3,2,1,0:T(8,128)(2,1)} %bitcast.191, bf16[2,2,48,768]{3,2,1,0:T(8,128)(2,1)} %bitcast.195, ...), custom_call_target="tpu_custom_call" | custom-call | tf_op jit(solution)/shard_map/pallas_call | solution.py:127
  208.0 8.4 gather_fusion
  216.4 8.4 gather_fusion.1
  233.2 7.7 reshape.390
  240.9 8.4 copy.82
  257.7 12.8 %maximum_maximum_fusion = bf16[1536,1536]{0,1:T(8,128)(2,1)S(1)} fusion(bf16[768,384]{0,1:T(8,128)(2,1)S(1)} %copy.79, bf16[768,384]{0,1:T(8,128)(2,1)} %copy-done.16, bf16[768,768]{0,1:T(8,128)(2,1)S(1)} %convolution_convert_fusion.7, bf16[768,1536]{0,1:T(8,128)(2,1)} %collective-permute-done), kind=kLoop, calls=%fused_computation.54 | loop fusion | flops 18874368 | bytes 9437184 | tf_op jit(solution)/shard_map/concatenate | solution.py:448
  273.0 79.6 %while.40 = (s32[]{:T(128)}, bf16[768,768]{0,1:T(8,128)(2,1)S(1)}, f32[12,768]{1,0:T(8,128)S(1)}, bf16[1536,768]{0,1:T(8,128)(2,1)}, bf16[768,768]{0,1:T(8,128)(...) while((s32[]{:T(128)}, bf16[768,768]{0,1:T(8,128)(2,1)S(1)}, ...), condition=%wide.region_7.9_spmd.clone, body=%wide.region_4.0_spmd.clone.sunk | while | flops 644184576 | bytes 36653868 | solution.py:478
  360.6 7.2 convolution_convert_fusion
  367.8 8.9 %fusion.18 = bf16[768,3072]{1,0:T(8,128)(2,1)S(1)} fusion(f32[768,3072]{1,0:T(8,128)S(1)} %fusion.71, bf16[3072,768]{1,0:T(8,128)(2,1)S(1)} %bitcast.178, bf16[768,768]{1,0:T(8,128)(2,1)S(1)} %copy-done.21), kind=kOutput, calls=%fused_computation.43 | convolution fusion | flops 3671064576 | bytes 20054016 | tf_op jit(solution)/shard_map/dot_general | solution.py:498
  387.8 6.6 copy.96
  394.4 8.5 copy.97
  402.9 8.0 reshape.397.c
  434.2 205.3 %while.41 = (s32[]{:T(128)}, bf16[768,768]{0,1:T(8,128)(2,1)}, f32[1536,768]{1,0:T(8,128)}, f32[1536,768]{1,0:T(8,128)}, bf16[1536,768]{0,1:T(8,128)(2,1)}, /*in...) while((s32[]{:T(128)}, bf16[768,768]{0,1:T(8,128)(2,1)}, ...), condition=%wide.region_14.16_spmd.clone, body=%wide.region_12.15_spmd.clone.sunk | while | flops 1543371264 | bytes 143000464 | solution.py:548
  442.4 6.5 multiply_reduce_fusion.6
  448.9 9.4 %multiply_convert_fusion.5 = bf16[2,768,1536]{2,1,0:T(8,128)(2,1)} fusion(f32[2,768,1536]{2,1,0:T(8,128)} %get-tuple-element.1040, f32[2,768,1536]{2,1,0:T(8,128)} %copy-done.2, f32[2,768]{1,0:T(2,128)S(1)} %get-tuple-element.1041), kind=kLoop, calls=%fused_computation.19.clone.1 | loop fusion | flops 7077888 | bytes 23599104 | tf_op jit(solution)/shard_map/while/body/eval_jaxpr/convert_element_type | solution.py:525
  483.2 9.4 %multiply_convert_fusion.5 = bf16[2,768,1536]{2,1,0:T(8,128)(2,1)} fusion(f32[2,768,1536]{2,1,0:T(8,128)} %get-tuple-element.1040, f32[2,768,1536]{2,1,0:T(8,128)} %copy-done.2, f32[2,768]{1,0:T(2,128)S(1)} %get-tuple-element.1041), kind=kLoop, calls=%fused_computation.19.clone.1 | loop fusion | flops 7077888 | bytes 23599104 | tf_op jit(solution)/shard_map/while/body/eval_jaxpr/convert_element_type | solution.py:525
  510.9 6.5 multiply_reduce_fusion.6
  517.4 9.4 %multiply_convert_fusion.5 = bf16[2,768,1536]{2,1,0:T(8,128)(2,1)} fusion(f32[2,768,1536]{2,1,0:T(8,128)} %get-tuple-element.1040, f32[2,768,1536]{2,1,0:T(8,128)} %copy-done.2, f32[2,768]{1,0:T(2,128)S(1)} %get-tuple-element.1041), kind=kLoop, calls=%fused_computation.19.clone.1 | loop fusion | flops 7077888 | bytes 23599104 | tf_op jit(solution)/shard_map/while/body/eval_jaxpr/convert_element_type | solution.py:525
  551.5 9.4 %multiply_convert_fusion.5 = bf16[2,768,1536]{2,1,0:T(8,128)(2,1)} fusion(f32[2,768,1536]{2,1,0:T(8,128)} %get-tuple-element.1040, f32[2,768,1536]{2,1,0:T(8,128)} %copy-done.2, f32[2,768]{1,0:T(2,128)S(1)} %get-tuple-element.1041), kind=kLoop, calls=%fused_computation.19.clone.1 | loop fusion | flops 7077888 | bytes 23599104 | tf_op jit(solution)/shard_map/while/body/eval_jaxpr/convert_element_type | solution.py:525
  585.7 9.4 %multiply_convert_fusion.5 = bf16[2,768,1536]{2,1,0:T(8,128)(2,1)} fusion(f32[2,768,1536]{2,1,0:T(8,128)} %get-tuple-element.1040, f32[2,768,1536]{2,1,0:T(8,128)} %copy-done.2, f32[2,768]{1,0:T(2,128)S(1)} %get-tuple-element.1041), kind=kLoop, calls=%fused_computation.19.clone.1 | loop fusion | flops 7077888 | bytes 23599104 | tf_op jit(solution)/shard_map/while/body/eval_jaxpr/convert_element_type | solution.py:525
  620.0 9.4 %multiply_convert_fusion.5 = bf16[2,768,1536]{2,1,0:T(8,128)(2,1)} fusion(f32[2,768,1536]{2,1,0:T(8,128)} %get-tuple-element.1040, f32[2,768,1536]{2,1,0:T(8,128)} %copy-done.2, f32[2,768]{1,0:T(2,128)S(1)} %get-tuple-element.1041), kind=kLoop, calls=%fused_computation.19.clone.1 | loop fusion | flops 7077888 | bytes 23599104 | tf_op jit(solution)/shard_map/while/body/eval_jaxpr/convert_element_type | solution.py:525
  649.5 9.5 %add_convert_fusion = bf16[768,768]{0,1:T(8,128)(2,1)} fusion(f32[768,768]{0,1:T(8,128)S(1)} %copy-done.8, bf16[3072,768]{1,0:T(8,128)(2,1)S(1)} %bitcast.181, f32[768,3072]{1,0:T(8,128)} %copy-done.58), kind=kOutput, calls=%fused_computation.78 | convolution fusion | flops 3646291968 | bytes 17694720 | tf_op jit(solution)/shard_map/dot_general | solution.py:495
  670.4 33.1 %collective-permute-done.1 = bf16[768,1536]{1,0:T(8,128)(2,1)} collective-permute-done((bf16[768,1536]{1,0:T(8,128)(2,1)S(1)}, bf16[768,1536]{1,0:T(8,128)(2,1)}, u32[]{:S(2)}, u32[]{:S(2)}) %collective-permute-start.1) | collective-permute-done | bytes 2359328 | tf_op jit(solution)/shard_map/ppermute | solution.py:275
  727.9 112.4 %shard_map.256 = (bf16[2,2,2,48,1024]{4,3,2,1,0:T(8,128)(2,1)}, bf16[2,2,48,768]{3,2,1,0:T(8,128)(2,1)}, bf16[6,2,2,48,512]{4,3,2,1,0:T(8,128)(2,1)}, bf16[6,2,2,32,768]{4,3,2,1,0:T(8,128)(2,1)}, f32[8,768]{1,0:T(8,128)}) custom-call(bf16[2,4,2,2,48,1024]{5,4,3,2,1,0:T(8,128)(2,1)} %bitcast.167, bf16[4,2,2,48,768]{4,3,2,1,0:T(8,128)(2,1)} %bitcast.192, ...), custom_call_target="tpu_custom_call" | custom-call | tf_op jit(solution)/shard_map/pallas_call | solution.py:259
  (415 shorter events, 375.5 us)
Async XLA Ops:
  188.9 8.3 copy-start.30
  192.0 160.7 %copy-start.4 = (bf16[768,768]{0,1:T(8,128)(2,1)}, bf16[768,768]{0,1:T(8,128)(2,1)S(1)}, u32[]{:S(2)}) copy-start(bf16[768,768]{0,1:T(8,128)(2,1)S(1)} %copy.78) | copy-start | bytes 3538948
  192.2 35.0 %copy-start.39 = (f32[768]{0:T(1024)}, f32[768]{0:T(1024)S(1)}, u32[]{:S(2)}) copy-start(f32[768]{0:T(1024)S(1)} %broadcast_multiply_fusion.1) | copy-start | bytes 9220
  193.2 34.0 %copy-start.45 = (f32[768]{0:T(1024)}, f32[768]{0:T(1024)S(1)}, u32[]{:S(2)}) copy-start(f32[768]{0:T(1024)S(1)} %fusion.59) | copy-start | bytes 9220
  196.2 31.0 %copy-start.41 = (f32[768]{0:T(1024)}, f32[768]{0:T(1024)S(1)}, u32[]{:S(2)}) copy-start(f32[768]{0:T(1024)S(1)} %get-tuple-element.721) | copy-start | bytes 9220
  199.8 8.0 copy-start.52
  199.8 8.1 copy-start
  201.4 56.3 %collective-permute-start = (bf16[768,1536]{0,1:T(8,128)(2,1)}, bf16[768,1536]{0,1:T(8,128)(2,1)}, u32[]{:S(2)}, u32[]{:S(2)}) collective-permute-start(bf16[768,1536]{0,1:T(8,128)(2,1)} %pad_maximum_fusion), channel_id=1, source_target_pairs={{0,1},{1,2},{2,3},{4,5},{5,6},{6,7},{8,9},{9,10},{10,11},{12,13},{... | collective-permute-start | bytes 7077896 | tf_op jit(solution)/shard_map/ppermute | solution.py:275
  208.0 8.4 copy-start.1
  355.6 26.4 %copy-start.6 = (f32[768,768]{0,1:T(8,128)}, f32[768,768]{0,1:T(8,128)S(1)}, u32[]{:S(2)}) copy-start(f32[768,768]{0,1:T(8,128)S(1)} %get-tuple-element.821) | copy-start | bytes 7077892
  356.3 11.5 %slice-start.3 = ((s8[4718592]{0:T(1024)(128)(4,1)}), s8[4194304]{0:T(1024)(128)(4,1)S(1)}, s32[]{:S(2)}) async-start(s8[4718592]{0:T(1024)(128)(4,1)} %bitcast.176), calls=%async_computation.3 | async-start | bytes 8388608
  360.6 7.3 copy-start.58
  360.6 7.3 slice-start.4
  442.4 6.5 copy-start.2
  476.7 6.5 copy-start.2
  510.9 6.5 copy-start.2
  545.0 6.5 copy-start.2
  613.5 6.5 copy-start.2
  639.5 10.0 %slice-start.5 = ((s8[4718592]{0:T(1024)(128)(4,1)}), s8[4194304]{0:T(1024)(128)(4,1)S(1)}, s32[]{:S(2)}) async-start(s8[4718592]{0:T(1024)(128)(4,1)} %bitcast.179), calls=%async_computation.5 | async-start | bytes 8388608
  647.8 55.7 %collective-permute-start.1 = (bf16[768,1536]{1,0:T(8,128)(2,1)S(1)}, bf16[768,1536]{1,0:T(8,128)(2,1)}, u32[]{:S(2)}, u32[]{:S(2)}) collective-permute-start(bf16[768,1536]{1,0:T(8,128)(2,1)S(1)} %slice.267), channel_id=1, source_target_pairs={{1,0},{2,1},{3,2},{5,4},{6,5},{7,6},{9,8},{10,9},{11,10},{13,12},{... | collective-permute-start | bytes 7077896 | tf_op jit(solution)/shard_map/ppermute | solution.py:275
  662.1 41.5 %slice-start = ((s8[9437184]{0:T(1024)(128)(4,1)}), s8[4194304]{0:T(1024)(128)(4,1)S(1)}, s32[]{:S(2)}) async-start(s8[9437184]{0:T(1024)(128)(4,1)} %bitcast.165), calls=%async_computation | async-start | bytes 8388608
  662.1 41.5 %slice-start.1 = ((s8[9437184]{0:T(1024)(128)(4,1)}), s8[4194304]{0:T(1024)(128)(4,1)S(1)}, s32[]{:S(2)}) async-start(s8[9437184]{0:T(1024)(128)(4,1)} %bitcast.165), calls=%async_computation.1 | async-start | bytes 8388608
  665.8 37.8 %slice-start.2 = ((s8[9437184]{0:T(1024)(128)(4,1)}), s8[1048576]{0:T(1024)(128)(4,1)S(1)}, s32[]{:S(2)}) async-start(s8[9437184]{0:T(1024)(128)(4,1)} %bitcast.165), calls=%async_computation.2 | async-start | bytes 2097152
  670.4 37.9 %copy-start.55 = (f32[768]{0:T(1024)S(1)}, f32[768]{0:T(1024)}, u32[]{:S(2)}) copy-start(f32[768]{0:T(1024)} %copy-done.53) | copy-start | bytes 9220
  (56 other events, 169.1 us)

commit v2 on v0

v2 whole, which is shorter than its diff:
```python
import functools

import jax
import jax.numpy as jnp
from jax import lax
from jax.experimental import pallas as pl
from jax.experimental.pallas import tpu as pltpu
from jax.sharding import PartitionSpec as P

MESH = pl.DeviceIdType.MESH

class Place:
    def __init__(self, fsdp):
        self.fsdp = fsdp
        r = lax.axis_index("rep")
        self.f = lax.axis_index("fsdp")
        self.k = lax.rem(r, 2)
        self.x = lax.rem(r // 2, 2)
        self.y = r // 4
        def rid(y, x, k): return (y * 2 + x) * 2 + k
        self.core = (rid(self.y, self.x, 1 - self.k), self.f)
        self.xn = (rid(self.y, 1 - self.x, self.k), self.f)
        self.yn = (rid(1 - self.y, self.x, self.k), self.f)
        self.r = r
        self.others = [lax.rem(self.f + j, fsdp) for j in range(1, fsdp)]
    def zdev(self, fo): return (self.r, fo)
    def barrier(self):
        bar = pltpu.get_barrier_semaphore()
        devs = [self.core, self.xn, self.yn] + [self.zdev(o) for o in self.others]
        for d in devs:
            pl.semaphore_signal(bar, inc=1, device_id=d, device_id_type=MESH)
        pl.semaphore_wait(bar, len(devs))

def drain(view, sem):
    pltpu.make_async_copy(view, view, sem).wait()

class Gather:
    def __init__(self, pc, buf, send, recv, xfirst):
        self.pc, self.buf, self.s, self.r, self.xf = pc, buf, send, recv, xfirst
        self.H = buf.shape[-1] // 2
        self.cols = pl.ds(pl.multiple_of(pc.k * self.H, 128), self.H)
    def push(self, view, stage, dev):
        pltpu.make_async_remote_copy(src_ref=view, dst_ref=view, send_sem=self.s.at[stage], recv_sem=self.r.at[stage], device_id=dev, device_id_type=MESH).start()
    def z_start(self):
        pc = self.pc
        v = self.buf.at[pc.f, pc.y, pc.x, :, self.cols]
        for o in pc.others: self.push(v, 0, pc.zdev(o))
    def three(self): return self.buf.at[pl.ds(0, self.pc.fsdp - 1), 0, 0, :, self.cols]
    def z_wait(self): drain(self.three(), self.r.at[0])
    def a_start(self):
        pc = self.pc
        for o in pc.others:
            v = self.buf.at[o, pc.y, pc.x, :, self.cols]
            self.push(v, 1, pc.xn); self.push(v, 2, pc.yn)
    def a_wait(self):
        drain(self.three(), self.r.at[1]); drain(self.three(), self.r.at[2])
    def b_start(self):
        pc = self.pc
        for o in pc.others:
            if self.xf: self.push(self.buf.at[o, 1 - pc.y, pc.x, :, self.cols], 3, pc.xn)
            else: self.push(self.buf.at[o, pc.y, 1 - pc.x, :, self.cols], 3, pc.yn)
    def b_wait(self): drain(self.three(), self.r.at[3])
    def c_start(self):
        pc = self.pc
        for o in pc.others: self.push(self.buf.at[o, :, :, :, self.cols], 4, pc.core)
    def big(self): return self.buf.at[pl.ds(0, self.pc.fsdp - 1), :, :, :, self.cols]
    def c_wait(self): drain(self.big(), self.r.at[4])
    def finish(self):
        for st in range(4): drain(self.three(), self.s.at[st])
        drain(self.big(), self.s.at[4])

Gather.STAGES = [
    lambda g: (g.z_wait(), g.a_start()),
    lambda g: (g.a_wait(), g.b_start()),
    lambda g: (g.b_wait(), g.c_start()),
    lambda g: (g.c_wait(), g.finish()),
]


class Reduce:
    def __init__(self, pc, buf, r1, r2, r3, r4, res, send, recv, xfirst):
        self.pc, self.buf, self.r1, self.r2, self.r3, self.r4, self.res = pc, buf, r1, r2, r3, r4, res
        self.s, self.r, self.xf = send, recv, xfirst
        self.H = H = buf.shape[-1] // 2
        self.cols = pl.ds(pl.multiple_of(pc.k * H, 128), H)
        self.ocols = pl.ds(pl.multiple_of((1 - pc.k) * H, 128), H)
        self.F = buf.shape[0]
    def send(self, src, dst, stage, dev):
        pltpu.make_async_remote_copy(src_ref=src, dst_ref=dst, send_sem=self.s.at[stage], recv_sem=self.r.at[stage], device_id=dev, device_id_type=MESH).start()
    def p1(self):
        self.send(self.buf.at[:, :, :, :, self.ocols], self.r1, 0, self.pc.core)
    def p2(self):
        pc = self.pc
        drain(self.r1, self.r.at[0])
        @pl.loop(0, self.F * 4)
        def _(i):
            a, b, c = i // 4, lax.rem(i // 2, 2), lax.rem(i, 2)
            self.r1[a, b, c] = (self.r1[a, b, c].astype(jnp.float32) + self.buf[a, b, c, :, self.cols].astype(jnp.float32)).astype(jnp.bfloat16)
        if self.xf: self.send(self.r1.at[:, :, 1 - pc.x], self.r2, 1, pc.xn)
        else: self.send(self.r1.at[:, 1 - pc.y], self.r2, 1, pc.yn)
    def p3(self):
        pc = self.pc
        drain(self.r2, self.r.at[1])
        @pl.loop(0, self.F * 2)
        def _(i):
            a, b = i // 2, lax.rem(i, 2)
            mine = self.r1[a, b, pc.x] if self.xf else self.r1[a, pc.y, b]
            self.r2[a, b] = (self.r2[a, b].astype(jnp.float32) + mine.astype(jnp.float32)).astype(jnp.bfloat16)
        if self.xf: self.send(self.r2.at[:, 1 - pc.y], self.r3, 2, pc.yn)
        else: self.send(self.r2.at[:, 1 - pc.x], self.r3, 2, pc.xn)
    def p4(self):
        pc = self.pc
        drain(self.r3, self.r.at[2])
        q = pc.y if self.xf else pc.x
        @pl.loop(0, self.F)
        def _(a):
            self.r3[a] = (self.r3[a].astype(jnp.float32) + self.r2[a, q].astype(jnp.float32)).astype(jnp.bfloat16)
        for o in pc.others: self.send(self.r3.at[o], self.r4.at[pc.f], 3, pc.zdev(o))
    def p5(self):
        pc = self.pc
        drain(self.r4.at[pl.ds(0, self.F - 1)], self.r.at[3])
        tot = self.r3[pc.f].astype(jnp.float32)
        for o in pc.others: tot = tot + self.r4[o].astype(jnp.float32)
        self.res[pc.y, pc.x, :, self.cols] = tot.astype(jnp.bfloat16)
        v = self.res.at[pc.y, pc.x, :, self.cols]
        self.send(v, v, 4, pc.xn); self.send(v, v, 5, pc.yn)
    def p6(self):
        pc = self.pc
        v = self.res.at[0, 0, :, self.cols]
        drain(v, self.r.at[4]); drain(v, self.r.at[5])
        if self.xf:
            v = self.res.at[1 - pc.y, pc.x, :, self.cols]; self.send(v, v, 6, pc.xn)
        else:
            v = self.res.at[pc.y, 1 - pc.x, :, self.cols]; self.send(v, v, 6, pc.yn)
    def p7(self):
        drain(self.res.at[0, 0, :, self.cols], self.r.at[6])
        v = self.res.at[:, :, :, self.cols]
        self.send(v, v, 7, self.pc.core)
    def p8(self):
        drain(self.res.at[:, :, :, self.cols], self.r.at[7])
    def finish(self):
        drain(self.r1, self.s.at[0]); drain(self.r2, self.s.at[1]); drain(self.r3, self.s.at[2])
        drain(self.r4.at[pl.ds(0, self.F - 1)], self.s.at[3])
        v = self.res.at[0, 0, :, self.cols]
        for i in (4, 5, 6): drain(v, self.s.at[i])
        drain(self.res.at[:, :, :, self.cols], self.s.at[7])

Reduce.STAGES = [Reduce.p1, Reduce.p2, Reduce.p3, Reduce.p4, Reduce.p5, Reduce.p6, Reduce.p7, Reduce.p8]

def red_shapes(shape):
    f, _, _, m, c = shape
    return (f, 2, 2, m, c // 2), (f, 2, m, c // 2), (f, m, c // 2), (f, m, c // 2)


HEAD = 64
BLOCK = 128
TRUNK = 512
TREE_LEN = 1024


epsilon = 1e-05
far_below = -1e30


def nt(a, b):
    return lax.dot_general(a, b, (((1,), (1,)), ((), ())), preferred_element_type=jnp.float32)


def tn(a, b):
    return lax.dot_general(a, b, (((0,), (0,)), ((), ())), preferred_element_type=jnp.float32)


def mm(a, b):
    return jnp.dot(a, b, preferred_element_type=jnp.float32)


def bf(a):
    return a.astype(jnp.bfloat16)


def f32(a):
    return a.astype(jnp.float32)


def row_tiles(rows):
    return 256 if rows % 256 == 0 else 128


def normalized(v):
    center = v - jnp.mean(v, axis=1, keepdims=True)
    inv = lax.rsqrt(jnp.mean(center * center, axis=1, keepdims=True) + epsilon)
    return center * inv, inv


class Span:
    def __init__(self, fsdp, rows, reach, f):
        self.rows, self.reach, self.f = rows, reach, f
        self.window = reach * rows
        self.blocks = rows // BLOCK
        self.first = f * self.blocks
        tree = TREE_LEN // BLOCK
        self.tree = tree
        self.start = (self.first // tree) * TREE_LEN - f * rows + self.window

    def kind(self, i):
        return lax.rem(self.first + i, self.tree)

    def base(self, i):
        return pl.multiple_of(((self.first + i) // self.tree) * TREE_LEN - self.f * self.rows + self.window, BLOCK)


def rows_at(start, size):
    return pl.ds(pl.multiple_of(start, BLOCK), size)


def make_bias(span, kseg, qrow, bias):
    @pl.loop(0, span.blocks)
    def _(i):
        b, base = span.kind(i), span.base(i)
        q_pos = b * BLOCK + lax.broadcasted_iota(jnp.int32, (1, BLOCK), 1)
        parent, own = qrow[i, 0:1, :], qrow[i, 1:2, :]

        def put(slot, key, count):
            k_pos = key + lax.broadcasted_iota(jnp.int32, (count, 1), 0)
            seg = kseg[rows_at(base + key, count), :]
            seen = (k_pos <= q_pos) & ((seg == parent) | (seg == own))
            bias[i, pl.ds(slot, count), :] = jnp.where(seen, 0.0, far_below)

        for n in range(TRUNK // BLOCK):

            @pl.when(b == n)
            def _():
                put(0, 0, (n + 1) * BLOCK)

        @pl.when(b >= 4)
        def _():
            put(256, b * BLOCK, BLOCK)

        @pl.when(b >= 6)
        def _():
            put(0, TRUNK, 256)


def by_kind(b, body):
    for n in range(TRUNK // BLOCK):

        @pl.when(b == n)
        def _():
            body([(0, (n + 1) * BLOCK, 0)])

    @pl.when((b >= 4) & (b < 6))
    def _():
        body([(0, 512, None), (None, BLOCK, 256)])

    @pl.when(b >= 6)
    def _():
        body([(0, 512, None), (512, 256, 0), (None, BLOCK, 256)])


def stacked(pair):
    low = lax.broadcasted_iota(jnp.int32, (1, 2 * HEAD), 1) < HEAD
    zero = jnp.zeros_like(pair)
    return jnp.concatenate([jnp.where(low, pair, zero), jnp.where(low, zero, pair)], axis=0)


def unstacked_t(wide):
    both = jnp.concatenate([wide[:HEAD, :BLOCK], wide[HEAD:, BLOCK:]], axis=0)
    return both.T


def part_rows(span, i, b, part):
    key, count, slot = part
    return rows_at(span.base(i) + (b * BLOCK if key is None else key), count)


def part_scores(q2, k, bias, i, part):
    s = nt(k, q2)
    slot = part[2]
    if slot is not None:
        one = bias[i, pl.ds(slot, part[1]), :]
        s = s + jnp.concatenate([one, one], axis=1)
    return s


def pair_cols(p):
    return pl.ds(pl.multiple_of(p * 2 * HEAD, 2 * HEAD), 2 * HEAD)


def transpose_pair(src, p, start, stop, dst):
    @pl.loop(start // BLOCK, stop // BLOCK)
    def _(j):
        dst[:, pl.ds(pl.multiple_of(j * BLOCK, BLOCK), BLOCK)] = src[rows_at(j * BLOCK, BLOCK), pair_cols(p)].T


def attend_pair(span, p, q, k, v, bias, v_t, mixed, lse):
    transpose_pair(v, p, span.start, span.window + span.rows, v_t)
    cols = pair_cols(p)

    @pl.loop(0, span.blocks)
    def _(i):
        b = span.kind(i)
        own = rows_at(i * BLOCK, BLOCK)
        q2 = stacked(q[own, cols])

        def body(parts):
            rows = [part_rows(span, i, b, part) for part in parts]
            scores = [part_scores(q2, k[r, cols], bias, i, part) for r, part in zip(rows, parts)]
            top = functools.reduce(jnp.maximum, [jnp.max(s, axis=0, keepdims=True) for s in scores])
            expo = [jnp.exp(s - top) for s in scores]
            total = sum(jnp.sum(e, axis=0, keepdims=True) for e in expo)
            inv = 1.0 / total
            out = sum(mm(v_t[:, r], bf(e * inv)) for r, e in zip(rows, expo))
            mixed[own, cols] = bf(unstacked_t(out))
            lse[p, pl.ds(i, 1), :] = top + jnp.log(total)

        by_kind(b, body)


def norm_tile(x, gain, shift):
    hat, _ = normalized(f32(x))
    return bf(hat * gain + shift)


def project(span, x, fv, lnp, w1, w2, n1, q, k, v):
    gain, shift = lnp[0:1, :], lnp[1:2, :]
    tile = row_tiles(span.rows)
    third = w1.shape[1] // 4
    half = 2 * third
    scale = HEAD ** (-0.5)

    @pl.loop(span.window // tile, (span.window + span.rows) // tile)
    def _(t):
        rows = rows_at(t * tile, tile)
        n = norm_tile(x[rows, :], gain, shift)
        own = rows_at(t * tile - span.window, tile)
        n1[own, :] = n
        a = mm(n, w1[...])
        q[own, :half] = bf(f32(bf(a[:, :half])) * scale)
        k[rows, :half] = bf(a[:, half:])
        a = mm(n, w2[...])
        q[own, half:] = bf(f32(bf(a[:, :third])) * scale)
        k[rows, half:] = bf(a[:, half:half + third])
        v[rows, :third] = bf(a[:, third:half])
        v[rows, third:third + BLOCK] = bf(a[:, half + third:half + third + BLOCK])
        v[rows, third + BLOCK:] = fv[rows, :]

    @pl.loop(span.start // tile, span.window // tile)
    def _(t):
        rows = rows_at(t * tile, tile)
        n = norm_tile(x[rows, :], gain, shift)
        k[rows, :half] = bf(mm(n, w1[:, half:]))
        a = mm(n, w2[:, third:])
        v[rows, :third] = bf(a[:, :third])
        k[rows, half:] = bf(a[:, third:half])
        v[rows, third:third + BLOCK] = bf(a[:, half:half + BLOCK])
        v[rows, third + BLOCK:] = fv[rows, :]


def branch_out(span, x, lnp, mixed, wo, resid, n2):
    gain, shift = lnp[2:3, :], lnp[3:4, :]
    tile = row_tiles(span.rows)

    @pl.loop(0, span.rows // tile)
    def _(t):
        rows = rows_at(t * tile, tile)
        r = f32(x[rows_at(span.window + t * tile, tile), :]) + mm(mixed[rows, :], wo[...])
        resid[rows, :] = r
        hat, _ = normalized(r)
        n2[rows, :] = bf(hat * gain + shift)


def forward_kernel(fsdp, reach, x, fv, lnp, w1, w2, wo, kseg, qrow, n1, q, k, v, mixed, lse, resid, n2, bias, v_t):
    span = Span(fsdp, q.shape[0], reach, lax.axis_index("fsdp"))
    make_bias(span, kseg, qrow, bias)
    project(span, x, fv, lnp, w1, w2, n1, q, k, v)

    @pl.loop(0, q.shape[1] // (2 * HEAD))
    def _(p):
        attend_pair(span, p, q, k, v, bias, v_t, mixed, lse)

    branch_out(span, x, lnp, mixed, wo, resid, n2)


VM = pl.BlockSpec(memory_space=pltpu.VMEM)


def forward_call(fsdp, reach, x, fv, lnp, w1, w2, wo, kseg, qrow):
    window, width = x.shape
    rows = window // (reach + 1)
    s = jax.ShapeDtypeStruct
    low, full = jnp.bfloat16, jnp.float32
    pairs, blocks = width // (2 * HEAD), rows // BLOCK
    outs = (
        s((rows, width), low), s((rows, width), low), s((window, width), low), s((window, width), low), s((rows, width), low),
        s((pairs, -(-blocks // 8) * 8, 2 * BLOCK), full), s((rows, width), full), s((rows, width), low),
    )
    return pl.pallas_call(
        functools.partial(forward_kernel, fsdp, reach),
        out_shape=outs, in_specs=[VM] * 8, out_specs=[VM] * 8,
        scratch_shapes=[pltpu.VMEM((blocks, TRUNK, BLOCK), full), pltpu.VMEM((2 * HEAD, window), low)],
        compiler_params=pltpu.CompilerParams(vmem_limit_bytes=50 << 20),
    )(x, fv, lnp, w1, w2, wo, kseg, qrow)


GELU_A = 0.7978845608028654
GELU_B = 0.044715


def gelu_both(u):
    sq = u * u
    t = jnp.tanh(GELU_A * u * (1.0 + GELU_B * sq))
    half = 0.5 * (1.0 + t)
    slope = half + 0.5 * u * (1.0 - t * t) * (GELU_A * (1.0 + 3.0 * GELU_B * sq))
    return u * half, slope


def transpose_all(src, dst):
    cols = src.shape[1] // BLOCK

    @pl.loop(0, src.shape[0] // BLOCK)
    def _(j):
        rows = rows_at(j * BLOCK, BLOCK)
        for c in range(cols):
            dst[c * BLOCK:(c + 1) * BLOCK, rows] = src[rows, c * BLOCK:(c + 1) * BLOCK].T


def mlp_chunk(rows, n2, n2_t, cot, win, wdn, out_acc, gn2_acc, hid, gact, gin, gdn):
    tile = row_tiles(rows)

    @pl.loop(0, rows // tile)
    def _(t):
        r = rows_at(t * tile, tile)
        h, slope = gelu_both(mm(n2[r, :], win()))
        h = bf(h)
        hid[r, :] = h
        out_acc[r, :] += mm(h, wdn())
        g = bf(nt(cot[r, :], wdn()) * slope)
        gact[r, :] = g
        gn2_acc[r, :] += nt(g, win())

    gdn(bf(tn(hid[...], cot[...])))
    gin(bf(mm(n2_t[...], gact[...])))


def norm_back(hat, inv, grad, gain):
    e = grad * gain
    return inv * (e - jnp.mean(e, axis=1, keepdims=True) - hat * jnp.mean(e * hat, axis=1, keepdims=True))


def second_norm_back(rows, lnp, resid, cot, gn2, gres, gbranch, sums):
    tile = row_tiles(rows)
    sums[...] = jnp.zeros_like(sums)

    @pl.loop(0, rows // tile)
    def _(t):
        r = rows_at(t * tile, tile)
        hat, inv = normalized(resid[r, :])
        g = gn2[r, :]
        gr = f32(cot[r, :]) + norm_back(hat, inv, g, lnp[2:3, :])
        gres[r, :] = gr
        gbranch[r, :] = bf(gr)
        sums[2:3, :] += jnp.sum(g * hat, axis=0, keepdims=True)
        sums[3:4, :] += jnp.sum(g, axis=0, keepdims=True)


def branch_back(rows, gbranch, wo, gmixed):
    tile = row_tiles(rows)

    @pl.loop(0, rows // tile)
    def _(t):
        r = rows_at(t * tile, tile)
        gmixed[r, :] = bf(nt(gbranch[r, :], wo[...]))


def mlp_kernel(n2, cot, resid, mixed, lnp, win, wdn, wo, outputs, gin, gdn, go, gres, gmixed, sums, n2_t, out_acc, gn2_acc, hid, gact, gbranch):
    rows = n2.shape[0]
    transpose_all(n2, n2_t)
    out_acc[...] = resid[...]
    gn2_acc[...] = jnp.zeros_like(gn2_acc)

    @pl.loop(0, win.shape[0])
    def _(c):
        def put_in(v):
            gin[c] = v

        def put_dn(v):
            gdn[c] = v

        mlp_chunk(rows, n2, n2_t, cot, lambda: win[c], lambda: wdn[c], out_acc, gn2_acc, hid, gact, put_in, put_dn)

    outputs[...] = bf(out_acc[...])
    second_norm_back(rows, lnp, resid, cot, gn2_acc, gres, gbranch, sums)
    branch_back(rows, gbranch, wo, gmixed)
    go[...] = bf(tn(mixed[...], gbranch[...]))


def mlp_call(n2, cot, resid, mixed, lnp, win, wdn, wo):
    rows, width = n2.shape
    n_ff, _, cols = win.shape
    s, low, full = jax.ShapeDtypeStruct, jnp.bfloat16, jnp.float32
    outs = (
        s((rows, width), low), s(win.shape, low), s(wdn.shape, low), s((width, width), low), s((rows, width), full),
        s((rows, width), low), s((8, width), full),
    )
    return pl.pallas_call(
        mlp_kernel, out_shape=outs, in_specs=[VM] * 8, out_specs=[VM] * 7,
        scratch_shapes=[
            pltpu.VMEM((width, rows), low), pltpu.VMEM((rows, width), full), pltpu.VMEM((rows, width), full),
            pltpu.VMEM((rows, cols), low), pltpu.VMEM((rows, cols), low), pltpu.VMEM((rows, width), low),
        ],
        compiler_params=pltpu.CompilerParams(vmem_limit_bytes=58 << 20),
    )(n2, cot, resid, mixed, lnp, win, wdn, wo)


def attend_back_pair(span, p, q, k, v, gmixed, bias, lse, k_t, dk_acc, dv_acc, dq):
    transpose_pair(k, p, span.start, span.window + span.rows, k_t)
    cols = pair_cols(p)

    @pl.loop(span.start // BLOCK, (span.window + span.rows) // BLOCK)
    def _(j):
        r = rows_at(j * BLOCK, BLOCK)
        dk_acc[r, :] = jnp.zeros((BLOCK, 2 * HEAD), jnp.float32)
        dv_acc[r, :] = jnp.zeros((BLOCK, 2 * HEAD), jnp.float32)

    @pl.loop(0, span.blocks)
    def _(i):
        b = span.kind(i)
        own = rows_at(i * BLOCK, BLOCK)
        q2, g2 = stacked(q[own, cols]), stacked(gmixed[own, cols])
        l = lse[p, pl.ds(i, 1), :]

        def body(parts):
            rows = [part_rows(span, i, b, part) for part in parts]
            probs = [jnp.exp(part_scores(q2, k[r, cols], bias, i, part) - l) for r, part in zip(rows, parts)]
            gw = [nt(v[r, cols], g2) for r in rows]
            inner = sum(jnp.sum(a * g, axis=0, keepdims=True) for a, g in zip(probs, gw))
            gs = [bf(a * (g - inner)) for a, g in zip(probs, gw)]
            out = sum(mm(k_t[:, r], g) for r, g in zip(rows, gs))
            dq[own, cols] = bf(unstacked_t(out) * HEAD ** (-0.5))
            for r, a, g in zip(rows, probs, gs):
                dk_acc[r, :] += mm(g, q2)
                dv_acc[r, :] += mm(bf(a), g2)

        by_kind(b, body)


def backward_kernel(fsdp, reach, q, k, v, gmixed, lse, kseg, qrow, dq, dk, dv, wk, wv, bias, k_t, dk_acc, dv_acc):
    span = Span(fsdp, q.shape[0], reach, lax.axis_index("fsdp"))
    make_bias(span, kseg, qrow, bias)
    wk[...] = jnp.zeros_like(wk)
    wv[...] = jnp.zeros_like(wv)

    @pl.loop(0, q.shape[1] // (2 * HEAD))
    def _(p):
        cols = pair_cols(p)
        attend_back_pair(span, p, q, k, v, gmixed, bias, lse, k_t, dk_acc, dv_acc, dq)
        dk[:, cols] = dk_acc[span.window:, :]
        dv[:, cols] = dv_acc[span.window:, :]

        @pl.loop(span.start // BLOCK, span.window // BLOCK)
        def _(j):
            r = rows_at(j * BLOCK, BLOCK)
            wk[r, cols] = bf(dk_acc[r, :])
            wv[r, cols] = bf(dv_acc[r, :])


def backward_call(fsdp, reach, q, k, v, gmixed, lse, kseg, qrow):
    window, width = k.shape
    rows = q.shape[0]
    s, low, full = jax.ShapeDtypeStruct, jnp.bfloat16, jnp.float32
    early = window - rows
    outs = (s((rows, width), low), s((rows, width), full), s((rows, width), full), s((early, width), low), s((early, width), low))
    return pl.pallas_call(
        functools.partial(backward_kernel, fsdp, reach), out_shape=outs, in_specs=[VM] * 7, out_specs=[VM] * 5,
        scratch_shapes=[
            pltpu.VMEM((rows // BLOCK, TRUNK, BLOCK), full), pltpu.VMEM((2 * HEAD, window), low),
            pltpu.VMEM((window, 2 * HEAD), full), pltpu.VMEM((window, 2 * HEAD), full),
        ],
        compiler_params=pltpu.CompilerParams(vmem_limit_bytes=58 << 20),
    )(q, k, v, gmixed, lse, kseg, qrow)


def projection_back(span, x, n1, dq, dk, dv, lnp, w1, w2, gres, gin, gfirst, g1, g2, sums, n1_t, cat1, cat2):
    rows = span.rows
    third = w1.shape[1] // 4
    half = 2 * third
    fresh = third + BLOCK
    tile = row_tiles(rows)
    transpose_all(n1, n1_t)

    @pl.loop(0, rows // tile)
    def _(t):
        r = rows_at(t * tile, tile)
        cat1[r, :half] = dq[r, :half]
        cat1[r, half:] = bf(dk[r, :half])
        cat2[r, :third] = dq[r, half:]
        cat2[r, third:half] = bf(dv[r, :third])
        cat2[r, half:half + third] = bf(dk[r, half:])
        cat2[r, half + third:half + third + BLOCK] = bf(dv[r, third:fresh])
        cat2[r, half + third + BLOCK:] = jnp.zeros((tile, BLOCK), jnp.bfloat16)
        gfirst[r, :] = dv[r, fresh:]

    g1[...] = bf(mm(n1_t[...], cat1[...]))
    g2[...] = bf(mm(n1_t[...], cat2[...]))

    @pl.loop(0, rows // tile)
    def _(t):
        r = rows_at(t * tile, tile)
        g = nt(cat1[r, :], w1[...]) + nt(cat2[r, :], w2[...])
        hat, inv = normalized(f32(x[rows_at(span.window + t * tile, tile), :]))
        gin[r, :] = gres[r, :] + norm_back(hat, inv, g, lnp[0:1, :])
        sums[0:1, :] += jnp.sum(g * hat, axis=0, keepdims=True)
        sums[1:2, :] += jnp.sum(g, axis=0, keepdims=True)


def projection_back_kernel(fsdp, reach, x, n1, dq, dk, dv, lnp, w1, w2, gres, sums_in, gin, gfirst, g1, g2, sums, n1_t, cat1, cat2):
    span = Span(fsdp, dq.shape[0], reach, lax.axis_index("fsdp"))
    sums[...] = sums_in[...]
    projection_back(span, x, n1, dq, dk, dv, lnp, w1, w2, gres, gin, gfirst, g1, g2, sums, n1_t, cat1, cat2)


def projection_back_call(fsdp, reach, x, n1, dq, dk, dv, lnp, w1, w2, gres, sums):
    rows, width = dq.shape
    s, low, full = jax.ShapeDtypeStruct, jnp.bfloat16, jnp.float32
    outs = (s((rows, width), full), s((rows, width // 2), full), s(w1.shape, low), s(w2.shape, low), s((8, width), full))
    return pl.pallas_call(
        functools.partial(projection_back_kernel, fsdp, reach), out_shape=outs, in_specs=[VM] * 10, out_specs=[VM] * 5,
        scratch_shapes=[pltpu.VMEM((width, rows), low), pltpu.VMEM((rows, w1.shape[1]), low), pltpu.VMEM((rows, w1.shape[1]), low)],
        compiler_params=pltpu.CompilerParams(vmem_limit_bytes=58 << 20),
    )(x, n1, dq, dk, dv, lnp, w1, w2, gres, sums)


def gather_steps(items, u):
    for s, stage in enumerate(Gather.STAGES):
        c = u - s

        @pl.when((c >= 0) & (c < items.count))
        def _():
            for g in items(c):
                stage(g)


def reduce_steps(items, u):
    for s, stage in enumerate(Reduce.STAGES):
        c = u - s

        @pl.when((c >= 0) & (c < items.count))
        def _():
            for g in items(c):
                stage(g)


class Chunks:
    def __init__(self, count, make):
        self.count, self.make = count, make

    def __call__(self, c):
        return self.make(c)


class Scratch:
    def __init__(self):
        self.names, self.shapes = [], []

    def add(self, name, shape):
        self.names.append(name)
        self.shapes.append(shape)

    def bind(self, refs):
        for name, ref in zip(self.names, refs):
            setattr(self, name, ref)
        return self


def layer_kernel(fsdp, n_ff, scratch, n_out, *refs):
    (inputs, first, cot_in, vec, a_q, a_k, a_v, a_o, a_in, a_dn, kseg, qrow) = refs[:12]
    (outputs, gin, gfirst, rs_q, rs_k, rs_v, rs_o, rs_in, rs_dn, rs_vec) = refs[12 : 12 + n_out]
    m = scratch.bind(refs[12 + n_out :])
    pc = Place(fsdp)
    f = pc.f
    rows, width = cot_in.shape
    span = Span(fsdp, rows, 1, f)
    tile = row_tiles(rows)
    tiles = rows // tile
    last = fsdp - 1
    flat = lambda ref: ref.reshape(-1, ref.shape[-1])
    w_q, w_k, w_v, w_o = (flat(b) for b in (m.b_q, m.b_k, m.b_v, m.b_o))
    mixed, cot = m.mixed.reshape(rows, width), m.cot.reshape(rows, width)
    x, q, k, v, n1, n2, tr = m.x, m.q, m.k, m.v, m.n1, m.n2, m.tr

    def local(src, dst, sem):
        c = pltpu.make_async_copy(src, dst, sem)
        c.start()
        return c

    lv = local(vec, m.vec.at[f], m.l_sem.at[0])
    lw = [local(a, b.at[f], m.l_sem.at[1 + i]) for i, (a, b) in enumerate(((a_q, m.b_q), (a_k, m.b_k), (a_v, m.b_v), (a_o, m.b_o)))]
    lx = local(inputs, x.at[pl.ds(rows, rows)], m.l_sem.at[5])
    lf = local(first, v.at[pl.ds(rows, rows), pl.ds(width // 2, width // 2)], m.l_sem.at[6])
    lc = local(cot_in, cot, m.l_sem.at[7])
    lk = local(kseg, m.dk_acc, m.l_sem.at[8])
    group = a_in.shape[-1] // fsdp

    def own_chunk(c, act):
        for g in range(fsdp):
            cols = pl.ds(pl.multiple_of(g * group + c * BLOCK, BLOCK), BLOCK)
            act(pltpu.make_async_copy(a_in.at[:, :, :, cols], m.b_in.at[c, f, :, :, :, pl.ds(g * BLOCK, BLOCK)], m.lc_sem.at[c, g]))
        act(pltpu.make_async_copy(a_dn.at[c], m.b_dn.at[c, f], m.lc_sem.at[c, fsdp]))

    @pl.loop(0, n_ff)
    def _(c):
        own_chunk(c, lambda d: d.start())

    pc.barrier()
    lv.wait()
    for o in pc.others:
        pltpu.make_async_remote_copy(
            src_ref=m.vec.at[f], dst_ref=m.vec.at[f], send_sem=m.v_send.at[0], recv_sem=m.v_recv.at[0], device_id=pc.zdev(o), device_id_type=MESH
        ).start()
    gat = [Gather(pc, b, m.g_send.at[i], m.g_recv.at[i], xf) for i, (b, xf) in enumerate(((m.b_q, True), (m.b_k, False), (m.b_v, True), (m.b_o, False)))]
    for l, g in zip(lw[:3], gat):
        l.wait()
        g.z_start()

    next_start = Span(fsdp, rows, 1, f + 1).start

    def window(t):
        r = pl.ds(t * tile, tile)
        nxt = (pc.r, f + 1)
        return [
            pltpu.make_async_remote_copy(src_ref=inputs.at[r], dst_ref=x.at[r], send_sem=m.w_send.at[0, t], recv_sem=m.w_recv.at[0, t], device_id=nxt, device_id_type=MESH),
            pltpu.make_async_remote_copy(
                src_ref=first.at[r], dst_ref=v.at[r, pl.ds(width // 2, width // 2)], send_sem=m.w_send.at[1, t], recv_sem=m.w_recv.at[1, t], device_id=nxt, device_id_type=MESH
            ),
        ]

    for t in range(tiles):

        @pl.when((f < last) & (t * tile >= next_start))
        def _():
            for c in window(t):
                c.start()

    lw[3].wait()
    gat[3].z_start()
    ff = Chunks(
        n_ff,
        lambda c: [Gather(pc, m.b_in.at[c], m.gi_send.at[c], m.gi_recv.at[c], True), Gather(pc, m.b_dn.at[c], m.gd_send.at[c], m.gd_recv.at[c], False)],
    )

    @pl.loop(0, n_ff)
    def _(c):
        own_chunk(c, lambda d: d.wait())
        for g in ff(c):
            g.z_start()

    for g in gat[:3]:
        g.z_wait()
        g.a_start()
    lk.wait()
    make_bias(span, m.dk_acc, qrow, m.bias)
    for g in gat[:3]:
        g.a_wait()
        g.b_start()
    gat[3].z_wait()
    gat[3].a_start()
    v3 = m.vec.at[pl.ds(0, last)]
    drain(v3, m.v_recv.at[0])
    drain(v3, m.v_send.at[0])
    m.lnp[...] = functools.reduce(lambda a, b: a + b, [m.vec[j] for j in range(fsdp)])
    gain, shift = m.lnp[0:1, :], m.lnp[1:2, :]
    lx.wait()

    @pl.loop(0, tiles)
    def _(t):
        n1[rows_at(t * tile, tile), :] = norm_tile(x[rows_at(rows + t * tile, tile), :], gain, shift)

    for g in gat[:3]:
        g.b_wait()
        g.c_start()
    gat[3].a_wait()
    gat[3].b_start()
    lf.wait()
    for g in gat[:3]:
        g.c_wait()
    half = width // 2

    @pl.loop(0, tiles)
    def _(t):
        r, own = rows_at(rows + t * tile, tile), rows_at(t * tile, tile)
        n = n1[own, :]
        q[own, :] = bf(f32(bf(mm(n, w_q[...]))) * HEAD ** (-0.5))
        k[r, :] = bf(mm(n, w_k[...]))
        v[r, :half] = bf(mm(n, w_v[:, :half]))

    for t in range(tiles):

        @pl.when(t * tile >= span.start)
        def _():
            drain(x.at[pl.ds(t * tile, tile)], m.w_recv.at[0, t])
            drain(v.at[pl.ds(t * tile, tile), pl.ds(half, half)], m.w_recv.at[1, t])

    @pl.loop(span.start // tile, tiles)
    def _(t):
        r = rows_at(t * tile, tile)
        n = norm_tile(x[r, :], gain, shift)
        k[r, :] = bf(mm(n, w_k[...]))
        v[r, :half] = bf(mm(n, w_v[:, :half]))

    gat[3].b_wait()
    gat[3].c_start()

    pairs = width // (2 * HEAD)

    @pl.loop(0, pairs)
    def _(p):
        attend_pair(span, p, q, k, v, m.bias, m.turned, mixed, m.lse)
        gather_steps(ff, p)

    gat[3].c_wait()
    branch_out(span, x, m.lnp, mixed, w_o, m.resid, n2)
    for g in gat:
        g.finish()

    lc.wait()
    transpose_all(n2, tr)
    m.acc1[...] = m.resid[...]
    m.acc2[...] = jnp.zeros_like(m.acc2)
    red = Chunks(
        n_ff,
        lambda c: [
            Reduce(pc, m.b_in.at[c], *(a.at[c] for a in m.r_in), rs_in.at[c], m.ri_send.at[c], m.ri_recv.at[c], True),
            Reduce(pc, m.b_dn.at[c], *(a.at[c] for a in m.r_dn), rs_dn.at[c], m.rd_send.at[c], m.rd_recv.at[c], False),
        ],
    )
    hid, gact = m.back.at[0, :, pl.ds(0, fsdp * BLOCK)], m.back.at[1, :, pl.ds(0, fsdp * BLOCK)]

    @pl.loop(0, n_ff)
    def _(c):
        gather_steps(ff, c + pairs)
        b_in, b_dn = flat(m.b_in.at[c]), flat(m.b_dn.at[c])

        def put_in(val):
            b_in[...] = val

        def put_dn(val):
            b_dn[...] = val

        mlp_chunk(rows, n2, tr, cot, lambda: b_in[...], lambda: b_dn[...], m.acc1, m.acc2, hid, gact, put_in, put_dn)
        reduce_steps(red, c)

    @pl.loop(0, tiles)
    def _(t):
        r = rows_at(t * tile, tile)
        m.back[0, r, :] = bf(m.acc1[r, :])

    lo = local(m.back.at[0], outputs, m.l_sem.at[0])
    m.sums[...] = jnp.zeros_like(m.sums)
    second_norm_back(rows, m.lnp, m.resid, cot, m.acc2, m.resid, n2, m.sums)
    branch_back(rows, n2, w_o, m.gmixed)

    @pl.loop(0, width // tile)
    def _(t):
        r = rows_at(t * tile, tile)
        w_o[r, :] = bf(tn(mixed[:, pl.ds(pl.multiple_of(t * tile, tile), tile)], n2[...]))

    lo.wait()

    @pl.when(f < last)
    def _():
        pl.semaphore_signal(m.ready, inc=1, device_id=(pc.r, f + 1), device_id_type=MESH)

    @pl.when(f > 0)
    def _():
        pl.semaphore_wait(m.ready, 1)

    transpose_all(n1, tr)
    stat = [
        Reduce(pc, b, *scr, res, m.rs_send.at[i], m.rs_recv.at[i], xf)
        for i, (b, scr, res, xf) in enumerate(
            ((m.b_o, m.r_o, rs_o, True), (m.mixed, m.r_q, rs_q, False), (m.cot, m.r_k, rs_k, True), (m.g_v, m.r_v, rs_v, False))
        )
    ]
    red_o, red_q, red_k, red_v = stat

    def early(t, p):
        r, cols = pl.ds(t * tile, tile), pair_cols(p)
        prev = (pc.r, f - 1)
        return [
            pltpu.make_async_remote_copy(
                src_ref=x.at[pl.ds(j * rows + t * tile, tile), cols], dst_ref=m.back.at[j, r, cols], send_sem=m.e_send.at[j, p, t], recv_sem=m.e_recv.at[j, p, t],
                device_id=prev, device_id_type=MESH,
            )
            for j in range(2)
        ]

    dk, dv = m.acc1, m.acc2

    @pl.loop(0, pairs)
    def _(p):
        cols = pair_cols(p)
        attend_back_pair(span, p, q, k, v, m.gmixed, m.bias, m.lse, m.turned, m.dk_acc, m.dv_acc, q)
        dk[:, cols] = m.dk_acc[rows:, :]
        dv[:, cols] = m.dv_acc[rows:, :]
        for t in range(tiles):

            @pl.when((f > 0) & (t * tile >= span.start))
            def _():
                r = pl.ds(t * tile, tile)
                x[r, cols] = bf(m.dk_acc[r, :])
                x[pl.ds(rows + t * tile, tile), cols] = bf(m.dv_acc[r, :])
                for c in early(t, p):
                    c.start()

        reduce_steps(red, n_ff + p)
        for s in range(6):

            @pl.when(p == s)
            def _():
                Reduce.STAGES[s](red_o)

    d_q = flat(m.mixed)
    wide = width // tile

    def weight_grad(dst, grad, cols):
        @pl.loop(0, wide)
        def _(t):
            r = rows_at(t * tile, tile)
            dst[r, :cols] = bf(mm(tr[r, :], grad[:, :cols]))

    weight_grad(d_q, q, width)
    red_q.p1()
    for u in range(n_ff + pairs, n_ff + 7):
        reduce_steps(red, u)
    red_o.p7()

    @pl.loop(0, pairs)
    def _(p):
        for t in range(tiles):

            @pl.when((f < last) & (t * tile >= next_start))
            def _():
                r, cols = pl.ds(t * tile, tile), pair_cols(p)
                for j, own in enumerate((dk, dv)):
                    drain(m.back.at[j, r, cols], m.e_recv.at[j, p, t])
                    own[r, cols] += f32(m.back[j, r, cols])

    red_q.p2()

    @pl.loop(0, tiles)
    def _(t):
        r = rows_at(t * tile, tile)
        k[r, :] = bf(dk[r, :])
        v[r, :half] = bf(dv[r, :half])

    gf = local(dv.at[:, pl.ds(half, half)], gfirst, m.l_sem.at[1])
    d_k, d_v = flat(m.cot), flat(m.g_v)
    weight_grad(d_k, k.at[pl.ds(0, rows)], width)
    red_k.p1()
    d_v[:, half:] = jnp.zeros((width, d_v.shape[1] - half), jnp.bfloat16)
    weight_grad(d_v, v.at[pl.ds(0, rows)], half)
    red_v.p1()
    red_q.p3()
    red_o.p8()

    @pl.loop(0, tiles)
    def _(t):
        r = rows_at(t * tile, tile)
        g = nt(q[r, :], w_q[...]) + nt(k[r, :], w_k[...]) + nt(v[r, :half], w_v[:, :half])
        dk[r, :] = g

    red_q.p4()
    red_k.p2()
    red_v.p2()
    lx = local(inputs, n1, m.l_sem.at[2])
    lx.wait()

    @pl.loop(0, tiles)
    def _(t):
        r = rows_at(t * tile, tile)
        g = dk[r, :]
        hat, inv = normalized(f32(n1[r, :]))
        m.resid[r, :] += norm_back(hat, inv, g, m.lnp[0:1, :])
        m.sums[0:1, :] += jnp.sum(g * hat, axis=0, keepdims=True)
        m.sums[1:2, :] += jnp.sum(g, axis=0, keepdims=True)

    gi = local(m.resid, gin, m.l_sem.at[3])
    red_q.p5()
    red_k.p3()
    red_v.p3()

    def exchange(src, dst, i, dev):
        c = pltpu.make_async_remote_copy(src_ref=src, dst_ref=dst, send_sem=m.v_send.at[i], recv_sem=m.v_recv.at[i], device_id=dev, device_id_type=MESH)
        c.start()
        return c

    cur = m.sums
    work = [(red_q.p6, red_k.p4, red_v.p4), (red_q.p7, red_k.p5, red_v.p5), (red_q.p8, red_k.p6, red_v.p6)]
    for i, dev in enumerate((pc.core, pc.xn, pc.yn)):
        c = exchange(cur, m.s_pair.at[i], 1 + i, dev)
        for step in work[i]:
            step()
        c.wait()
        m.s_pair[i] = m.s_pair[i] + cur[...]
        cur = m.s_pair.at[i]
    for o in pc.others:
        exchange(cur, m.s_z.at[f], 4, pc.zdev(o))
    red_k.p7()
    red_v.p7()
    z3 = m.s_z.at[pl.ds(0, last)]
    drain(z3, m.v_recv.at[4])
    drain(z3, m.v_send.at[4])
    m.s_z[f] = cur[...]
    rs_vec[...] = functools.reduce(lambda a, b: a + b, [m.s_z[j] for j in range(fsdp)])
    red_k.p8()
    red_v.p8()
    for g in stat:
        g.finish()

    @pl.loop(0, n_ff)
    def _(c):
        for g in red(c):
            g.finish()

    for t in range(tiles):

        @pl.when((f < last) & (t * tile >= next_start))
        def _():
            for c in window(t):
                c.wait_send()

    @pl.loop(0, pairs)
    def _(p):
        for t in range(tiles):

            @pl.when((f > 0) & (t * tile >= span.start))
            def _():
                for c in early(t, p):
                    c.wait_send()

    gf.wait()
    gi.wait()


def layer_call(fsdp, inputs, first, cot, vec, w_query, w_key, w_value, w_out, w_in, w_down, kseg, qrow):
    rows, width = inputs.shape
    shard = w_query.shape[0]
    n_ff = w_down.shape[0] // BLOCK
    low, full = jnp.bfloat16, jnp.float32
    mq, md = shard // 4, BLOCK // 4
    pairs, blocks = width // (2 * HEAD), rows // BLOCK
    value = jnp.pad(w_value, ((0, 0), (0, BLOCK)))
    split = lambda a: a.reshape(2, 2, mq, a.shape[1])
    buf = lambda m, c, lead=(): (*lead, fsdp, 2, 2, m, c)
    chunk = fsdp * BLOCK
    sc = Scratch()
    V, D = pltpu.VMEM, pltpu.SemaphoreType.DMA
    for name, shape in (
        ("b_q", buf(mq, width)), ("b_k", buf(mq, width)), ("b_v", buf(mq, value.shape[1])), ("b_o", buf(mq, width)),
        ("b_in", buf(mq, chunk, (n_ff,))), ("b_dn", buf(md, width, (n_ff,))), ("g_v", buf(mq, value.shape[1])),
        ("mixed", buf(mq, width)), ("cot", buf(mq, width)), ("x", (2 * rows, width)), ("k", (2 * rows, width)), ("v", (2 * rows, width)),
        ("q", (rows, width)), ("n1", (rows, width)), ("n2", (rows, width)), ("tr", (width, rows)), ("gmixed", (rows, width)), ("back", (2, rows, width)),
        ("turned", (2 * HEAD, 2 * rows)),
    ):
        sc.add(name, V(shape, low))
    for name, shape in (
        ("vec", (fsdp, 8, width)), ("lnp", (8, width)), ("sums", (8, width)), ("s_pair", (3, 8, width)), ("s_z", (fsdp, 8, width)),
        ("resid", (rows, width)), ("acc1", (rows, width)), ("acc2", (rows, width)), ("bias", (blocks, TRUNK, BLOCK)),
        ("dk_acc", (2 * rows, 2 * HEAD)), ("dv_acc", (2 * rows, 2 * HEAD)), ("lse", (pairs, -(-blocks // 8) * 8, 2 * BLOCK)),
    ):
        sc.add(name, V(shape, full))
    for name, shape in (
        ("l_sem", (9,)), ("lc_sem", (n_ff, fsdp + 1)), ("v_send", (5,)), ("v_recv", (5,)), ("g_send", (4, 5)), ("g_recv", (4, 5)),
        ("w_send", (2, rows // row_tiles(rows))), ("w_recv", (2, rows // row_tiles(rows))),
        ("gi_send", (n_ff, 5)), ("gi_recv", (n_ff, 5)), ("gd_send", (n_ff, 5)), ("gd_recv", (n_ff, 5)),
        ("ri_send", (n_ff, 8)), ("ri_recv", (n_ff, 8)), ("rd_send", (n_ff, 8)), ("rd_recv", (n_ff, 8)), ("rs_send", (4, 8)), ("rs_recv", (4, 8)),
        ("e_send", (2, pairs, rows // row_tiles(rows))), ("e_recv", (2, pairs, rows // row_tiles(rows))),
    ):
        sc.add(name, D(shape))
    sc.add("ready", pltpu.SemaphoreType.REGULAR)
    groups = (("r_in", buf(mq, chunk), n_ff), ("r_dn", buf(md, width), n_ff), ("r_o", buf(mq, width), 0), ("r_q", buf(mq, width), 0), ("r_k", buf(mq, width), 0), ("r_v", buf(mq, value.shape[1]), 0))
    for name, shape, lead in groups:
        for i, sub in enumerate(red_shapes(shape)):
            sc.add(f"{name}{i}", V((lead, *sub) if lead else sub, low))

    n_out = 10
    s = jax.ShapeDtypeStruct
    outs = (
        s((rows, width), low), s((rows, width), full), s((rows, width // 2), full),
        s((2, 2, mq, width), low), s((2, 2, mq, width), low), s((2, 2, mq, value.shape[1]), low), s((2, 2, mq, width), low),
        s((n_ff, 2, 2, mq, chunk), low), s((n_ff, 2, 2, md, width), low), s((8, width), full),
    )

    def body(*refs):
        names = Scratch()
        names.names, names.shapes = sc.names, sc.shapes
        bound = names.bind(refs[12 + n_out :])
        for name, _, _ in groups:
            setattr(bound, name, [getattr(bound, f"{name}{i}") for i in range(4)])
        layer_kernel(fsdp, n_ff, bound, n_out, *refs)

    any_ = pl.BlockSpec(memory_space=pl.ANY)
    return pl.pallas_call(
        body, out_shape=outs, in_specs=[any_] * 11 + [VM], out_specs=[any_] * 3 + [VM] * 7, scratch_shapes=sc.shapes,
        compiler_params=pltpu.CompilerParams(collective_id=3, has_side_effects=True, vmem_limit_bytes=61 << 20),
    )(inputs, first, cot, vec, split(w_query), split(w_key), split(value), split(w_out), split(w_in), w_down.reshape(n_ff, 2, 2, md, width), kseg, qrow)


def shifted(block, axis, distance):
    devices = range(lax.axis_size(axis))
    route = [(i - distance, i) for i in devices if i - distance in devices]
    return lax.ppermute(block, axis, route)


def path_rows(tree_ids, segment_ids, path_table):
    seg_count = path_table.shape[1]
    flat_table = path_table.reshape(-1, 3)
    lookup = tree_ids * seg_count + segment_ids
    onehot = (lookup[:, None] == jnp.arange(flat_table.shape[0], dtype=jnp.int32)[None, :]).astype(
        jnp.int32
    )
    return jnp.sum(onehot[:, :, None] * flat_table[None, :, :], axis=1)


def reorder_rows(grad_block, fsdp_count, rep_count):
    return grad_block.reshape(fsdp_count, rep_count, -1).transpose(1, 0, 2).reshape(-1)


def packed_qkv(query, key, value):
    h, pad = query.shape[1] * 2 // 3, jnp.zeros_like(value[:, : value.shape[1] // 3])
    n = value.shape[1] * 2 // 3
    return jnp.concatenate([query[:, :h], key[:, :h], query[:, h:], value[:, :n], key[:, h:], value[:, n:], pad], axis=1)


def unpacked_qkv(first, second):
    h = first.shape[-1] // 2
    q = h // 2
    return (
        jnp.concatenate([first[..., :h], second[..., :q]], axis=-1),
        jnp.concatenate([first[..., h:], second[..., h : h + q]], axis=-1),
        jnp.concatenate([second[..., q:h], second[..., h + q : h + q + q // 2]], axis=-1),
    )


def segment_info(tree_ids, segment_ids, path_table, row_start, row_count, reach):
    seg_win = lax.dynamic_slice_in_dim(jnp.pad(segment_ids, (reach * row_count, 0)), row_start, (reach + 1) * row_count, 0)
    tree_own = lax.dynamic_slice_in_dim(tree_ids, row_start, row_count, 0)
    seg_own = seg_win[reach * row_count:]
    parent = path_rows(tree_own, seg_own, path_table)[:, 1]
    blocks = row_count // BLOCK
    rows = jnp.stack([parent.reshape(blocks, BLOCK), seg_own.reshape(blocks, BLOCK)], axis=1)
    return seg_win[:, None].astype(jnp.float32), jnp.pad(rows, ((0, 0), (0, 6), (0, 0))).astype(jnp.float32)


def gathered(fsdp, gain1, shift1, gain2, shift2, w_query, w_key, w_value, w_out, w_in, w_down):
    width = w_query.shape[1]
    n_ff = w_down.shape[0] // BLOCK
    packed = packed_qkv(w_query, w_key, w_value)
    full = [lax.all_gather(v, "fsdp", axis=0, tiled=True) for v in (packed, w_out, w_in, w_down)]
    vec = lax.all_gather(jnp.stack([gain1, shift1, gain2, shift2]), "fsdp", axis=1, tiled=True).astype(jnp.float32)
    half = packed.shape[1] // 2
    inner = full[2].reshape(width, fsdp, n_ff, BLOCK).transpose(2, 0, 1, 3).reshape(n_ff, width, -1)
    down = full[3].reshape(fsdp, n_ff, BLOCK, width).transpose(1, 0, 2, 3).reshape(n_ff, -1, width)
    return jnp.pad(vec, ((0, 4), (0, 0))), full[0][:, :half], full[0][:, half:], full[1], inner, down


def reduced(fsdp, sums, g1, g2, go, gin, gdn):
    width = go.shape[0]
    rows = width // fsdp
    n_ff = gin.shape[0]
    both = ("rep", "fsdp")
    rep = lax.axis_size("rep")

    def total(a):
        piece = lax.psum_scatter(reorder_rows(a.astype(jnp.float32), fsdp, rep), both, scatter_dimension=0, tiled=True)
        return lax.all_gather(piece.astype(jnp.bfloat16), "rep", axis=0, tiled=True)

    first, second, ro = (total(a).reshape(rows, -1) for a in (g1, g2, go))
    ri = total(gin.transpose(1, 0, 2)).reshape(rows, n_ff, -1).transpose(1, 0, 2)
    rd = total(gdn.reshape(n_ff, fsdp, BLOCK, width).transpose(1, 0, 2, 3)).reshape(n_ff, BLOCK, width)
    return lax.psum(sums, both), *unpacked_qkv(first, second), ro, ri, rd


def one_kernel(inputs, first_values, cotangent, kseg, qrow, gain1, shift1, gain2, shift2, w_query, w_key, w_value, w_out, w_in, w_down):
    fsdp = lax.axis_size("fsdp")
    rows, width = w_query.shape
    vec = jnp.pad(jnp.stack([gain1, shift1, gain2, shift2]).astype(jnp.float32), ((0, 4), (0, width - rows)))
    vec = jnp.roll(vec, lax.axis_index("fsdp") * rows, axis=1)
    kseg = jnp.broadcast_to(kseg, (kseg.shape[0], BLOCK))
    outputs, input_grad, first_grad, rq, rk, rv, ro, ri, rd, sums = layer_call(
        fsdp, inputs, first_values, cotangent, vec, w_query, w_key, w_value, w_out, w_in, w_down, kseg, qrow
    )
    rq, rk, rv, ro, ri, rd = (a.reshape(*a.shape[:-4], -1, a.shape[-1]) for a in (rq, rk, rv, ro, ri, rd))
    return outputs, input_grad, first_grad, sums, rq, rk, rv[:, : width // 2], ro, ri, rd


def several_kernels(reach, inputs, first_values, cotangent, kseg, qrow, gain1, shift1, gain2, shift2, w_query, w_key, w_value, w_out, w_in, w_down):
    row_count, width = inputs.shape
    fsdp = lax.axis_size("fsdp")
    lnp, w1, w2, wo, win, wdn = gathered(fsdp, gain1, shift1, gain2, shift2, w_query, w_key, w_value, w_out, w_in, w_down)
    x = jnp.concatenate([shifted(inputs, "fsdp", d) for d in range(reach, 0, -1)] + [inputs], axis=0)
    fv = jnp.concatenate([shifted(first_values, "fsdp", d) for d in range(reach, 0, -1)] + [first_values], axis=0)
    n1, q, k, v, mixed, lse, resid, n2 = forward_call(fsdp, reach, x, fv, lnp, w1, w2, wo, kseg, qrow)
    outputs, gin, gdn, go, gres, gmixed, sums = mlp_call(n2, cotangent, resid, mixed, lnp, win, wdn, wo)
    dq, dk, dv, wk, wv = backward_call(fsdp, reach, q, k, v, gmixed, lse, kseg, qrow)
    for d in range(1, reach + 1):
        early = slice((reach - d) * row_count, (reach - d + 1) * row_count)
        both = shifted(jnp.concatenate([wk[early], wv[early]], axis=1), "fsdp", -d).astype(jnp.float32)
        dk, dv = dk + both[:, :width], dv + both[:, width:]
    input_grad, first_grad, g1, g2, sums = projection_back_call(fsdp, reach, x, n1, dq, dk, dv, lnp, w1, w2, gres, sums)
    return outputs, input_grad, first_grad, *reduced(fsdp, sums, g1, g2, go, gin, gdn)


def on_device(
    inputs,
    first_values,
    cotangent,
    tree_ids,
    segment_ids,
    path_table,
    attn_gain,
    attn_shift,
    w_query,
    w_key,
    w_value,
    w_out,
    mlp_gain,
    mlp_shift,
    w_in,
    w_down,
):
    row_count, width = inputs.shape
    fsdp = lax.axis_size("fsdp")
    reach = 0
    for device_pos in range(fsdp):
        offset = device_pos * row_count % TREE_LEN
        reach = max(reach, (offset + row_count - 1) // row_count)
    row_start = lax.axis_index("fsdp") * row_count
    kseg, qrow = segment_info(tree_ids, segment_ids, path_table, row_start, row_count, reach)
    weights = (attn_gain, attn_shift, mlp_gain, mlp_shift, w_query, w_key, w_value, w_out, w_in, w_down)
    if lax.axis_size("rep") == 8 and reach == 1 and row_count == width:
        results = one_kernel(inputs, first_values, cotangent, kseg, qrow, *weights)
    else:
        results = several_kernels(reach, inputs, first_values, cotangent, kseg, qrow, *weights)
    outputs, input_grad, first_grad, sums, d_q, d_k, d_v, d_o, d_in, d_dn = results
    rows = w_query.shape[0]
    sums = lax.dynamic_slice_in_dim(sums, lax.axis_index("fsdp") * rows, rows, 1)
    d_in = d_in.reshape(-1, rows, fsdp, BLOCK).transpose(1, 2, 0, 3).reshape(rows, -1)
    d_q, d_k, d_v, d_o, d_in, d_dn = (a.astype(jnp.float32) for a in (d_q, d_k, d_v, d_o, d_in, d_dn.reshape(-1, width)))
    return (outputs, input_grad, first_grad, sums[0], sums[1], d_q, d_k, d_v, d_o, sums[2], sums[3], d_in, d_dn)


def solution(mesh):
    placed = (
        P(("rep", "fsdp"), None),
        P(("rep", "fsdp"), None),
        P(("rep", "fsdp"), None),
        P("rep"),
        P("rep"),
        P("rep", None, None),
        P("fsdp"),
        P("fsdp"),
        P("fsdp", None),
        P("fsdp", None),
        P("fsdp", None),
        P("fsdp", None),
        P("fsdp"),
        P("fsdp"),
        P("fsdp", None),
        P("fsdp", None),
    )
    return jax.shard_map(
        on_device,
        mesh=mesh,
        in_specs=placed,
        out_specs=(
            P(("rep", "fsdp"), None),
            P(("rep", "fsdp"), None),
            P(("rep", "fsdp"), None),
            P("fsdp"),
            P("fsdp"),
            P("fsdp", None),
            P("fsdp", None),
            P("fsdp", None),
            P("fsdp", None),
            P("fsdp"),
            P("fsdp"),
            P("fsdp", None),
            P("fsdp", None),
        ),
        check_vma=False,
    )
```

time: 1330 us -> 292 us (0.22)
  blocking collectives: 522 us -> 0 us
  matrix products: 271 us -> 0 us
  Pallas kernels: 0 us -> 260 us
  local copies, waits for them, and re-layouts: 220 us -> 19.5 us
  other arithmetic: 161 us -> 10.7 us
  waiting for transfers between devices: 124 us -> 0 us
  between operations: 16.8 us -> 0.74 us
    unnamed x3 -> x0, blocking collectives: 463 us -> none
    dot_general x60 -> x0, matrix products: 271 us -> none  [the longest x12 63.7 us: pair_scores(): jnp.einsum('qhd,khd->hqk', query_pair, key_pair, preferred_element_type=j...]
    pallas_call x0 -> x1, Pallas kernels: none -> 260 us  [layer_call(): pl.pallas_call(body, out_shape=outs, in_specs=[any_] * 11 + [VM], out_spe...]
    all_gather x7 -> x0, waiting for transfers between devices: 77.4 us -> none  [the longest x1 63.1 us: on_device(): lax.all_gather(w_in, 'fsdp', axis=0, tiled=True)]
    reshape x21 -> x0, local copies, waits for them, and re-layouts: 74.3 us -> none  [the longest x14 63.8 us: reorder_rows(): grad_block.reshape(fsdp_count, rep_count, -1).transpose(1, 0, 2).reshape(-1)]
    all_gather x5 -> x0, blocking collectives: 59.5 us -> none  [the longest x1 23.2 us: on_device(): lax.all_gather(w_value, 'fsdp', axis=0, tiled=True)]
    unnamed x159 -> x16, local copies, waits for them, and re-layouts: 58.6 us -> 5.91 us
    convert_element_type x11 -> x6, other arithmetic: 58.2 us -> 9.02 us  [the longest x4 7.62 us: on_device(): a.astype(jnp.float32)]
  transfers between devices with their start and end apart: 9 -> 0, of which waited for: 4 -> 0; matrix products, arithmetic and copies ran while one was open for 22% -> 0% of each run, Pallas kernels for 0% -> 0%
where the time goes in v2:
time: 292 us; the launch traced here: 291 us
  Pallas kernels  260 us (89%)
  local copies, waits for them, and re-layouts  19.5 us (7%)
  other arithmetic  10.7 us (4%)
    pallas_call x1, Pallas kernels, layer_call(): pl.pallas_call(body, out_shape=outs, in_specs=[any_] * 11 + [VM], out_spe...  260 us
    convert_element_type x4, other arithmetic, on_device(): a.astype(jnp.float32)  7.62 us
    convert_element_type x3, local copies, waits for them, and re-layouts, on_device(): a.astype(jnp.float32)  6.54 us
    unnamed x16, local copies, waits for them, and re-layouts  5.91 us

profile of v2, /device:TPU:0, one launch (start us, length us, event | category | flops | bytes accessed | tf_op | source)
XLA Modules:
  0.0 291.1 jit_solution(18058703545055524884)
XLA Ops:
  0.7 0.7 stack.18
  1.3 0.7 stack.19
  2.0 0.7 stack.20
  2.6 0.7 stack.21
  3.3 0.7 copy.35
  4.1 0.8 multiply_add_fusion
  4.9 0.8 fusion.15
  5.7 0.7 fusion.7.refs_3_
  7.2 1.6 pad.18
  8.8 1.1 broadcast_in_dim.2.refs_10_
  10.0 260.2 %shard_map.255 = (bf16[768,768]{1,0:T(8,128)(2,1)}, f32[768,768]{1,0:T(8,128)}, f32[768,384]{1,0:T(8,128)}, bf16[2,2,48,768]{3,2,1,0:T(8,128)(2,1)}, bf16[2,2,48...) custom-call(bf16[768,768]{1,0:T(8,128)(2,1)} %refs_0_.1, ...), custom_call_target="tpu_custom_call" | custom-call | tf_op jit(solution)/shard_map/pallas_call | solution.py:1103
  270.2 1.5 fusion.16
  271.7 1.6 slice_convert_fusion
  273.4 1.9 bitcast_convert_fusion.3
  275.3 1.1 bitcast_convert_fusion.1
  276.4 1.8 reshape.108
  278.2 3.1 %copy.38 = f32[6,192,4,128]{3,0,2,1:T(8,128)S(1)} copy(f32[6,192,4,128]{3,2,1,0:T(4,128)} %reshape.108) | data formatting | bytes 4718592 | tf_op jit(solution)/shard_map/convert_element_type | solution.py:1249
  281.3 1.7 reshape.106
  283.0 2.9 %bitcast_convert_fusion = f32[768,768]{1,0:T(8,128)} fusion(bf16[6,2,2,32,768]{4,3,2,1,0:T(8,128)(2,1)} %get-tuple-element.32), kind=kLoop, calls=%fused_computation.1 | loop fusion | flops 589824 | bytes 3538944 | tf_op jit(solution)/shard_map/convert_element_type | solution.py:1249
  285.9 1.0 copy.42
  286.9 1.1 copy-done
  288.0 1.4 copy.43
  289.4 0.7 copy-done.2
  290.1 1.0 copy.44
  (18 shorter events, 0.9 us)
Async XLA Ops:
  270.2 5.1 %copy-start.4 = (bf16[2,2,48,768]{3,2,1,0:T(8,128)(2,1)S(1)}, bf16[2,2,48,768]{3,2,1,0:T(8,128)(2,1)}, u32[]{:S(2)}) copy-start(bf16[2,2,48,768]{3,2,1,0:T(8,128)(2,1)} %get-tuple-element.28) | copy-start | bytes 884740
  270.2 5.1 %copy-start.5 = (bf16[2,2,48,768]{3,2,1,0:T(8,128)(2,1)S(1)}, bf16[2,2,48,768]{3,2,1,0:T(8,128)(2,1)}, u32[]{:S(2)}) copy-start(bf16[2,2,48,768]{3,2,1,0:T(8,128)(2,1)} %get-tuple-element.30) | copy-start | bytes 884740
  273.4 3.0 %copy-start.1 = (bf16[6,2,2,48,512]{4,3,2,1,0:T(8,128)(2,1)S(1)}, bf16[6,2,2,48,512]{4,3,2,1,0:T(8,128)(2,1)}, u32[]{:S(2)}) copy-start(bf16[6,2,2,48,512]{4,3,2,1,0:T(8,128)(2,1)} %get-tuple-element.31) | copy-start | bytes 3538948
  283.0 2.9 %copy-start.3 = (bf16[768,768]{1,0:T(8,128)(2,1)S(1)}, bf16[768,768]{1,0:T(8,128)(2,1)}, u32[]{:S(2)}) copy-start(bf16[768,768]{1,0:T(8,128)(2,1)} %get-tuple-element.54) | copy-start | bytes 3538948
  285.9 2.1 copy-start
  288.0 2.1 copy-start.2

commit v3 on v2

--- a/solution.py
+++ b/solution.py
@@ -95,7 +95,7 @@
         @pl.loop(0, self.F * 4)
         def _(i):
             a, b, c = i // 4, lax.rem(i // 2, 2), lax.rem(i, 2)
-            self.r1[a, b, c] = (self.r1[a, b, c].astype(jnp.float32) + self.buf[a, b, c, :, self.cols].astype(jnp.float32)).astype(jnp.bfloat16)
+            self.r1[a, b, c] = self.r1[a, b, c] + self.buf[a, b, c, :, self.cols]
         if self.xf: self.send(self.r1.at[:, :, 1 - pc.x], self.r2, 1, pc.xn)
         else: self.send(self.r1.at[:, 1 - pc.y], self.r2, 1, pc.yn)
     def p3(self):
@@ -105,7 +105,7 @@
         def _(i):
             a, b = i // 2, lax.rem(i, 2)
             mine = self.r1[a, b, pc.x] if self.xf else self.r1[a, pc.y, b]
-            self.r2[a, b] = (self.r2[a, b].astype(jnp.float32) + mine.astype(jnp.float32)).astype(jnp.bfloat16)
+            self.r2[a, b] = self.r2[a, b] + mine
         if self.xf: self.send(self.r2.at[:, 1 - pc.y], self.r3, 2, pc.yn)
         else: self.send(self.r2.at[:, 1 - pc.x], self.r3, 2, pc.xn)
     def p4(self):
@@ -114,7 +114,7 @@
         q = pc.y if self.xf else pc.x
         @pl.loop(0, self.F)
         def _(a):
-            self.r3[a] = (self.r3[a].astype(jnp.float32) + self.r2[a, q].astype(jnp.float32)).astype(jnp.bfloat16)
+            self.r3[a] = self.r3[a] + self.r2[a, q]
         for o in pc.others: self.send(self.r3.at[o], self.r4.at[pc.f], 3, pc.zdev(o))
     def p5(self):
         pc = self.pc
@@ -213,48 +213,59 @@
     return pl.ds(pl.multiple_of(start, BLOCK), size)
 
 
-def make_bias(span, kseg, qrow, bias):
-    @pl.loop(0, span.blocks)
+def make_bias(span, segs, trees, table, bias, extra=0):
+    @pl.loop(0, span.blocks + extra)
     def _(i):
-        b, base = span.kind(i), span.base(i)
+        b = span.kind(i)
+        first = ((span.first + i) // span.tree) * span.tree
         q_pos = b * BLOCK + lax.broadcasted_iota(jnp.int32, (1, BLOCK), 1)
-        parent, own = qrow[i, 0:1, :], qrow[i, 1:2, :]
-
-        def put(slot, key, count):
-            k_pos = key + lax.broadcasted_iota(jnp.int32, (count, 1), 0)
-            seg = kseg[rows_at(base + key, count), :]
-            seen = (k_pos <= q_pos) & ((seg == parent) | (seg == own))
-            bias[i, pl.ds(slot, count), :] = jnp.where(seen, 0.0, far_below)
-
-        for n in range(TRUNK // BLOCK):
-
-            @pl.when(b == n)
-            def _():
-                put(0, 0, (n + 1) * BLOCK)
-
-        @pl.when(b >= 4)
-        def _():
-            put(256, b * BLOCK, BLOCK)
+        own = segs[pl.ds(span.first + i, 1), :]
+
+        def put(slot, key, related):
+            k_pos = key * BLOCK + lax.broadcasted_iota(jnp.int32, (BLOCK, 1), 0)
+            column = jnp.broadcast_to(f32(segs[pl.ds(first + key, 1), :]), (BLOCK, BLOCK)).T
+            seen = (k_pos <= q_pos) & (column == f32(related))
+            bias[i, pl.ds(slot, BLOCK), :] = jnp.where(seen, 0.0, far_below)
+
+        put(256, b, own)
 
         @pl.when(b >= 6)
         def _():
-            put(0, TRUNK, 256)
-
-
-def by_kind(b, body):
+            tree = trees[first * BLOCK]
+            parent = jnp.zeros_like(own)
+            for leaf in range(table.shape[1]):
+                parent = jnp.where(own == leaf, table[tree, leaf, 1], parent)
+            put(0, 4, parent)
+            put(BLOCK, 5, parent)
+
+
+def by_kind(b, body, lent=None):
     for n in range(TRUNK // BLOCK):
 
         @pl.when(b == n)
         def _():
-            body([(0, (n + 1) * BLOCK, 0)])
+            body([(0, n * BLOCK, None)][: n] + [(None, BLOCK, 256)])
 
     @pl.when((b >= 4) & (b < 6))
     def _():
         body([(0, 512, None), (None, BLOCK, 256)])
 
-    @pl.when(b >= 6)
-    def _():
-        body([(0, 512, None), (512, 256, 0), (None, BLOCK, 256)])
+    leaf_parts = [(0, 512, None), (512, 256, 0), (None, BLOCK, 256)]
+    if lent is None:
+
+        @pl.when(b >= 6)
+        def _():
+            body(leaf_parts)
+
+    else:
+
+        @pl.when((b >= 6) & jnp.logical_not(lent))
+        def _():
+            body(leaf_parts)
+
+        @pl.when((b >= 6) & lent)
+        def _():
+            body(leaf_parts, only_own=True)
 
 
 def stacked(pair):
@@ -292,11 +303,11 @@
         dst[:, pl.ds(pl.multiple_of(j * BLOCK, BLOCK), BLOCK)] = src[rows_at(j * BLOCK, BLOCK), pair_cols(p)].T
 
 
-def attend_pair(span, p, q, k, v, bias, v_t, mixed, lse):
-    transpose_pair(v, p, span.start, span.window + span.rows, v_t)
+def attend_pair(span, p, lo, hi, start, stop, q, k, v, bias, v_t, mixed, lse):
+    transpose_pair(v, p, start, stop, v_t)
     cols = pair_cols(p)
 
-    @pl.loop(0, span.blocks)
+    @pl.loop(lo, hi)
     def _(i):
         b = span.kind(i)
         own = rows_at(i * BLOCK, BLOCK)
@@ -369,22 +380,24 @@
         n2[rows, :] = bf(hat * gain + shift)
 
 
-def forward_kernel(fsdp, reach, x, fv, lnp, w1, w2, wo, kseg, qrow, n1, q, k, v, mixed, lse, resid, n2, bias, v_t):
+def forward_kernel(fsdp, reach, x, fv, lnp, w1, w2, wo, segs, trees, table, n1, q, k, v, mixed, lse, resid, n2, bias, v_t):
     span = Span(fsdp, q.shape[0], reach, lax.axis_index("fsdp"))
-    make_bias(span, kseg, qrow, bias)
+    rows = q.shape[0]
+    make_bias(span, segs, trees, table, bias)
     project(span, x, fv, lnp, w1, w2, n1, q, k, v)
 
     @pl.loop(0, q.shape[1] // (2 * HEAD))
     def _(p):
-        attend_pair(span, p, q, k, v, bias, v_t, mixed, lse)
+        attend_pair(span, p, 0, span.blocks, span.start, span.window + rows, q, k, v, bias, v_t, mixed, lse)
 
     branch_out(span, x, lnp, mixed, wo, resid, n2)
 
 
 VM = pl.BlockSpec(memory_space=pltpu.VMEM)
-
-
-def forward_call(fsdp, reach, x, fv, lnp, w1, w2, wo, kseg, qrow):
+SM = pl.BlockSpec(memory_space=pltpu.SMEM)
+
+
+def forward_call(fsdp, reach, x, fv, lnp, w1, w2, wo, segs, trees, table):
     window, width = x.shape
     rows = window // (reach + 1)
     s = jax.ShapeDtypeStruct
@@ -396,10 +409,10 @@
     )
     return pl.pallas_call(
         functools.partial(forward_kernel, fsdp, reach),
-        out_shape=outs, in_specs=[VM] * 8, out_specs=[VM] * 8,
-        scratch_shapes=[pltpu.VMEM((blocks, TRUNK, BLOCK), full), pltpu.VMEM((2 * HEAD, window), low)],
+        out_shape=outs, in_specs=[VM] * 7 + [SM] * 2, out_specs=[VM] * 8,
+        scratch_shapes=[pltpu.VMEM((blocks, 3 * BLOCK, BLOCK), full), pltpu.VMEM((2 * HEAD, window), low)],
         compiler_params=pltpu.CompilerParams(vmem_limit_bytes=50 << 20),
-    )(x, fv, lnp, w1, w2, wo, kseg, qrow)
+    )(x, fv, lnp, w1, w2, wo, segs, trees, table)
 
 
 GELU_A = 0.7978845608028654
@@ -512,7 +525,7 @@
     )(n2, cot, resid, mixed, lnp, win, wdn, wo)
 
 
-def attend_back_pair(span, p, q, k, v, gmixed, bias, lse, k_t, dk_acc, dv_acc, dq):
+def attend_back_pair(span, p, q, k, v, gmixed, bias, lse, k_t, dk_acc, dv_acc, dq, lent=None):
     transpose_pair(k, p, span.start, span.window + span.rows, k_t)
     cols = pair_cols(p)
 
@@ -529,7 +542,7 @@
         q2, g2 = stacked(q[own, cols]), stacked(gmixed[own, cols])
         l = lse[p, pl.ds(i, 1), :]
 
-        def body(parts):
+        def body(parts, only_own=False):
             rows = [part_rows(span, i, b, part) for part in parts]
             probs = [jnp.exp(part_scores(q2, k[r, cols], bias, i, part) - l) for r, part in zip(rows, parts)]
             gw = [nt(v[r, cols], g2) for r in rows]
@@ -537,16 +550,43 @@
             gs = [bf(a * (g - inner)) for a, g in zip(probs, gw)]
             out = sum(mm(k_t[:, r], g) for r, g in zip(rows, gs))
             dq[own, cols] = bf(unstacked_t(out) * HEAD ** (-0.5))
-            for r, a, g in zip(rows, probs, gs):
+            for r, a, g, part in zip(rows, probs, gs, parts):
+                if only_own and part[0] is not None:
+                    continue
                 dk_acc[r, :] += mm(g, q2)
                 dv_acc[r, :] += mm(bf(a), g2)
 
-        by_kind(b, body)
-
-
-def backward_kernel(fsdp, reach, q, k, v, gmixed, lse, kseg, qrow, dq, dk, dv, wk, wv, bias, k_t, dk_acc, dv_acc):
+        by_kind(b, body, None if lent is None else lent & (i < span.tree - 6))
+
+
+def lent_sums(gmixed, mixed):
+    heads = lax.broadcasted_iota(jnp.int32, (16, mixed.shape[1]), 0)
+    cols = lax.broadcasted_iota(jnp.int32, (16, mixed.shape[1]), 1)
+    pick = ((cols >= heads * HEAD) & (cols < heads * HEAD + HEAD)).astype(jnp.float32)
+    return lax.dot_general(pick, f32(gmixed) * f32(mixed), (((1,), (1,)), ((), ())), precision=lax.Precision.HIGHEST, preferred_element_type=jnp.float32)
+
+
+def borrowed_back(span, p, q, g, k, v, bias, lse, inner, dk, dv):
+    cols = pair_cols(p)
+
+    @pl.loop(0, 2)
+    def _(j):
+        r = rows_at(j * BLOCK, BLOCK)
+        q2, g2 = stacked(q[r, cols]), stacked(g[r, cols])
+        l = lse[p, pl.ds(j, 1), :]
+        mean = inner[p, pl.ds(j, 1), :]
+        for part in ((0, 512, None), (512, 256, 0)):
+            rows = rows_at(span.window + part[0], part[1])
+            own = rows_at(part[0], part[1])
+            probs = jnp.exp(part_scores(q2, k[rows, cols], bias, span.blocks + j, part) - l)
+            gs = bf(probs * (nt(v[rows, cols], g2) - mean))
+            dk[own, cols] += mm(gs, q2)
+            dv[own, cols] += mm(bf(probs), g2)
+
+
+def backward_kernel(fsdp, reach, q, k, v, gmixed, lse, segs, trees, table, dq, dk, dv, wk, wv, bias, k_t, dk_acc, dv_acc):
     span = Span(fsdp, q.shape[0], reach, lax.axis_index("fsdp"))
-    make_bias(span, kseg, qrow, bias)
+    make_bias(span, segs, trees, table, bias)
     wk[...] = jnp.zeros_like(wk)
     wv[...] = jnp.zeros_like(wv)
 
@@ -564,20 +604,20 @@
             wv[r, cols] = bf(dv_acc[r, :])
 
 
-def backward_call(fsdp, reach, q, k, v, gmixed, lse, kseg, qrow):
+def backward_call(fsdp, reach, q, k, v, gmixed, lse, segs, trees, table):
     window, width = k.shape
     rows = q.shape[0]
     s, low, full = jax.ShapeDtypeStruct, jnp.bfloat16, jnp.float32
     early = window - rows
     outs = (s((rows, width), low), s((rows, width), full), s((rows, width), full), s((early, width), low), s((early, width), low))
     return pl.pallas_call(
-        functools.partial(backward_kernel, fsdp, reach), out_shape=outs, in_specs=[VM] * 7, out_specs=[VM] * 5,
+        functools.partial(backward_kernel, fsdp, reach), out_shape=outs, in_specs=[VM] * 6 + [SM] * 2, out_specs=[VM] * 5,
         scratch_shapes=[
-            pltpu.VMEM((rows // BLOCK, TRUNK, BLOCK), full), pltpu.VMEM((2 * HEAD, window), low),
+            pltpu.VMEM((rows // BLOCK, 3 * BLOCK, BLOCK), full), pltpu.VMEM((2 * HEAD, window), low),
             pltpu.VMEM((window, 2 * HEAD), full), pltpu.VMEM((window, 2 * HEAD), full),
         ],
         compiler_params=pltpu.CompilerParams(vmem_limit_bytes=58 << 20),
-    )(q, k, v, gmixed, lse, kseg, qrow)
+    )(q, k, v, gmixed, lse, segs, trees, table)
 
 
 def projection_back(span, x, n1, dq, dk, dv, lnp, w1, w2, gres, gin, gfirst, g1, g2, sums, n1_t, cat1, cat2):
@@ -658,6 +698,9 @@
         return self.make(c)
 
 
+N_IN = 13
+
+
 class Scratch:
     def __init__(self):
         self.names, self.shapes = [], []
@@ -673,9 +716,9 @@
 
 
 def layer_kernel(fsdp, n_ff, scratch, n_out, *refs):
-    (inputs, first, cot_in, vec, a_q, a_k, a_v, a_o, a_in, a_dn, kseg, qrow) = refs[:12]
-    (outputs, gin, gfirst, rs_q, rs_k, rs_v, rs_o, rs_in, rs_dn, rs_vec) = refs[12 : 12 + n_out]
-    m = scratch.bind(refs[12 + n_out :])
+    (inputs, first, cot_in, a_q, a_k, a_v, a_o, a_in, a_dn, norms, segs, trees, table) = refs[:N_IN]
+    (outputs, gin, gfirst, rs_q, rs_k, rs_v, rs_o, rs_in, rs_dn, rs_vec) = refs[N_IN : N_IN + n_out]
+    m = scratch.bind(refs[N_IN + n_out :])
     pc = Place(fsdp)
     f = pc.f
     rows, width = cot_in.shape
@@ -688,17 +731,32 @@
     mixed, cot = m.mixed.reshape(rows, width), m.cot.reshape(rows, width)
     x, q, k, v, n1, n2, tr = m.x, m.q, m.k, m.v, m.n1, m.n2, m.tr
 
+    guest = span.kind(0) == 6
+    host = (f < last) & (lax.rem(span.first + span.blocks, span.tree) == 6)
+    gq, gg = x.at[pl.ds(0, 2 * BLOCK)], x.at[pl.ds(2 * BLOCK, 2 * BLOCK)]
+
+    def lend(i, src, dst):
+        return pltpu.make_async_remote_copy(src_ref=src, dst_ref=dst, send_sem=m.b_send.at[i], recv_sem=m.b_recv.at[i], device_id=(pc.r, f - 1), device_id_type=MESH)
+
+    two = pl.ds(0, 2 * BLOCK)
+    lent = [lambda: lend(0, q.at[two], gq), lambda: lend(1, m.lse, m.g_lse), lambda: lend(2, m.inner, m.g_inner)]
+
+    def lent_pair(p):
+        return lend(3 + p, m.gmixed.at[two, pair_cols(p)], gg.at[:, pair_cols(p)])
+
     def local(src, dst, sem):
         c = pltpu.make_async_copy(src, dst, sem)
         c.start()
         return c
 
-    lv = local(vec, m.vec.at[f], m.l_sem.at[0])
-    lw = [local(a, b.at[f], m.l_sem.at[1 + i]) for i, (a, b) in enumerate(((a_q, m.b_q), (a_k, m.b_k), (a_v, m.b_v), (a_o, m.b_o)))]
+    half = width // 2
+    lw = [
+        local(a, b.at[f, :, :, :, pl.ds(0, a.shape[-1])], m.l_sem.at[1 + i])
+        for i, (a, b) in enumerate(((a_q, m.b_q), (a_k, m.b_k), (a_v, m.b_v), (a_o, m.b_o)))
+    ]
     lx = local(inputs, x.at[pl.ds(rows, rows)], m.l_sem.at[5])
     lf = local(first, v.at[pl.ds(rows, rows), pl.ds(width // 2, width // 2)], m.l_sem.at[6])
     lc = local(cot_in, cot, m.l_sem.at[7])
-    lk = local(kseg, m.dk_acc, m.l_sem.at[8])
     group = a_in.shape[-1] // fsdp
 
     def own_chunk(c, act):
@@ -711,79 +769,69 @@
     def _(c):
         own_chunk(c, lambda d: d.start())
 
+    pad = m.b_v.shape[-1] - half
+    m.b_v[f, :, :, :, half:] = jnp.zeros((2, 2, m.b_v.shape[3], pad), jnp.bfloat16)
+    own_norms = jnp.concatenate([f32(norms[...]), jnp.zeros((4, norms.shape[1]), jnp.float32)], axis=0)
+    own_norms = jnp.concatenate([own_norms, jnp.zeros((8, width - norms.shape[1]), jnp.float32)], axis=1)
+    m.vec[f] = pltpu.roll(own_norms, f * norms.shape[1], 1)
     pc.barrier()
-    lv.wait()
     for o in pc.others:
         pltpu.make_async_remote_copy(
             src_ref=m.vec.at[f], dst_ref=m.vec.at[f], send_sem=m.v_send.at[0], recv_sem=m.v_recv.at[0], device_id=pc.zdev(o), device_id_type=MESH
         ).start()
     gat = [Gather(pc, b, m.g_send.at[i], m.g_recv.at[i], xf) for i, (b, xf) in enumerate(((m.b_q, True), (m.b_k, False), (m.b_v, True), (m.b_o, False)))]
-    for l, g in zip(lw[:3], gat):
+    for l, g in zip(lw, gat):
         l.wait()
         g.z_start()
 
     next_start = Span(fsdp, rows, 1, f + 1).start
 
     def window(t):
-        r = pl.ds(t * tile, tile)
+        r, own = pl.ds(t * tile, tile), pl.ds(rows + t * tile, tile)
         nxt = (pc.r, f + 1)
         return [
-            pltpu.make_async_remote_copy(src_ref=inputs.at[r], dst_ref=x.at[r], send_sem=m.w_send.at[0, t], recv_sem=m.w_recv.at[0, t], device_id=nxt, device_id_type=MESH),
+            pltpu.make_async_remote_copy(src_ref=x.at[own], dst_ref=x.at[r], send_sem=m.w_send.at[0, t], recv_sem=m.w_recv.at[0, t], device_id=nxt, device_id_type=MESH),
             pltpu.make_async_remote_copy(
-                src_ref=first.at[r], dst_ref=v.at[r, pl.ds(width // 2, width // 2)], send_sem=m.w_send.at[1, t], recv_sem=m.w_recv.at[1, t], device_id=nxt, device_id_type=MESH
+                src_ref=v.at[own, pl.ds(half, half)], dst_ref=v.at[r, pl.ds(half, half)], send_sem=m.w_send.at[1, t], recv_sem=m.w_recv.at[1, t], device_id=nxt, device_id_type=MESH
             ),
         ]
 
-    for t in range(tiles):
-
-        @pl.when((f < last) & (t * tile >= next_start))
-        def _():
-            for c in window(t):
-                c.start()
-
-    lw[3].wait()
-    gat[3].z_start()
     ff = Chunks(
         n_ff,
         lambda c: [Gather(pc, m.b_in.at[c], m.gi_send.at[c], m.gi_recv.at[c], True), Gather(pc, m.b_dn.at[c], m.gd_send.at[c], m.gd_recv.at[c], False)],
     )
 
-    @pl.loop(0, n_ff)
-    def _(c):
-        own_chunk(c, lambda d: d.wait())
-        for g in ff(c):
-            g.z_start()
-
+    make_bias(span, segs, trees, table, m.bias, jnp.where(host, 2, 0))
     for g in gat[:3]:
         g.z_wait()
         g.a_start()
-    lk.wait()
-    make_bias(span, m.dk_acc, qrow, m.bias)
-    for g in gat[:3]:
-        g.a_wait()
-        g.b_start()
-    gat[3].z_wait()
-    gat[3].a_start()
+    lx.wait()
+    lf.wait()
+    for t in range(tiles):
+
+        @pl.when((f < last) & (t * tile >= next_start))
+        def _():
+            for c in window(t):
+                c.start()
+
     v3 = m.vec.at[pl.ds(0, last)]
     drain(v3, m.v_recv.at[0])
     drain(v3, m.v_send.at[0])
     m.lnp[...] = functools.reduce(lambda a, b: a + b, [m.vec[j] for j in range(fsdp)])
     gain, shift = m.lnp[0:1, :], m.lnp[1:2, :]
-    lx.wait()
 
     @pl.loop(0, tiles)
     def _(t):
         n1[rows_at(t * tile, tile), :] = norm_tile(x[rows_at(rows + t * tile, tile), :], gain, shift)
 
     for g in gat[:3]:
+        g.a_wait()
+        g.b_start()
+    for g in gat[:3]:
         g.b_wait()
         g.c_start()
-    gat[3].a_wait()
-    gat[3].b_start()
-    lf.wait()
     for g in gat[:3]:
         g.c_wait()
-    half = width // 2
 
     @pl.loop(0, tiles)
     def _(t):
@@ -793,6 +841,28 @@
         k[r, :] = bf(mm(n, w_k[...]))
         v[r, :half] = bf(mm(n, w_v[:, :half]))
 
+    pairs = width // (2 * HEAD)
+    here = lax.rem(span.tree - lax.rem(span.first, span.tree), span.tree)
+    here = jnp.minimum(here, span.blocks)
+    border = span.base(here)
+
+    @pl.loop(0, pairs)
+    def _(p):
+        attend_pair(span, p, here, span.blocks, border, 2 * rows, q, k, v, m.bias, m.turned, mixed, m.lse)
+        for when, step in ((0, lambda: (gat[3].z_wait(), gat[3].a_start())), (2, lambda: (gat[3].a_wait(), gat[3].b_start())), (4, lambda: (gat[3].b_wait(), gat[3].c_start()))):
+
+            @pl.when(p == when)
+            def _():
+                step()
+
+        @pl.when(p >= pairs // 2)
+        def _():
+            for j in range(2):
+                c = 2 * (p - pairs // 2) + j
+                own_chunk(c, lambda d: d.wait())
+                for g in ff(c):
+                    g.z_start()
+
     for t in range(tiles):
 
         @pl.when(t * tile >= span.start)
@@ -807,15 +877,19 @@
         k[r, :] = bf(mm(n, w_k[...]))
         v[r, :half] = bf(mm(n, w_v[:, :half]))
 
-    gat[3].b_wait()
-    gat[3].c_start()
-
-    pairs = width // (2 * HEAD)
 
     @pl.loop(0, pairs)
     def _(p):
-        attend_pair(span, p, q, k, v, m.bias, m.turned, mixed, m.lse)
-        gather_steps(ff, p)
+        attend_pair(span, p, 0, here, span.start, border, q, k, v, m.bias, m.turned, mixed, m.lse)
+
+        @pl.when(p >= pairs // 2)
+        def _():
+            gather_steps(ff, p - pairs // 2)
+
+    @pl.when(guest)
+    def _():
+        lent[0]().start()
+        lent[1]().start()
 
     gat[3].c_wait()
     branch_out(span, x, m.lnp, mixed, w_o, m.resid, n2)
@@ -837,7 +911,7 @@
 
     @pl.loop(0, n_ff)
     def _(c):
-        gather_steps(ff, c + pairs)
+        gather_steps(ff, c + 3)
         b_in, b_dn = flat(m.b_in.at[c]), flat(m.b_dn.at[c])
 
         def put_in(val):
@@ -859,6 +933,18 @@
     second_norm_back(rows, m.lnp, m.resid, cot, m.acc2, m.resid, n2, m.sums)
     branch_back(rows, n2, w_o, m.gmixed)
 
+    @pl.when(guest)
+    def _():
+        sums = lent_sums(m.gmixed[two, :], mixed[two, :])
+        for p in range(pairs):
+            for j in range(2):
+                at = slice(j * BLOCK, (j + 1) * BLOCK)
+                m.inner[p, j:j + 1, :] = jnp.concatenate([sums[2 * p:2 * p + 1, at], sums[2 * p + 1:2 * p + 2, at]], axis=1)
+        lent[2]().start()
+        for p in range(pairs):
+            lent_pair(p).start()
+
+
     @pl.loop(0, width // tile)
     def _(t):
         r = rows_at(t * tile, tile)
@@ -866,22 +952,38 @@
 
     lo.wait()
 
-    @pl.when(f < last)
+    @pl.when((f < last) & jnp.logical_not(host))
     def _():
         pl.semaphore_signal(m.ready, inc=1, device_id=(pc.r, f + 1), device_id_type=MESH)
 
-    @pl.when(f > 0)
+    for t in range(tiles):
+
+        @pl.when((f < last) & (t * tile >= next_start))
+        def _():
+            for c in window(t):
+                c.wait_send()
+
+    @pl.when(guest)
     def _():
-        pl.semaphore_wait(m.ready, 1)
+        lent[0]().wait_send()
 
     transpose_all(n1, tr)
+    mid, end = half + (pairs // 2 - 1) * BLOCK, width
+    wide = 2 * (mid - half)
+    rest = lambda ref: (ref.at[..., pl.ds(0, wide)], ref.at[..., pl.ds(wide, 2 * BLOCK)])
+    narrow = lambda refs, i: [ref.at[..., pl.ds(0, wide // 2) if i == 0 else pl.ds(wide // 2, BLOCK)] for ref in refs]
+    buf1, buf2 = rest(m.cot)
+    res1, res2 = rest(rs_k)
     stat = [
         Reduce(pc, b, *scr, res, m.rs_send.at[i], m.rs_recv.at[i], xf)
         for i, (b, scr, res, xf) in enumerate(
-            ((m.b_o, m.r_o, rs_o, True), (m.mixed, m.r_q, rs_q, False), (m.cot, m.r_k, rs_k, True), (m.g_v, m.r_v, rs_v, False))
+            (
+                (m.b_o, m.r_o, rs_o, True), (m.mixed, m.r_q, rs_q, False), (m.g_v, m.r_v, rs_v, True),
+                (buf1, narrow(m.r_k, 0), res1, True), (buf2, narrow(m.r_k, 1), res2, False),
+            )
         )
     ]
-    red_o, red_q, red_k, red_v = stat
+    red_o, red_0, red_v, red_1, red_2 = stat
 
     def early(t, p):
         r, cols = pl.ds(t * tile, tile), pair_cols(p)
@@ -896,15 +998,53 @@
 
     dk, dv = m.acc1, m.acc2
 
+    def complete(p):
+        cols = pl.ds(p * BLOCK, BLOCK)
+        for t in range(tiles):
+            r = pl.ds(t * tile, tile)
+
+            @pl.when((f < last) & jnp.logical_not(host) & (t * tile >= next_start))
+            def _():
+                for j, own in enumerate((dk, dv)):
+                    drain(m.back.at[j, r, cols], m.e_recv.at[j, p, t])
+                    own[r, cols] += f32(m.back[j, r, cols])
+
+            k[r, cols] = bf(dk[r, cols])
+            if p < pairs // 2:
+                v[r, cols] = bf(dv[r, cols])
+
+    def weight_grad(dst, at, grad, lo, hi):
+        @pl.loop(0, width // tile)
+        def _(t):
+            r = rows_at(t * tile, tile)
+            dst[r, at:at + hi - lo] = bf(mm(tr[r, :], grad[pl.ds(0, rows), lo:hi]))
+
+    d_0, d_v, d_1 = flat(m.mixed), flat(m.g_v), flat(m.cot)
+
+    def run_0():
+        for p in range(pairs // 2):
+            complete(p)
+        weight_grad(d_0, 0, q, 0, half)
+        weight_grad(d_0, half, k, 0, half)
+        red_0.p1()
+        d_v[:, half:] = jnp.zeros((width, d_v.shape[1] - half), jnp.bfloat16)
+        weight_grad(d_v, 0, v, 0, half)
+        red_v.p1()
+
     @pl.loop(0, pairs)
     def _(p):
         cols = pair_cols(p)
-        attend_back_pair(span, p, q, k, v, m.gmixed, m.bias, m.lse, m.turned, m.dk_acc, m.dv_acc, q)
+        attend_back_pair(span, p, q, k, v, m.gmixed, m.bias, m.lse, m.turned, m.dk_acc, m.dv_acc, q, guest)
         dk[:, cols] = m.dk_acc[rows:, :]
         dv[:, cols] = m.dv_acc[rows:, :]
+
+        @pl.when((p == 0) & (f > 0) & jnp.logical_not(guest))
+        def _():
+            pl.semaphore_wait(m.ready, 1)
+
         for t in range(tiles):
 
-            @pl.when((f > 0) & (t * tile >= span.start))
+            @pl.when((f > 0) & jnp.logical_not(guest) & (t * tile >= span.start))
             def _():
                 r = pl.ds(t * tile, tile)
                 x[r, cols] = bf(m.dk_acc[r, :])
@@ -913,66 +1053,61 @@
                     c.start()
 
         reduce_steps(red, n_ff + p)
+
+        @pl.when(host)
+        def _():
+            @pl.when(p == 0)
+            def _():
+                for c in lent:
+                    c().wait_recv()
+
+            lent_pair(p).wait_recv()
+            borrowed_back(span, p, gq, gg, k, v, m.bias, m.g_lse, m.g_inner, dk, dv)
+
         for s in range(6):
 
             @pl.when(p == s)
             def _():
                 Reduce.STAGES[s](red_o)
 
-    d_q = flat(m.mixed)
-    wide = width // tile
-
-    def weight_grad(dst, grad, cols):
-        @pl.loop(0, wide)
-        def _(t):
-            r = rows_at(t * tile, tile)
-            dst[r, :cols] = bf(mm(tr[r, :], grad[:, :cols]))
-
-    weight_grad(d_q, q, width)
-    red_q.p1()
+        @pl.when(p == pairs - 2)
+        def _():
+            run_0()
+
+        @pl.when(p == pairs - 1)
+        def _():
+            red_0.p2()
+            red_v.p2()
+
+    red_o.p7()
+    for p in range(pairs // 2, pairs - 1):
+        complete(p)
+    weight_grad(d_1, 0, q, half, mid)
+    weight_grad(d_1, mid - half, k, half, mid)
+    red_1.p1()
+    red_0.p3()
+    red_v.p3()
+    weight_grad(d_1, wide, q, mid, end)
+    complete(pairs - 1)
+    weight_grad(d_1, wide + BLOCK, k, mid, end)
+    red_2.p1()
+    gf = local(dv.at[:, pl.ds(half, half)], gfirst, m.l_sem.at[1])
+    red_1.p2()
     for u in range(n_ff + pairs, n_ff + 7):
         reduce_steps(red, u)
-    red_o.p7()
-
-    @pl.loop(0, pairs)
-    def _(p):
-        for t in range(tiles):
-
-            @pl.when((f < last) & (t * tile >= next_start))
-            def _():
-                r, cols = pl.ds(t * tile, tile), pair_cols(p)
-                for j, own in enumerate((dk, dv)):
-                    drain(m.back.at[j, r, cols], m.e_recv.at[j, p, t])
-                    own[r, cols] += f32(m.back[j, r, cols])
-
-    red_q.p2()
+    lx = local(inputs, n1, m.l_sem.at[2])
+    red_2.p2()
+    red_0.p4()
+    red_v.p4()
+    red_o.p8()
 
     @pl.loop(0, tiles)
     def _(t):
         r = rows_at(t * tile, tile)
-        k[r, :] = bf(dk[r, :])
-        v[r, :half] = bf(dv[r, :half])
-
-    gf = local(dv.at[:, pl.ds(half, half)], gfirst, m.l_sem.at[1])
-    d_k, d_v = flat(m.cot), flat(m.g_v)
-    weight_grad(d_k, k.at[pl.ds(0, rows)], width)
-    red_k.p1()
-    d_v[:, half:] = jnp.zeros((width, d_v.shape[1] - half), jnp.bfloat16)
-    weight_grad(d_v, v.at[pl.ds(0, rows)], half)
-    red_v.p1()
-    red_q.p3()
-    red_o.p8()
-
-    @pl.loop(0, tiles)
-    def _(t):
-        r = rows_at(t * tile, tile)
-        g = nt(q[r, :], w_q[...]) + nt(k[r, :], w_k[...]) + nt(v[r, :half], w_v[:, :half])
-        dk[r, :] = g
-
-    red_q.p4()
-    red_k.p2()
-    red_v.p2()
-    lx = local(inputs, n1, m.l_sem.at[2])
+        dk[r, :] = nt(q[r, :], w_q[...]) + nt(k[r, :], w_k[...]) + nt(v[r, :half], w_v[:, :half])
+
+    red_1.p3()
+    red_2.p3()
     lx.wait()
 
     @pl.loop(0, tiles)
@@ -985,9 +1120,10 @@
         m.sums[1:2, :] += jnp.sum(g, axis=0, keepdims=True)
 
     gi = local(m.resid, gin, m.l_sem.at[3])
-    red_q.p5()
-    red_k.p3()
-    red_v.p3()
+    red_0.p5()
+    red_v.p5()
+    red_1.p4()
+    red_2.p4()
 
     def exchange(src, dst, i, dev):
         c = pltpu.make_async_remote_copy(src_ref=src, dst_ref=dst, send_sem=m.v_send.at[i], recv_sem=m.v_recv.at[i], device_id=dev, device_id_type=MESH)
@@ -995,7 +1131,9 @@
         return c
 
     cur = m.sums
-    work = [(red_q.p6, red_k.p4, red_v.p4), (red_q.p7, red_k.p5, red_v.p5), (red_q.p8, red_k.p6, red_v.p6)]
+    work = [
+        (red_0.p6, red_v.p6, red_1.p5, red_2.p5), (red_0.p7, red_v.p7, red_1.p6, red_2.p6), (red_0.p8, red_v.p8, red_1.p7, red_2.p7),
+    ]
     for i, dev in enumerate((pc.core, pc.xn, pc.yn)):
         c = exchange(cur, m.s_pair.at[i], 1 + i, dev)
         for step in work[i]:
@@ -1005,15 +1143,13 @@
         cur = m.s_pair.at[i]
     for o in pc.others:
         exchange(cur, m.s_z.at[f], 4, pc.zdev(o))
-    red_k.p7()
-    red_v.p7()
+    red_1.p8()
+    red_2.p8()
     z3 = m.s_z.at[pl.ds(0, last)]
     drain(z3, m.v_recv.at[4])
     drain(z3, m.v_send.at[4])
     m.s_z[f] = cur[...]
     rs_vec[...] = functools.reduce(lambda a, b: a + b, [m.s_z[j] for j in range(fsdp)])
-    red_k.p8()
-    red_v.p8()
     for g in stat:
         g.finish()
 
@@ -1022,42 +1158,42 @@
         for g in red(c):
             g.finish()
 
-    for t in range(tiles):
-
-        @pl.when((f < last) & (t * tile >= next_start))
-        def _():
-            for c in window(t):
-                c.wait_send()
-
     @pl.loop(0, pairs)
     def _(p):
         for t in range(tiles):
 
-            @pl.when((f > 0) & (t * tile >= span.start))
+            @pl.when((f > 0) & jnp.logical_not(guest) & (t * tile >= span.start))
             def _():
                 for c in early(t, p):
                     c.wait_send()
 
+    @pl.when(guest)
+    def _():
+        for c in lent[1:]:
+            c().wait_send()
+        for p in range(pairs):
+            lent_pair(p).wait_send()
+
     gf.wait()
     gi.wait()
 
 
-def layer_call(fsdp, inputs, first, cot, vec, w_query, w_key, w_value, w_out, w_in, w_down, kseg, qrow):
+def layer_call(fsdp, inputs, first, cot, norms, w_query, w_key, w_value, w_out, w_in, w_down, segs, trees, table):
     rows, width = inputs.shape
     shard = w_query.shape[0]
     n_ff = w_down.shape[0] // BLOCK
     low, full = jnp.bfloat16, jnp.float32
     mq, md = shard // 4, BLOCK // 4
     pairs, blocks = width // (2 * HEAD), rows // BLOCK
-    value = jnp.pad(w_value, ((0, 0), (0, BLOCK)))
+    wide_v = width // 2 + BLOCK
     split = lambda a: a.reshape(2, 2, mq, a.shape[1])
     buf = lambda m, c, lead=(): (*lead, fsdp, 2, 2, m, c)
     chunk = fsdp * BLOCK
     sc = Scratch()
     V, D = pltpu.VMEM, pltpu.SemaphoreType.DMA
     for name, shape in (
-        ("b_q", buf(mq, width)), ("b_k", buf(mq, width)), ("b_v", buf(mq, value.shape[1])), ("b_o", buf(mq, width)),
-        ("b_in", buf(mq, chunk, (n_ff,))), ("b_dn", buf(md, width, (n_ff,))), ("g_v", buf(mq, value.shape[1])),
+        ("b_q", buf(mq, width)), ("b_k", buf(mq, width)), ("b_v", buf(mq, wide_v)), ("b_o", buf(mq, width)),
+        ("b_in", buf(mq, chunk, (n_ff,))), ("b_dn", buf(md, width, (n_ff,))), ("g_v", buf(mq, wide_v)),
         ("mixed", buf(mq, width)), ("cot", buf(mq, width)), ("x", (2 * rows, width)), ("k", (2 * rows, width)), ("v", (2 * rows, width)),
         ("q", (rows, width)), ("n1", (rows, width)), ("n2", (rows, width)), ("tr", (width, rows)), ("gmixed", (rows, width)), ("back", (2, rows, width)),
         ("turned", (2 * HEAD, 2 * rows)),
@@ -1065,7 +1201,7 @@
         sc.add(name, V(shape, low))
     for name, shape in (
         ("vec", (fsdp, 8, width)), ("lnp", (8, width)), ("sums", (8, width)), ("s_pair", (3, 8, width)), ("s_z", (fsdp, 8, width)),
-        ("resid", (rows, width)), ("acc1", (rows, width)), ("acc2", (rows, width)), ("bias", (blocks, TRUNK, BLOCK)),
+        ("resid", (rows, width)), ("acc1", (rows, width)), ("acc2", (rows, width)), ("bias", (blocks + 2, 3 * BLOCK, BLOCK)), ("inner", (pairs, 8, 2 * BLOCK)), ("g_inner", (pairs, 8, 2 * BLOCK)), ("g_lse", (pairs, -(-blocks // 8) * 8, 2 * BLOCK)),
         ("dk_acc", (2 * rows, 2 * HEAD)), ("dv_acc", (2 * rows, 2 * HEAD)), ("lse", (pairs, -(-blocks // 8) * 8, 2 * BLOCK)),
     ):
         sc.add(name, V(shape, full))
@@ -1073,12 +1209,12 @@
         ("l_sem", (9,)), ("lc_sem", (n_ff, fsdp + 1)), ("v_send", (5,)), ("v_recv", (5,)), ("g_send", (4, 5)), ("g_recv", (4, 5)),
         ("w_send", (2, rows // row_tiles(rows))), ("w_recv", (2, rows // row_tiles(rows))),
         ("gi_send", (n_ff, 5)), ("gi_recv", (n_ff, 5)), ("gd_send", (n_ff, 5)), ("gd_recv", (n_ff, 5)),
-        ("ri_send", (n_ff, 8)), ("ri_recv", (n_ff, 8)), ("rd_send", (n_ff, 8)), ("rd_recv", (n_ff, 8)), ("rs_send", (4, 8)), ("rs_recv", (4, 8)),
-        ("e_send", (2, pairs, rows // row_tiles(rows))), ("e_recv", (2, pairs, rows // row_tiles(rows))),
+        ("ri_send", (n_ff, 8)), ("ri_recv", (n_ff, 8)), ("rd_send", (n_ff, 8)), ("rd_recv", (n_ff, 8)), ("rs_send", (5, 8)), ("rs_recv", (5, 8)),
+        ("b_send", (3 + pairs,)), ("b_recv", (3 + pairs,)), ("e_send", (2, pairs, rows // row_tiles(rows))), ("e_recv", (2, pairs, rows // row_tiles(rows))),
     ):
         sc.add(name, D(shape))
     sc.add("ready", pltpu.SemaphoreType.REGULAR)
-    groups = (("r_in", buf(mq, chunk), n_ff), ("r_dn", buf(md, width), n_ff), ("r_o", buf(mq, width), 0), ("r_q", buf(mq, width), 0), ("r_k", buf(mq, width), 0), ("r_v", buf(mq, value.shape[1]), 0))
+    groups = (("r_in", buf(mq, chunk), n_ff), ("r_dn", buf(md, width), n_ff), ("r_o", buf(mq, width), 0), ("r_q", buf(mq, width), 0), ("r_k", buf(mq, width), 0), ("r_v", buf(mq, wide_v), 0))
     for name, shape, lead in groups:
         for i, sub in enumerate(red_shapes(shape)):
             sc.add(f"{name}{i}", V((lead, *sub) if lead else sub, low))
@@ -1087,39 +1223,102 @@
     s = jax.ShapeDtypeStruct
     outs = (
         s((rows, width), low), s((rows, width), full), s((rows, width // 2), full),
-        s((2, 2, mq, width), low), s((2, 2, mq, width), low), s((2, 2, mq, value.shape[1]), low), s((2, 2, mq, width), low),
+        s((2, 2, mq, width), low), s((2, 2, mq, width), low), s((2, 2, mq, wide_v), low), s((2, 2, mq, width), low),
         s((n_ff, 2, 2, mq, chunk), low), s((n_ff, 2, 2, md, width), low), s((8, width), full),
     )
 
     def body(*refs):
         names = Scratch()
         names.names, names.shapes = sc.names, sc.shapes
-        bound = names.bind(refs[12 + n_out :])
+        bound = names.bind(refs[N_IN + n_out :])
         for name, _, _ in groups:
             setattr(bound, name, [getattr(bound, f"{name}{i}") for i in range(4)])
         layer_kernel(fsdp, n_ff, bound, n_out, *refs)
 
     any_ = pl.BlockSpec(memory_space=pl.ANY)
     return pl.pallas_call(
-        body, out_shape=outs, in_specs=[any_] * 11 + [VM], out_specs=[any_] * 3 + [VM] * 7, scratch_shapes=sc.shapes,
+        body, out_shape=outs, in_specs=[any_] * 9 + [VM] * 2 + [SM] * 2, out_specs=[any_] * 3 + [VM] * 7, scratch_shapes=sc.shapes,
         compiler_params=pltpu.CompilerParams(collective_id=3, has_side_effects=True, vmem_limit_bytes=61 << 20),
-    )(inputs, first, cot, vec, split(w_query), split(w_key), split(value), split(w_out), split(w_in), w_down.reshape(n_ff, 2, 2, md, width), kseg, qrow)
+    )(inputs, first, cot, split(w_query), split(w_key), split(w_value), split(w_out), split(w_in), w_down.reshape(n_ff, 2, 2, md, width), norms, segs, trees, table)
+
+
+def finish_kernel(o_in, g_in, f_in, vec, *refs):
+    src, (o_out, g_out, f_out, *dst), rows_out = refs[:6], refs[6:15], refs[15]
+    low, full, passed, sem, load = refs[16:22], refs[22:28], refs[28:31], refs[31], refs[32]
+    copies = []
+
+    def go(src, dst):
+        c = pltpu.make_async_copy(src, dst, sem.at[len(copies)])
+        c.start()
+        copies.append(c)
+
+    loads = [pltpu.make_async_copy(a, b, load.at[i]) for i, (a, b) in enumerate(zip((*src, g_in, o_in, f_in), (*low, *passed)))]
+    for c in loads:
+        c.start()
+    (l_in, l_dn, l_0, l_1, l_o, l_v), (d_in, d_dn, d_q, d_k, d_o, d_v) = low, full
+
+    def done(i, mid):
+        go(mid, dst[i])
+
+    n_ff, width = l_in.shape[0], l_0.shape[1]
+    half = width // 2
+    loads[0].wait()
+    for j in range(n_ff):
+        for g in range(l_in.shape[2] // BLOCK):
+            at = (g * n_ff + j) * BLOCK
+            d_in[:, at:at + BLOCK] = f32(l_in[j, :, g * BLOCK:(g + 1) * BLOCK])
+    done(0, d_in)
+    for c, a, b in zip(loads[6:], passed, (g_out, o_out, f_out)):
+        c.wait()
+        go(a, b)
+    loads[1].wait()
+    for j in range(n_ff):
+        d_dn[j * BLOCK:(j + 1) * BLOCK, :] = f32(l_dn[j])
+    done(1, d_dn)
+    loads[2].wait()
+    loads[3].wait()
+    rest = half - BLOCK
+    for i, mid in ((2, d_q), (3, d_k)):
+        s = i - 2
+        mid[:, :half] = f32(l_0[:, s * half:(s + 1) * half])
+        mid[:, half:half + rest] = f32(l_1[:, s * rest:(s + 1) * rest])
+        mid[:, half + rest:] = f32(l_1[:, 2 * rest + s * BLOCK:2 * rest + (s + 1) * BLOCK])
+        done(i, mid)
+    loads[4].wait()
+    d_o[...] = f32(l_o[...])
+    done(4, d_o)
+    loads[5].wait()
+    d_v[...] = f32(l_v[:, :half])
+    done(5, d_v)
+    rows, width = rows_out.shape[1], vec.shape[1]
+    turned = pltpu.roll(vec[...], lax.rem(width - lax.axis_index("fsdp") * rows, width), 1)
+    rows_out[...] = turned[:, :rows]
+    for c in copies:
+        c.wait()
+
+
+def finish_call(outputs, gin, gfirst, rq, rk, rv, ro, ri, rd, vec):
+    rows, width = rq.shape
+    full = jnp.float32
+    s = jax.ShapeDtypeStruct
+    grads = (ri, rd, rq, rk, ro, rv)
+    shapes = [(rows, ri.shape[0] * ri.shape[2]), (rd.shape[0] * BLOCK, width), (rows, width), (rows, width), (rows, width), (rows, width // 2)]
+    hbm = pl.BlockSpec(memory_space=pltpu.HBM)
+    out = pl.pallas_call(
+        finish_kernel,
+        out_shape=(s(outputs.shape, outputs.dtype), s(gin.shape, full), s(gfirst.shape, full), *(s(a, full) for a in shapes), s((8, rows), full)),
+        in_specs=[hbm] * 3 + [VM] + [hbm] * 6, out_specs=[hbm] * 9 + [VM],
+        scratch_shapes=[*(pltpu.VMEM(a.shape, a.dtype) for a in grads), *(pltpu.VMEM(a, full) for a in shapes), *(pltpu.VMEM(a.shape, a.dtype) for a in (gin, outputs, gfirst)), pltpu.SemaphoreType.DMA((9,)), pltpu.SemaphoreType.DMA((9,))],
+        compiler_params=pltpu.CompilerParams(vmem_limit_bytes=61 << 20),
+    )(outputs, gin, gfirst, vec, *grads)
+    din, ddn, dq, dk, do, dv = out[3:9]
+    return out[0], out[1], out[2], dq, dk, dv, do, din, ddn, out[9]
 
 
 def shifted(block, axis, distance):
     devices = range(lax.axis_size(axis))
     route = [(i - distance, i) for i in devices if i - distance in devices]
     return lax.ppermute(block, axis, route)
-
-
-def path_rows(tree_ids, segment_ids, path_table):
-    seg_count = path_table.shape[1]
-    flat_table = path_table.reshape(-1, 3)
-    lookup = tree_ids * seg_count + segment_ids
-    onehot = (lookup[:, None] == jnp.arange(flat_table.shape[0], dtype=jnp.int32)[None, :]).astype(
-        jnp.int32
-    )
-    return jnp.sum(onehot[:, :, None] * flat_table[None, :, :], axis=1)
 
 
 def reorder_rows(grad_block, fsdp_count, rep_count):
@@ -1140,16 +1339,6 @@
         jnp.concatenate([first[..., h:], second[..., h : h + q]], axis=-1),
         jnp.concatenate([second[..., q:h], second[..., h + q : h + q + q // 2]], axis=-1),
     )
-
-
-def segment_info(tree_ids, segment_ids, path_table, row_start, row_count, reach):
-    seg_win = lax.dynamic_slice_in_dim(jnp.pad(segment_ids, (reach * row_count, 0)), row_start, (reach + 1) * row_count, 0)
-    tree_own = lax.dynamic_slice_in_dim(tree_ids, row_start, row_count, 0)
-    seg_own = seg_win[reach * row_count:]
-    parent = path_rows(tree_own, seg_own, path_table)[:, 1]
-    blocks = row_count // BLOCK
-    rows = jnp.stack([parent.reshape(blocks, BLOCK), seg_own.reshape(blocks, BLOCK)], axis=1)
-    return seg_win[:, None].astype(jnp.float32), jnp.pad(rows, ((0, 0), (0, 6), (0, 0))).astype(jnp.float32)
 
 
 def gathered(fsdp, gain1, shift1, gain2, shift2, w_query, w_key, w_value, w_out, w_in, w_down):
@@ -1181,28 +1370,27 @@
     return lax.psum(sums, both), *unpacked_qkv(first, second), ro, ri, rd
 
 
-def one_kernel(inputs, first_values, cotangent, kseg, qrow, gain1, shift1, gain2, shift2, w_query, w_key, w_value, w_out, w_in, w_down):
+def one_kernel(inputs, first_values, cotangent, segs, trees, table, gain1, shift1, gain2, shift2, w_query, w_key, w_value, w_out, w_in, w_down):
     fsdp = lax.axis_size("fsdp")
     rows, width = w_query.shape
-    vec = jnp.pad(jnp.stack([gain1, shift1, gain2, shift2]).astype(jnp.float32), ((0, 4), (0, width - rows)))
-    vec = jnp.roll(vec, lax.axis_index("fsdp") * rows, axis=1)
-    kseg = jnp.broadcast_to(kseg, (kseg.shape[0], BLOCK))
+    norms = jnp.concatenate([gain1, shift1, gain2, shift2]).reshape(4, rows)
     outputs, input_grad, first_grad, rq, rk, rv, ro, ri, rd, sums = layer_call(
-        fsdp, inputs, first_values, cotangent, vec, w_query, w_key, w_value, w_out, w_in, w_down, kseg, qrow
+        fsdp, inputs, first_values, cotangent, norms, w_query, w_key, w_value, w_out, w_in, w_down, segs, trees, table
     )
     rq, rk, rv, ro, ri, rd = (a.reshape(*a.shape[:-4], -1, a.shape[-1]) for a in (rq, rk, rv, ro, ri, rd))
-    return outputs, input_grad, first_grad, sums, rq, rk, rv[:, : width // 2], ro, ri, rd
-
-
-def several_kernels(reach, inputs, first_values, cotangent, kseg, qrow, gain1, shift1, gain2, shift2, w_query, w_key, w_value, w_out, w_in, w_down):
+    outputs, input_grad, first_grad, rq, rk, rv, ro, ri, rd, sums = finish_call(outputs, input_grad, first_grad, rq, rk, rv, ro, ri, rd, sums)
+    return outputs, input_grad, first_grad, sums[0], sums[1], rq, rk, rv, ro, sums[2], sums[3], ri, rd
+
+
+def several_kernels(reach, inputs, first_values, cotangent, segs, trees, table, gain1, shift1, gain2, shift2, w_query, w_key, w_value, w_out, w_in, w_down):
     row_count, width = inputs.shape
     fsdp = lax.axis_size("fsdp")
     lnp, w1, w2, wo, win, wdn = gathered(fsdp, gain1, shift1, gain2, shift2, w_query, w_key, w_value, w_out, w_in, w_down)
     x = jnp.concatenate([shifted(inputs, "fsdp", d) for d in range(reach, 0, -1)] + [inputs], axis=0)
     fv = jnp.concatenate([shifted(first_values, "fsdp", d) for d in range(reach, 0, -1)] + [first_values], axis=0)
-    n1, q, k, v, mixed, lse, resid, n2 = forward_call(fsdp, reach, x, fv, lnp, w1, w2, wo, kseg, qrow)
+    n1, q, k, v, mixed, lse, resid, n2 = forward_call(fsdp, reach, x, fv, lnp, w1, w2, wo, segs, trees, table)
     outputs, gin, gdn, go, gres, gmixed, sums = mlp_call(n2, cotangent, resid, mixed, lnp, win, wdn, wo)
-    dq, dk, dv, wk, wv = backward_call(fsdp, reach, q, k, v, gmixed, lse, kseg, qrow)
+    dq, dk, dv, wk, wv = backward_call(fsdp, reach, q, k, v, gmixed, lse, segs, trees, table)
     for d in range(1, reach + 1):
         early = slice((reach - d) * row_count, (reach - d + 1) * row_count)
         both = shifted(jnp.concatenate([wk[early], wv[early]], axis=1), "fsdp", -d).astype(jnp.float32)
@@ -1235,13 +1423,11 @@
     for device_pos in range(fsdp):
         offset = device_pos * row_count % TREE_LEN
         reach = max(reach, (offset + row_count - 1) // row_count)
-    row_start = lax.axis_index("fsdp") * row_count
-    kseg, qrow = segment_info(tree_ids, segment_ids, path_table, row_start, row_count, reach)
+    marks = (segment_ids.reshape(-1, BLOCK), tree_ids, path_table)
     weights = (attn_gain, attn_shift, mlp_gain, mlp_shift, w_query, w_key, w_value, w_out, w_in, w_down)
     if lax.axis_size("rep") == 8 and reach == 1 and row_count == width:
-        results = one_kernel(inputs, first_values, cotangent, kseg, qrow, *weights)
-    else:
-        results = several_kernels(reach, inputs, first_values, cotangent, kseg, qrow, *weights)
+        return one_kernel(inputs, first_values, cotangent, *marks, *weights)
+    results = several_kernels(reach, inputs, first_values, cotangent, *marks, *weights)
     outputs, input_grad, first_grad, sums, d_q, d_k, d_v, d_o, d_in, d_dn = results
     rows = w_query.shape[0]
     sums = lax.dynamic_slice_in_dim(sums, lax.axis_index("fsdp") * rows, rows, 1)

time: 292 us -> 244 us (0.84)
  Pallas kernels: 260 us -> 239 us
  local copies, waits for them, and re-layouts: 19.5 us -> 3.48 us
  other arithmetic: 10.7 us -> 0.78 us
    pallas_call x1 -> x2, Pallas kernels: 260 us -> 239 us  [the longest x1 230 us: layer_call(): pl.pallas_call(body, out_shape=outs, in_specs=[any_] * 9 + [VM] * 2 + [SM...]
    convert_element_type x7 -> x0, other arithmetic: 9.03 us -> none  [the longest x4 7.62 us: on_device(): a.astype(jnp.float32)]
    convert_element_type x3 -> x0, local copies, waits for them, and re-layouts: 6.54 us -> none  [on_device(): a.astype(jnp.float32)]
    unnamed x16 -> x1, local copies, waits for them, and re-layouts: 5.91 us -> 1.39 us
where the time goes in v3:
time: 244 us
  Pallas kernels  239 us (98%)
  local copies, waits for them, and re-layouts  3.48 us (1%)
    pallas_call x1, Pallas kernels, layer_call(): pl.pallas_call(body, out_shape=outs, in_specs=[any_] * 9 + [VM] * 2 + [SM...  230 us
    pallas_call x1, Pallas kernels, finish_call(): pl.pallas_call(finish_kernel, out_shape=(s(outputs.shape, outputs.dtype),...  8.24 us

profile of v3, /device:TPU:0, one launch (start us, length us, event | category | flops | bytes accessed | tf_op | source)
XLA Modules:
  0.0 243.6 jit_solution(11301632839170332577)
XLA Ops:
  0.6 0.8 pad_maximum_fusion
  1.4 0.7 reshape.74.refs_9_
  2.1 1.4 copy.29.refs_12_
  3.5 230.5 %shard_map.255 = (bf16[768,768]{1,0:T(8,128)(2,1)}, f32[768,768]{1,0:T(8,128)}, f32[768,384]{1,0:T(8,128)}, bf16[2,2,48,768]{3,2,1,0:T(8,128)(2,1)}, bf16[2,2,48...) custom-call(bf16[768,768]{1,0:T(8,128)(2,1)} %refs_0_.1, ...), custom_call_target="tpu_custom_call" | custom-call | tf_op jit(solution)/shard_map/pallas_call | solution.py:1239
  234.0 8.2 %shard_map.256 = (bf16[768,768]{1,0:T(8,128)(2,1)}, f32[768,768]{1,0:T(8,128)}, f32[768,384]{1,0:T(8,128)}, f32[192,3072]{1,0:T(8,128)}, f32[768,768]{1,0:T(8,12...) custom-call(bf16[768,768]{1,0:T(8,128)(2,1)} %get-tuple-element.33.o, ...), custom_call_target="tpu_custom_call" | custom-call | tf_op jit(solution)/shard_map/pallas_call | solution.py:1307
  242.2 1.4 fusion

commit v4 on v3

--- a/solution.py
+++ b/solution.py
@@ -298,9 +298,11 @@
 
 
 def transpose_pair(src, p, start, stop, dst):
-    @pl.loop(start // BLOCK, stop // BLOCK)
+    step = row_tiles(src.shape[0])
+
+    @pl.loop(start // step, stop // step)
     def _(j):
-        dst[:, pl.ds(pl.multiple_of(j * BLOCK, BLOCK), BLOCK)] = src[rows_at(j * BLOCK, BLOCK), pair_cols(p)].T
+        dst[:, pl.ds(pl.multiple_of(j * step, step), step)] = src[rows_at(j * step, step), pair_cols(p)].T
 
 
 def attend_pair(span, p, lo, hi, start, stop, q, k, v, bias, v_t, mixed, lse):
@@ -319,9 +321,8 @@
             top = functools.reduce(jnp.maximum, [jnp.max(s, axis=0, keepdims=True) for s in scores])
             expo = [jnp.exp(s - top) for s in scores]
             total = sum(jnp.sum(e, axis=0, keepdims=True) for e in expo)
-            inv = 1.0 / total
-            out = sum(mm(v_t[:, r], bf(e * inv)) for r, e in zip(rows, expo))
-            mixed[own, cols] = bf(unstacked_t(out))
+            out = sum(mm(v_t[:, r], bf(e)) for r, e in zip(rows, expo))
+            mixed[own, cols] = bf(unstacked_t(out * (1.0 / total)))
             lse[p, pl.ds(i, 1), :] = top + jnp.log(total)
 
         by_kind(b, body)
@@ -525,7 +526,7 @@
     )(n2, cot, resid, mixed, lnp, win, wdn, wo)
 
 
-def attend_back_pair(span, p, q, k, v, gmixed, bias, lse, k_t, dk_acc, dv_acc, dq, lent=None):
+def attend_back_pair(span, p, q, k, v, gmixed, bias, lse, inner, k_t, dk_acc, dv_acc, dq, lent=None):
     transpose_pair(k, p, span.start, span.window + span.rows, k_t)
     cols = pair_cols(p)
 
@@ -540,14 +541,12 @@
         b = span.kind(i)
         own = rows_at(i * BLOCK, BLOCK)
         q2, g2 = stacked(q[own, cols]), stacked(gmixed[own, cols])
-        l = lse[p, pl.ds(i, 1), :]
+        l, mean = lse[p, pl.ds(i, 1), :], inner[p, pl.ds(i, 1), :]
 
         def body(parts, only_own=False):
             rows = [part_rows(span, i, b, part) for part in parts]
             probs = [jnp.exp(part_scores(q2, k[r, cols], bias, i, part) - l) for r, part in zip(rows, parts)]
-            gw = [nt(v[r, cols], g2) for r in rows]
-            inner = sum(jnp.sum(a * g, axis=0, keepdims=True) for a, g in zip(probs, gw))
-            gs = [bf(a * (g - inner)) for a, g in zip(probs, gw)]
+            gs = [bf(a * (nt(v[r, cols], g2) - mean)) for a, r in zip(probs, rows)]
             out = sum(mm(k_t[:, r], g) for r, g in zip(rows, gs))
             dq[own, cols] = bf(unstacked_t(out) * HEAD ** (-0.5))
             for r, a, g, part in zip(rows, probs, gs, parts):
@@ -559,11 +558,21 @@
         by_kind(b, body, None if lent is None else lent & (i < span.tree - 6))
 
 
-def lent_sums(gmixed, mixed):
-    heads = lax.broadcasted_iota(jnp.int32, (16, mixed.shape[1]), 0)
-    cols = lax.broadcasted_iota(jnp.int32, (16, mixed.shape[1]), 1)
-    pick = ((cols >= heads * HEAD) & (cols < heads * HEAD + HEAD)).astype(jnp.float32)
-    return lax.dot_general(pick, f32(gmixed) * f32(mixed), (((1,), (1,)), ((), ())), precision=lax.Precision.HIGHEST, preferred_element_type=jnp.float32)
+def head_sums(gmixed, mixed, inner):
+    width = mixed.shape[1]
+    heads = lax.broadcasted_iota(jnp.int32, (16, width), 0)
+    cols = lax.broadcasted_iota(jnp.int32, (16, width), 1)
+    pick = bf(((cols >= heads * HEAD) & (cols < heads * HEAD + HEAD)).astype(jnp.float32))
+    tile = row_tiles(mixed.shape[0])
+    for t in range(mixed.shape[0] // tile):
+        r = slice(t * tile, (t + 1) * tile)
+        each = f32(gmixed[r, :]) * f32(mixed[r, :])
+        high = bf(each)
+        sums = nt(pick, high) + nt(pick, bf(each - f32(high)))
+        for j in range(tile // BLOCK):
+            at, i = slice(j * BLOCK, (j + 1) * BLOCK), t * (tile // BLOCK) + j
+            for p in range(width // (2 * HEAD)):
+                inner[p, i:i + 1, :] = jnp.concatenate([sums[2 * p:2 * p + 1, at], sums[2 * p + 1:2 * p + 2, at]], axis=1)
 
 
 def borrowed_back(span, p, q, g, k, v, bias, lse, inner, dk, dv):
@@ -584,16 +593,17 @@
             dv[own, cols] += mm(bf(probs), g2)
 
 
-def backward_kernel(fsdp, reach, q, k, v, gmixed, lse, segs, trees, table, dq, dk, dv, wk, wv, bias, k_t, dk_acc, dv_acc):
+def backward_kernel(fsdp, reach, q, k, v, gmixed, mixed, lse, segs, trees, table, dq, dk, dv, wk, wv, bias, inner, k_t, dk_acc, dv_acc):
     span = Span(fsdp, q.shape[0], reach, lax.axis_index("fsdp"))
     make_bias(span, segs, trees, table, bias)
+    head_sums(gmixed, mixed, inner)
     wk[...] = jnp.zeros_like(wk)
     wv[...] = jnp.zeros_like(wv)
 
     @pl.loop(0, q.shape[1] // (2 * HEAD))
     def _(p):
         cols = pair_cols(p)
-        attend_back_pair(span, p, q, k, v, gmixed, bias, lse, k_t, dk_acc, dv_acc, dq)
+        attend_back_pair(span, p, q, k, v, gmixed, bias, lse, inner, k_t, dk_acc, dv_acc, dq)
         dk[:, cols] = dk_acc[span.window:, :]
         dv[:, cols] = dv_acc[span.window:, :]
 
@@ -604,20 +614,20 @@
             wv[r, cols] = bf(dv_acc[r, :])
 
 
-def backward_call(fsdp, reach, q, k, v, gmixed, lse, segs, trees, table):
+def backward_call(fsdp, reach, q, k, v, gmixed, mixed, lse, segs, trees, table):
     window, width = k.shape
     rows = q.shape[0]
     s, low, full = jax.ShapeDtypeStruct, jnp.bfloat16, jnp.float32
     early = window - rows
     outs = (s((rows, width), low), s((rows, width), full), s((rows, width), full), s((early, width), low), s((early, width), low))
     return pl.pallas_call(
-        functools.partial(backward_kernel, fsdp, reach), out_shape=outs, in_specs=[VM] * 6 + [SM] * 2, out_specs=[VM] * 5,
+        functools.partial(backward_kernel, fsdp, reach), out_shape=outs, in_specs=[VM] * 7 + [SM] * 2, out_specs=[VM] * 5,
         scratch_shapes=[
-            pltpu.VMEM((rows // BLOCK, 3 * BLOCK, BLOCK), full), pltpu.VMEM((2 * HEAD, window), low),
+            pltpu.VMEM((rows // BLOCK, 3 * BLOCK, BLOCK), full), pltpu.VMEM(lse.shape, full), pltpu.VMEM((2 * HEAD, window), low),
             pltpu.VMEM((window, 2 * HEAD), full), pltpu.VMEM((window, 2 * HEAD), full),
         ],
         compiler_params=pltpu.CompilerParams(vmem_limit_bytes=58 << 20),
-    )(q, k, v, gmixed, lse, segs, trees, table)
+    )(q, k, v, gmixed, mixed, lse, segs, trees, table)
 
 
 def projection_back(span, x, n1, dq, dk, dv, lnp, w1, w2, gres, gin, gfirst, g1, g2, sums, n1_t, cat1, cat2):
@@ -671,7 +681,7 @@
 
 
 def gather_steps(items, u):
-    for s, stage in enumerate(Gather.STAGES):
+    for s, stage in enumerate(Gather.STAGES[:3]):
         c = u - s
 
         @pl.when((c >= 0) & (c < items.count))
@@ -680,9 +690,12 @@
                 stage(g)
 
 
+REDUCE_AT = (0, 1, 2, 3, 5, 6, 7)
+
+
 def reduce_steps(items, u):
-    for s, stage in enumerate(Reduce.STAGES):
-        c = u - s
+    for s, stage in enumerate(Reduce.STAGES[:7]):
+        c = u - REDUCE_AT[s]
 
         @pl.when((c >= 0) & (c < items.count))
         def _():
@@ -849,12 +862,6 @@
     @pl.loop(0, pairs)
     def _(p):
         attend_pair(span, p, here, span.blocks, border, 2 * rows, q, k, v, m.bias, m.turned, mixed, m.lse)
-        for when, step in ((0, lambda: (gat[3].z_wait(), gat[3].a_start())), (2, lambda: (gat[3].a_wait(), gat[3].b_start())), (4, lambda: (gat[3].b_wait(), gat[3].c_start()))):
-
-            @pl.when(p == when)
-            def _():
-                step()
-
         @pl.when(p >= pairs // 2)
         def _():
             for j in range(2):
@@ -882,9 +889,13 @@
     def _(p):
         attend_pair(span, p, 0, here, span.start, border, q, k, v, m.bias, m.turned, mixed, m.lse)
 
-        @pl.when(p >= pairs // 2)
-        def _():
-            gather_steps(ff, p - pairs // 2)
+        for s, stage in enumerate(Gather.STAGES[:3]):
+
+            @pl.when(p == s)
+            def _():
+                stage(gat[3])
+
+        gather_steps(ff, p - 2)
 
     @pl.when(guest)
     def _():
@@ -911,7 +922,10 @@
 
     @pl.loop(0, n_ff)
     def _(c):
-        gather_steps(ff, c + 3)
+        gather_steps(ff, c + pairs - 2)
+        for g in ff(c):
+            Gather.STAGES[3](g)
+
         b_in, b_dn = flat(m.b_in.at[c]), flat(m.b_dn.at[c])
 
         def put_in(val):
@@ -932,14 +946,10 @@
     m.sums[...] = jnp.zeros_like(m.sums)
     second_norm_back(rows, m.lnp, m.resid, cot, m.acc2, m.resid, n2, m.sums)
     branch_back(rows, n2, w_o, m.gmixed)
+    head_sums(m.gmixed, mixed, m.inner)
 
     @pl.when(guest)
     def _():
-        sums = lent_sums(m.gmixed[two, :], mixed[two, :])
-        for p in range(pairs):
-            for j in range(2):
-                at = slice(j * BLOCK, (j + 1) * BLOCK)
-                m.inner[p, j:j + 1, :] = jnp.concatenate([sums[2 * p:2 * p + 1, at], sums[2 * p + 1:2 * p + 2, at]], axis=1)
         lent[2]().start()
         for p in range(pairs):
             lent_pair(p).start()
@@ -1034,7 +1044,7 @@
     @pl.loop(0, pairs)
     def _(p):
         cols = pair_cols(p)
-        attend_back_pair(span, p, q, k, v, m.gmixed, m.bias, m.lse, m.turned, m.dk_acc, m.dv_acc, q, guest)
+        attend_back_pair(span, p, q, k, v, m.gmixed, m.bias, m.lse, m.inner, m.turned, m.dk_acc, m.dv_acc, q, guest)
         dk[:, cols] = m.dk_acc[rows:, :]
         dv[:, cols] = m.dv_acc[rows:, :]
 
@@ -1064,9 +1074,9 @@
             lent_pair(p).wait_recv()
             borrowed_back(span, p, gq, gg, k, v, m.bias, m.g_lse, m.g_inner, dk, dv)
 
-        for s in range(6):
-
-            @pl.when(p == s)
+        for s in range(5):
+
+            @pl.when(p == REDUCE_AT[s])
             def _():
                 Reduce.STAGES[s](red_o)
 
@@ -1079,35 +1089,34 @@
             red_0.p2()
             red_v.p2()
 
-    red_o.p7()
     for p in range(pairs // 2, pairs - 1):
         complete(p)
     weight_grad(d_1, 0, q, half, mid)
     weight_grad(d_1, mid - half, k, half, mid)
     red_1.p1()
+    weight_grad(d_1, wide, q, mid, end)
     red_0.p3()
     red_v.p3()
-    weight_grad(d_1, wide, q, mid, end)
+    red_o.p6()
     complete(pairs - 1)
     weight_grad(d_1, wide + BLOCK, k, mid, end)
     red_2.p1()
     gf = local(dv.at[:, pl.ds(half, half)], gfirst, m.l_sem.at[1])
+    lx = local(inputs, n1, m.l_sem.at[2])
     red_1.p2()
-    for u in range(n_ff + pairs, n_ff + 7):
-        reduce_steps(red, u)
-    lx = local(inputs, n1, m.l_sem.at[2])
     red_2.p2()
     red_0.p4()
     red_v.p4()
-    red_o.p8()
 
     @pl.loop(0, tiles)
     def _(t):
         r = rows_at(t * tile, tile)
         dk[r, :] = nt(q[r, :], w_q[...]) + nt(k[r, :], w_k[...]) + nt(v[r, :half], w_v[:, :half])
 
+    red_2.p3()
     red_1.p3()
-    red_2.p3()
+    reduce_steps(red, n_ff + pairs)
+    red_o.p7()
     lx.wait()
 
     @pl.loop(0, tiles)
@@ -1120,10 +1129,6 @@
         m.sums[1:2, :] += jnp.sum(g, axis=0, keepdims=True)
 
     gi = local(m.resid, gin, m.l_sem.at[3])
-    red_0.p5()
-    red_v.p5()
-    red_1.p4()
-    red_2.p4()
 
     def exchange(src, dst, i, dev):
         c = pltpu.make_async_remote_copy(src_ref=src, dst_ref=dst, send_sem=m.v_send.at[i], recv_sem=m.v_recv.at[i], device_id=dev, device_id_type=MESH)
@@ -1132,7 +1137,7 @@
 
     cur = m.sums
     work = [
-        (red_0.p6, red_v.p6, red_1.p5, red_2.p5), (red_0.p7, red_v.p7, red_1.p6, red_2.p6), (red_0.p8, red_v.p8, red_1.p7, red_2.p7),
+        (red_2.p4, red_1.p4, red_0.p5, red_v.p5), (red_0.p6, red_v.p6), (red_2.p5, red_1.p5, red_0.p7, red_v.p7),
     ]
     for i, dev in enumerate((pc.core, pc.xn, pc.yn)):
         c = exchange(cur, m.s_pair.at[i], 1 + i, dev)
@@ -1143,19 +1148,25 @@
         cur = m.s_pair.at[i]
     for o in pc.others:
         exchange(cur, m.s_z.at[f], 4, pc.zdev(o))
-    red_1.p8()
-    red_2.p8()
+    red_2.p6()
+    red_1.p6()
+    for u in range(n_ff + pairs + 1, n_ff + REDUCE_AT[-1]):
+        reduce_steps(red, u)
+    red_2.p7()
+    red_1.p7()
     z3 = m.s_z.at[pl.ds(0, last)]
     drain(z3, m.v_recv.at[4])
     drain(z3, m.v_send.at[4])
     m.s_z[f] = cur[...]
     rs_vec[...] = functools.reduce(lambda a, b: a + b, [m.s_z[j] for j in range(fsdp)])
     for g in stat:
+        g.p8()
         g.finish()
 
     @pl.loop(0, n_ff)
     def _(c):
         for g in red(c):
+            g.p8()
             g.finish()
 
     @pl.loop(0, pairs)
@@ -1238,7 +1249,7 @@
     any_ = pl.BlockSpec(memory_space=pl.ANY)
     return pl.pallas_call(
         body, out_shape=outs, in_specs=[any_] * 9 + [VM] * 2 + [SM] * 2, out_specs=[any_] * 3 + [VM] * 7, scratch_shapes=sc.shapes,
-        compiler_params=pltpu.CompilerParams(collective_id=3, has_side_effects=True, vmem_limit_bytes=61 << 20),
+        compiler_params=pltpu.CompilerParams(collective_id=3, has_side_effects=True, vmem_limit_bytes=63 << 20),
     )(inputs, first, cot, split(w_query), split(w_key), split(w_value), split(w_out), split(w_in), w_down.reshape(n_ff, 2, 2, md, width), norms, segs, trees, table)
 
 
@@ -1253,7 +1264,7 @@
         copies.append(c)
 
     loads = [pltpu.make_async_copy(a, b, load.at[i]) for i, (a, b) in enumerate(zip((*src, g_in, o_in, f_in), (*low, *passed)))]
-    for c in loads:
+    for c in loads[6:] + loads[:6]:
         c.start()
     (l_in, l_dn, l_0, l_1, l_o, l_v), (d_in, d_dn, d_q, d_k, d_o, d_v) = low, full
 
@@ -1262,15 +1273,15 @@
 
     n_ff, width = l_in.shape[0], l_0.shape[1]
     half = width // 2
+    for c, a, b in zip(loads[6:], passed, (g_out, o_out, f_out)):
+        c.wait()
+        go(a, b)
     loads[0].wait()
     for j in range(n_ff):
         for g in range(l_in.shape[2] // BLOCK):
             at = (g * n_ff + j) * BLOCK
             d_in[:, at:at + BLOCK] = f32(l_in[j, :, g * BLOCK:(g + 1) * BLOCK])
     done(0, d_in)
-    for c, a, b in zip(loads[6:], passed, (g_out, o_out, f_out)):
-        c.wait()
-        go(a, b)
     loads[1].wait()
     for j in range(n_ff):
         d_dn[j * BLOCK:(j + 1) * BLOCK, :] = f32(l_dn[j])
@@ -1390,7 +1401,7 @@
     fv = jnp.concatenate([shifted(first_values, "fsdp", d) for d in range(reach, 0, -1)] + [first_values], axis=0)
     n1, q, k, v, mixed, lse, resid, n2 = forward_call(fsdp, reach, x, fv, lnp, w1, w2, wo, segs, trees, table)
     outputs, gin, gdn, go, gres, gmixed, sums = mlp_call(n2, cotangent, resid, mixed, lnp, win, wdn, wo)
-    dq, dk, dv, wk, wv = backward_call(fsdp, reach, q, k, v, gmixed, lse, segs, trees, table)
+    dq, dk, dv, wk, wv = backward_call(fsdp, reach, q, k, v, gmixed, mixed, lse, segs, trees, table)
     for d in range(1, reach + 1):
         early = slice((reach - d) * row_count, (reach - d + 1) * row_count)
         both = shifted(jnp.concatenate([wk[early], wv[early]], axis=1), "fsdp", -d).astype(jnp.float32)

time: 244 us -> 231 us (0.947)
  Pallas kernels: 239 us -> 226 us
    pallas_call x1, Pallas kernels: 230 us -> 218 us  [layer_call(): pl.pallas_call(body, out_shape=outs, in_specs=[any_] * 9 + [VM] * 2 + [SM...]
where the time goes in v4:
time: 231 us
  Pallas kernels  226 us (98%)
  local copies, waits for them, and re-layouts  3.48 us (2%)
    pallas_call x1, Pallas kernels, layer_call(): pl.pallas_call(body, out_shape=outs, in_specs=[any_] * 9 + [VM] * 2 + [SM...  218 us
    pallas_call x1, Pallas kernels, finish_call(): pl.pallas_call(finish_kernel, out_shape=(s(outputs.shape, outputs.dtype),...  7.68 us

profile of v4, /device:TPU:0, one launch (start us, length us, event | category | flops | bytes accessed | tf_op | source)
XLA Modules:
  0.0 231.0 jit_solution(3480164320615338867)
XLA Ops:
  0.6 0.8 pad_maximum_fusion
  1.4 0.7 reshape.74.refs_9_
  2.1 1.4 copy.29.refs_12_
  3.5 218.4 %shard_map.255 = (bf16[768,768]{1,0:T(8,128)(2,1)}, f32[768,768]{1,0:T(8,128)}, f32[768,384]{1,0:T(8,128)}, bf16[2,2,48,768]{3,2,1,0:T(8,128)(2,1)}, bf16[2,2,48...) custom-call(bf16[768,768]{1,0:T(8,128)(2,1)} %refs_0_.1, ...), custom_call_target="tpu_custom_call" | custom-call | tf_op jit(solution)/shard_map/pallas_call | solution.py:1250
  221.9 7.7 %shard_map.256 = (bf16[768,768]{1,0:T(8,128)(2,1)}, f32[768,768]{1,0:T(8,128)}, f32[768,384]{1,0:T(8,128)}, f32[192,3072]{1,0:T(8,128)}, f32[768,768]{1,0:T(8,12...) custom-call(bf16[768,768]{1,0:T(8,128)(2,1)} %get-tuple-element.33.o, ...), custom_call_target="tpu_custom_call" | custom-call | tf_op jit(solution)/shard_map/pallas_call | solution.py:1318
  229.6 1.4 fusion

commit v5 on v4

--- a/solution.py
+++ b/solution.py
@@ -22,11 +22,12 @@
         self.xn = (rid(self.y, 1 - self.x, self.k), self.f)
         self.yn = (rid(1 - self.y, self.x, self.k), self.f)
         self.r = r
+        self.diagonal = (rid(1 - self.y, 1 - self.x, self.k), self.f)
         self.others = [lax.rem(self.f + j, fsdp) for j in range(1, fsdp)]
     def zdev(self, fo): return (self.r, fo)
     def barrier(self):
         bar = pltpu.get_barrier_semaphore()
-        devs = [self.core, self.xn, self.yn] + [self.zdev(o) for o in self.others]
+        devs = [self.core, self.xn, self.yn, self.diagonal] + [self.zdev(o) for o in self.others]
         for d in devs:
             pl.semaphore_signal(bar, inc=1, device_id=d, device_id_type=MESH)
         pl.semaphore_wait(bar, len(devs))
@@ -35,8 +36,8 @@
     pltpu.make_async_copy(view, view, sem).wait()
 
 class Gather:
-    def __init__(self, pc, buf, send, recv, xfirst):
-        self.pc, self.buf, self.s, self.r, self.xf = pc, buf, send, recv, xfirst
+    def __init__(self, pc, buf, send, recv, xfirst, direct=False):
+        self.pc, self.buf, self.s, self.r, self.xf, self.direct = pc, buf, send, recv, xfirst, direct
         self.H = buf.shape[-1] // 2
         self.cols = pl.ds(pl.multiple_of(pc.k * self.H, 128), self.H)
     def push(self, view, stage, dev):
@@ -52,10 +53,12 @@
         for o in pc.others:
             v = self.buf.at[o, pc.y, pc.x, :, self.cols]
             self.push(v, 1, pc.xn); self.push(v, 2, pc.yn)
+            if self.direct: self.push(v, 3, pc.diagonal)
     def a_wait(self):
         drain(self.three(), self.r.at[1]); drain(self.three(), self.r.at[2])
     def b_start(self):
         pc = self.pc
+        if self.direct: return
         for o in pc.others:
             if self.xf: self.push(self.buf.at[o, 1 - pc.y, pc.x, :, self.cols], 3, pc.xn)
             else: self.push(self.buf.at[o, pc.y, 1 - pc.x, :, self.cols], 3, pc.yn)
@@ -65,8 +68,8 @@
         for o in pc.others: self.push(self.buf.at[o, :, :, :, self.cols], 4, pc.core)
     def big(self): return self.buf.at[pl.ds(0, self.pc.fsdp - 1), :, :, :, self.cols]
     def c_wait(self): drain(self.big(), self.r.at[4])
-    def finish(self):
-        for st in range(4): drain(self.three(), self.s.at[st])
+    def finish(self, first=0):
+        for st in range(first, 4): drain(self.three(), self.s.at[st])
         drain(self.big(), self.s.at[4])
 
 Gather.STAGES = [
@@ -233,8 +236,9 @@
         def _():
             tree = trees[first * BLOCK]
             parent = jnp.zeros_like(own)
+            rows = table[tree]
             for leaf in range(table.shape[1]):
-                parent = jnp.where(own == leaf, table[tree, leaf, 1], parent)
+                parent = jnp.where(own == leaf, rows[leaf:leaf + 1, 1:2], parent)
             put(0, 4, parent)
             put(BLOCK, 5, parent)
 
@@ -246,26 +250,30 @@
         def _():
             body([(0, n * BLOCK, None)][: n] + [(None, BLOCK, 256)])
 
-    @pl.when((b >= 4) & (b < 6))
-    def _():
-        body([(0, 512, None), (None, BLOCK, 256)])
-
+    branch_parts = [(0, 512, None), (None, BLOCK, 256)]
     leaf_parts = [(0, 512, None), (512, 256, 0), (None, BLOCK, 256)]
     if lent is None:
 
+        @pl.when((b >= 4) & (b < 6))
+        def _():
+            body(branch_parts)
+
         @pl.when(b >= 6)
         def _():
             body(leaf_parts)
 
     else:
-
-        @pl.when((b >= 6) & jnp.logical_not(lent))
-        def _():
-            body(leaf_parts)
-
-        @pl.when((b >= 6) & lent)
-        def _():
-            body(leaf_parts, only_own=True)
+        for upto in (0, 512, 768):
+
+            if upto < 768:
+
+                @pl.when((b >= 4) & (b < 6) & (lent == upto))
+                def _():
+                    body(branch_parts, upto)
+
+            @pl.when((b >= 6) & (lent == upto))
+            def _():
+                body(leaf_parts, upto)
 
 
 def stacked(pair):
@@ -305,25 +313,33 @@
         dst[:, pl.ds(pl.multiple_of(j * step, step), step)] = src[rows_at(j * step, step), pair_cols(p)].T
 
 
-def attend_pair(span, p, lo, hi, start, stop, q, k, v, bias, v_t, mixed, lse):
-    transpose_pair(v, p, start, stop, v_t)
-    cols = pair_cols(p)
-
+def group_cols(p, j, n):
+    return pl.ds(pl.multiple_of((p * n + j) * 2 * HEAD, 2 * HEAD), 2 * HEAD)
+
+
+GROUP = 2
+
+
+def attend_group(span, p, lo, hi, q, k, v, bias, mixed, lse):
     @pl.loop(lo, hi)
     def _(i):
         b = span.kind(i)
         own = rows_at(i * BLOCK, BLOCK)
-        q2 = stacked(q[own, cols])
 
         def body(parts):
             rows = [part_rows(span, i, b, part) for part in parts]
-            scores = [part_scores(q2, k[r, cols], bias, i, part) for r, part in zip(rows, parts)]
-            top = functools.reduce(jnp.maximum, [jnp.max(s, axis=0, keepdims=True) for s in scores])
-            expo = [jnp.exp(s - top) for s in scores]
-            total = sum(jnp.sum(e, axis=0, keepdims=True) for e in expo)
-            out = sum(mm(v_t[:, r], bf(e)) for r, e in zip(rows, expo))
-            mixed[own, cols] = bf(unstacked_t(out * (1.0 / total)))
-            lse[p, pl.ds(i, 1), :] = top + jnp.log(total)
+            state = []
+            for j in range(GROUP):
+                cols = group_cols(p, j, GROUP)
+                q2 = stacked(q[own, cols])
+                state.append((j, cols, [part_scores(q2, k[r, cols], bias, i, part) for r, part in zip(rows, parts)]))
+            for j, cols, scores in state:
+                top = functools.reduce(jnp.maximum, [jnp.max(s, axis=0, keepdims=True) for s in scores])
+                expo = [jnp.exp(s - top) for s in scores]
+                total = sum(jnp.sum(e, axis=0, keepdims=True) for e in expo)
+                out = sum(tn(v[r, cols], bf(e)) for r, e in zip(rows, expo))
+                mixed[own, cols] = bf(unstacked_t(out * (1.0 / total)))
+                lse[p * GROUP + j, pl.ds(i, 1), :] = top + jnp.log(total)
 
         by_kind(b, body)
 
@@ -381,15 +397,15 @@
         n2[rows, :] = bf(hat * gain + shift)
 
 
-def forward_kernel(fsdp, reach, x, fv, lnp, w1, w2, wo, segs, trees, table, n1, q, k, v, mixed, lse, resid, n2, bias, v_t):
+def forward_kernel(fsdp, reach, x, fv, lnp, w1, w2, wo, segs, trees, table, n1, q, k, v, mixed, lse, resid, n2, bias):
     span = Span(fsdp, q.shape[0], reach, lax.axis_index("fsdp"))
     rows = q.shape[0]
     make_bias(span, segs, trees, table, bias)
     project(span, x, fv, lnp, w1, w2, n1, q, k, v)
 
-    @pl.loop(0, q.shape[1] // (2 * HEAD))
+    @pl.loop(0, q.shape[1] // (2 * HEAD) // GROUP)
     def _(p):
-        attend_pair(span, p, 0, span.blocks, span.start, span.window + rows, q, k, v, bias, v_t, mixed, lse)
+        attend_group(span, p, 0, span.blocks, q, k, v, bias, mixed, lse)
 
     branch_out(span, x, lnp, mixed, wo, resid, n2)
 
@@ -410,8 +426,8 @@
     )
     return pl.pallas_call(
         functools.partial(forward_kernel, fsdp, reach),
-        out_shape=outs, in_specs=[VM] * 7 + [SM] * 2, out_specs=[VM] * 8,
-        scratch_shapes=[pltpu.VMEM((blocks, 3 * BLOCK, BLOCK), full), pltpu.VMEM((2 * HEAD, window), low)],
+        out_shape=outs, in_specs=[VM] * 7 + [SM, VM], out_specs=[VM] * 8,
+        scratch_shapes=[pltpu.VMEM((blocks, 3 * BLOCK, BLOCK), full)],
         compiler_params=pltpu.CompilerParams(vmem_limit_bytes=50 << 20),
     )(x, fv, lnp, w1, w2, wo, segs, trees, table)
 
@@ -438,8 +454,8 @@
             dst[c * BLOCK:(c + 1) * BLOCK, rows] = src[rows, c * BLOCK:(c + 1) * BLOCK].T
 
 
-def mlp_chunk(rows, n2, n2_t, cot, win, wdn, out_acc, gn2_acc, hid, gact, gin, gdn):
-    tile = row_tiles(rows)
+def mlp_chunk(rows, n2, n2_t, cot, win, wdn, out_acc, gn2_acc, hid, gact, gin, gdn, between=lambda: None):
+    tile = 384 if rows % 384 == 0 else row_tiles(rows)
 
     @pl.loop(0, rows // tile)
     def _(t):
@@ -452,6 +468,7 @@
         gact[r, :] = g
         gn2_acc[r, :] += nt(g, win())
 
+    between()
     gdn(bf(tn(hid[...], cot[...])))
     gin(bf(mm(n2_t[...], gact[...])))
 
@@ -526,36 +543,41 @@
     )(n2, cot, resid, mixed, lnp, win, wdn, wo)
 
 
-def attend_back_pair(span, p, q, k, v, gmixed, bias, lse, inner, k_t, dk_acc, dv_acc, dq, lent=None):
-    transpose_pair(k, p, span.start, span.window + span.rows, k_t)
-    cols = pair_cols(p)
-
+def attend_back_group(span, p, lo, hi, q, k, v, gmixed, bias, lse, inner, dk_acc, dv_acc, dq, lent=None):
+    @pl.loop(lo, hi)
+    def _(i):
+        b = span.kind(i)
+        own = rows_at(i * BLOCK, BLOCK)
+
+        def body(parts, upto=0):
+            rows = [part_rows(span, i, b, part) for part in parts]
+            state = []
+            for j in range(GROUP):
+                cols = group_cols(p, j, GROUP)
+                q2, g2 = stacked(q[own, cols]), stacked(gmixed[own, cols])
+                state.append((j, cols, q2, g2, [part_scores(q2, k[r, cols], bias, i, part) for r, part in zip(rows, parts)]))
+            for j, cols, q2, g2, scores in state:
+                l, mean = lse[p * GROUP + j, pl.ds(i, 1), :], inner[p * GROUP + j, pl.ds(i, 1), :]
+                probs = [jnp.exp(s - l) for s in scores]
+                gs = [bf(a * (nt(v[r, cols], g2) - mean)) for a, r in zip(probs, rows)]
+                out = sum(tn(k[r, cols], g) for r, g in zip(rows, gs))
+                dq[own, cols] = bf(unstacked_t(out) * HEAD ** (-0.5))
+                at = slice(j * 2 * HEAD, (j + 1) * 2 * HEAD)
+                for r, a, g, part in zip(rows, probs, gs, parts):
+                    if part[0] is not None and part[0] < upto:
+                        continue
+                    dk_acc[r, at] += mm(g, q2)
+                    dv_acc[r, at] += mm(bf(a), g2)
+
+        by_kind(b, body, None if lent is None else jnp.where(i < span.tree - span.kind(0), lent, 0))
+
+
+def clear_rows(span, *refs):
     @pl.loop(span.start // BLOCK, (span.window + span.rows) // BLOCK)
     def _(j):
         r = rows_at(j * BLOCK, BLOCK)
-        dk_acc[r, :] = jnp.zeros((BLOCK, 2 * HEAD), jnp.float32)
-        dv_acc[r, :] = jnp.zeros((BLOCK, 2 * HEAD), jnp.float32)
-
-    @pl.loop(0, span.blocks)
-    def _(i):
-        b = span.kind(i)
-        own = rows_at(i * BLOCK, BLOCK)
-        q2, g2 = stacked(q[own, cols]), stacked(gmixed[own, cols])
-        l, mean = lse[p, pl.ds(i, 1), :], inner[p, pl.ds(i, 1), :]
-
-        def body(parts, only_own=False):
-            rows = [part_rows(span, i, b, part) for part in parts]
-            probs = [jnp.exp(part_scores(q2, k[r, cols], bias, i, part) - l) for r, part in zip(rows, parts)]
-            gs = [bf(a * (nt(v[r, cols], g2) - mean)) for a, r in zip(probs, rows)]
-            out = sum(mm(k_t[:, r], g) for r, g in zip(rows, gs))
-            dq[own, cols] = bf(unstacked_t(out) * HEAD ** (-0.5))
-            for r, a, g, part in zip(rows, probs, gs, parts):
-                if only_own and part[0] is not None:
-                    continue
-                dk_acc[r, :] += mm(g, q2)
-                dv_acc[r, :] += mm(bf(a), g2)
-
-        by_kind(b, body, None if lent is None else lent & (i < span.tree - 6))
+        for ref in refs:
+            ref[r, :] = jnp.zeros((BLOCK, ref.shape[1]), jnp.float32)
 
 
 def head_sums(gmixed, mixed, inner):
@@ -575,35 +597,39 @@
                 inner[p, i:i + 1, :] = jnp.concatenate([sums[2 * p:2 * p + 1, at], sums[2 * p + 1:2 * p + 2, at]], axis=1)
 
 
-def borrowed_back(span, p, q, g, k, v, bias, lse, inner, dk, dv):
-    cols = pair_cols(p)
-
-    @pl.loop(0, 2)
-    def _(j):
-        r = rows_at(j * BLOCK, BLOCK)
-        q2, g2 = stacked(q[r, cols]), stacked(g[r, cols])
-        l = lse[p, pl.ds(j, 1), :]
-        mean = inner[p, pl.ds(j, 1), :]
-        for part in ((0, 512, None), (512, 256, 0)):
-            rows = rows_at(span.window + part[0], part[1])
-            own = rows_at(part[0], part[1])
-            probs = jnp.exp(part_scores(q2, k[rows, cols], bias, span.blocks + j, part) - l)
-            gs = bf(probs * (nt(v[rows, cols], g2) - mean))
-            dk[own, cols] += mm(gs, q2)
-            dv[own, cols] += mm(bf(probs), g2)
-
-
-def backward_kernel(fsdp, reach, q, k, v, gmixed, mixed, lse, segs, trees, table, dq, dk, dv, wk, wv, bias, inner, k_t, dk_acc, dv_acc):
+def borrowed_back(span, p, cols, j, parts, q, g, k, v, bias, lse, inner, dk, dv):
+    join = lambda of: jnp.concatenate([of(0), of(1)], axis=0)
+    q2 = join(lambda n: stacked(q[rows_at((j + n) * BLOCK, BLOCK), cols]))
+    g2 = join(lambda n: stacked(g[rows_at((j + n) * BLOCK, BLOCK), cols]))
+    row = lambda ref: jnp.concatenate([ref[p, pl.ds(j, 1), :], ref[p, pl.ds(j + 1, 1), :]], axis=1)
+    l, mean = row(lse), row(inner)
+    base = span.base(span.blocks - 1)
+    for key, count, slot in parts:
+        rows, own = rows_at(base + key, count), rows_at(base - span.window + key, count)
+        s = nt(k[rows, cols], q2)
+        if slot is not None:
+            both = [bias[span.blocks + n, pl.ds(slot, count), :] for n in range(2)]
+            s = s + jnp.concatenate([both[0], both[0], both[1], both[1]], axis=1)
+        probs = jnp.exp(s - l)
+        gs = bf(probs * (nt(v[rows, cols], g2) - mean))
+        dk[own, cols] += mm(gs, q2)
+        dv[own, cols] += mm(bf(probs), g2)
+
+
+def backward_kernel(fsdp, reach, q, k, v, gmixed, mixed, lse, segs, trees, table, dq, dk, dv, wk, wv, bias, inner, dk_acc, dv_acc):
     span = Span(fsdp, q.shape[0], reach, lax.axis_index("fsdp"))
     make_bias(span, segs, trees, table, bias)
     head_sums(gmixed, mixed, inner)
     wk[...] = jnp.zeros_like(wk)
     wv[...] = jnp.zeros_like(wv)
 
-    @pl.loop(0, q.shape[1] // (2 * HEAD))
+    size = GROUP * 2 * HEAD
+
+    @pl.loop(0, q.shape[1] // size)
     def _(p):
-        cols = pair_cols(p)
-        attend_back_pair(span, p, q, k, v, gmixed, bias, lse, inner, k_t, dk_acc, dv_acc, dq)
+        cols = pl.ds(pl.multiple_of(p * size, size), size)
+        clear_rows(span, dk_acc, dv_acc)
+        attend_back_group(span, p, 0, span.blocks, q, k, v, gmixed, bias, lse, inner, dk_acc, dv_acc, dq)
         dk[:, cols] = dk_acc[span.window:, :]
         dv[:, cols] = dv_acc[span.window:, :]
 
@@ -621,10 +647,10 @@
     early = window - rows
     outs = (s((rows, width), low), s((rows, width), full), s((rows, width), full), s((early, width), low), s((early, width), low))
     return pl.pallas_call(
-        functools.partial(backward_kernel, fsdp, reach), out_shape=outs, in_specs=[VM] * 7 + [SM] * 2, out_specs=[VM] * 5,
+        functools.partial(backward_kernel, fsdp, reach), out_shape=outs, in_specs=[VM] * 7 + [SM, VM], out_specs=[VM] * 5,
         scratch_shapes=[
-            pltpu.VMEM((rows // BLOCK, 3 * BLOCK, BLOCK), full), pltpu.VMEM(lse.shape, full), pltpu.VMEM((2 * HEAD, window), low),
-            pltpu.VMEM((window, 2 * HEAD), full), pltpu.VMEM((window, 2 * HEAD), full),
+            pltpu.VMEM((rows // BLOCK, 3 * BLOCK, BLOCK), full), pltpu.VMEM(lse.shape, full),
+            pltpu.VMEM((window, GROUP * 2 * HEAD), full), pltpu.VMEM((window, GROUP * 2 * HEAD), full),
         ],
         compiler_params=pltpu.CompilerParams(vmem_limit_bytes=58 << 20),
     )(q, k, v, gmixed, mixed, lse, segs, trees, table)
@@ -690,7 +716,7 @@
                 stage(g)
 
 
-REDUCE_AT = (0, 1, 2, 3, 5, 6, 7)
+REDUCE_AT = (0, 1, 3, 4, 6, 7, 8)
 
 
 def reduce_steps(items, u):
@@ -744,18 +770,37 @@
     mixed, cot = m.mixed.reshape(rows, width), m.cot.reshape(rows, width)
     x, q, k, v, n1, n2, tr = m.x, m.q, m.k, m.v, m.n1, m.n2, m.tr
 
-    guest = span.kind(0) == 6
-    host = (f < last) & (lax.rem(span.first + span.blocks, span.tree) == 6)
-    gq, gg = x.at[pl.ds(0, 2 * BLOCK)], x.at[pl.ds(2 * BLOCK, 2 * BLOCK)]
+    kind, next_kind = span.kind(0), lax.rem(span.first + span.blocks, span.tree)
+    guest = kind >= 4
+    host = (f < last) & (next_kind >= 4)
+    lent_keys = jnp.where(kind == 6, 768, jnp.where(kind == 4, 512, 0))
+    size = GROUP * 2 * HEAD
+
+    def run_cols(p):
+        return pl.ds(pl.multiple_of(p * size, size), size)
 
     def lend(i, src, dst):
         return pltpu.make_async_remote_copy(src_ref=src, dst_ref=dst, send_sem=m.b_send.at[i], recv_sem=m.b_recv.at[i], device_id=(pc.r, f - 1), device_id_type=MESH)
 
-    two = pl.ds(0, 2 * BLOCK)
-    lent = [lambda: lend(0, q.at[two], gq), lambda: lend(1, m.lse, m.g_lse), lambda: lend(2, m.inner, m.g_inner)]
-
-    def lent_pair(p):
-        return lend(3 + p, m.gmixed.at[two, pair_cols(p)], gg.at[:, pair_cols(p)])
+    most = 4 * BLOCK
+    gq, gg = x.at[pl.ds(0, most)], x.at[pl.ds(most, most)]
+
+    def sized(own, act):
+        for start in (4, 6):
+            ok = (f > 0) & (kind == start) if own else (f < last) & (next_kind == start)
+
+            @pl.when(ok)
+            def _():
+                act((8 - start) * BLOCK)
+
+    def lent_q(n):
+        return lend(0, q.at[pl.ds(0, n)], gq.at[pl.ds(0, n)])
+
+    def lent_rows():
+        return [lend(1, m.lse, m.g_lse), lend(2, m.inner, m.g_inner)]
+
+    def lent_run(p, n):
+        return lend(3 + p, n2.at[pl.ds(0, n), run_cols(p)], gg.at[pl.ds(0, n), run_cols(p)])
 
     def local(src, dst, sem):
         c = pltpu.make_async_copy(src, dst, sem)
@@ -792,7 +837,7 @@
         pltpu.make_async_remote_copy(
             src_ref=m.vec.at[f], dst_ref=m.vec.at[f], send_sem=m.v_send.at[0], recv_sem=m.v_recv.at[0], device_id=pc.zdev(o), device_id_type=MESH
         ).start()
-    gat = [Gather(pc, b, m.g_send.at[i], m.g_recv.at[i], xf) for i, (b, xf) in enumerate(((m.b_q, True), (m.b_k, False), (m.b_v, True), (m.b_o, False)))]
+    gat = [Gather(pc, b, m.g_send.at[i], m.g_recv.at[i], xf, i < 3) for i, (b, xf) in enumerate(((m.b_q, True), (m.b_k, False), (m.b_v, True), (m.b_o, False)))]
     for l, g in zip(lw, gat):
         l.wait()
         g.z_start()
@@ -814,19 +859,22 @@
         lambda c: [Gather(pc, m.b_in.at[c], m.gi_send.at[c], m.gi_recv.at[c], True), Gather(pc, m.b_dn.at[c], m.gd_send.at[c], m.gd_recv.at[c], False)],
     )
 
-    make_bias(span, segs, trees, table, m.bias, jnp.where(host, 2, 0))
+    make_bias(span, segs, trees, table, m.bias, jnp.where((f < last) & (next_kind == 6), 2, 0))
+    for g in gat:
+        drain(g.three(), g.s.at[0])
+    lx.wait()
+    lf.wait()
+    for t in range(tiles):
+
+        @pl.when((f < last) & (t * tile >= next_start))
+        def _():
+            for c in window(t):
+                c.start()
+
+
     for g in gat[:3]:
         g.z_wait()
         g.a_start()
-    lx.wait()
-    lf.wait()
-    for t in range(tiles):
-
-        @pl.when((f < last) & (t * tile >= next_start))
-        def _():
-            for c in window(t):
-                c.start()
-
     v3 = m.vec.at[pl.ds(0, last)]
     drain(v3, m.v_recv.at[0])
     drain(v3, m.v_send.at[0])
@@ -859,53 +907,56 @@
     here = jnp.minimum(here, span.blocks)
     border = span.base(here)
 
-    @pl.loop(0, pairs)
+    groups = pairs // GROUP
+
+    @pl.loop(0, groups)
     def _(p):
-        attend_pair(span, p, here, span.blocks, border, 2 * rows, q, k, v, m.bias, m.turned, mixed, m.lse)
-        @pl.when(p >= pairs // 2)
-        def _():
-            for j in range(2):
-                c = 2 * (p - pairs // 2) + j
-                own_chunk(c, lambda d: d.wait())
-                for g in ff(c):
-                    g.z_start()
+        attend_group(span, p, here, span.blocks, q, k, v, m.bias, mixed, m.lse)
 
     for t in range(tiles):
 
+        @pl.when((f < last) & (t * tile >= next_start))
+        def _():
+            for c in window(t):
+                c.wait_send()
+
+    @pl.loop(0, n_ff)
+    def _(c):
+        own_chunk(c, lambda d: d.wait())
+        for g in ff(c):
+            g.z_start()
+
+    for stage in Gather.STAGES[:3]:
+        stage(gat[3])
+
+    for t in range(tiles):
+
         @pl.when(t * tile >= span.start)
         def _():
-            drain(x.at[pl.ds(t * tile, tile)], m.w_recv.at[0, t])
-            drain(v.at[pl.ds(t * tile, tile), pl.ds(half, half)], m.w_recv.at[1, t])
-
-    @pl.loop(span.start // tile, tiles)
-    def _(t):
-        r = rows_at(t * tile, tile)
-        n = norm_tile(x[r, :], gain, shift)
-        k[r, :] = bf(mm(n, w_k[...]))
-        v[r, :half] = bf(mm(n, w_v[:, :half]))
-
-
-    @pl.loop(0, pairs)
-    def _(p):
-        attend_pair(span, p, 0, here, span.start, border, q, k, v, m.bias, m.turned, mixed, m.lse)
-
-        for s, stage in enumerate(Gather.STAGES[:3]):
-
-            @pl.when(p == s)
-            def _():
-                stage(gat[3])
-
-        gather_steps(ff, p - 2)
-
-    @pl.when(guest)
-    def _():
-        lent[0]().start()
-        lent[1]().start()
+            r = pl.ds(t * tile, tile)
+            drain(x.at[r], m.w_recv.at[0, t])
+            drain(v.at[r, pl.ds(half, half)], m.w_recv.at[1, t])
+            n = norm_tile(x[r, :], gain, shift)
+            k[r, :] = bf(mm(n, w_k[...]))
+            v[r, :half] = bf(mm(n, w_v[:, :half]))
+
+
+    @pl.loop(0, 2 * groups)
+    def _(s):
+        p, part = s // 2, lax.rem(s, 2)
+        middle = here // 2
+        attend_group(span, p, part * middle, jnp.where(part == 0, middle, here), q, k, v, m.bias, mixed, m.lse)
+        gather_steps(ff, s - 2 * groups + 2)
 
     gat[3].c_wait()
     branch_out(span, x, m.lnp, mixed, w_o, m.resid, n2)
+    @pl.when(host)
+    def _():
+        pl.semaphore_signal(m.freed, inc=1, device_id=(pc.r, f + 1), device_id_type=MESH)
+
+    gather_steps(ff, 2)
     for g in gat:
-        g.finish()
+        g.finish(1)
 
     lc.wait()
     transpose_all(n2, tr)
@@ -922,7 +973,6 @@
 
     @pl.loop(0, n_ff)
     def _(c):
-        gather_steps(ff, c + pairs - 2)
         for g in ff(c):
             Gather.STAGES[3](g)
 
@@ -934,8 +984,14 @@
         def put_dn(val):
             b_dn[...] = val
 
-        mlp_chunk(rows, n2, tr, cot, lambda: b_in[...], lambda: b_dn[...], m.acc1, m.acc2, hid, gact, put_in, put_dn)
+        mlp_chunk(rows, n2, tr, cot, lambda: b_in[...], lambda: b_dn[...], m.acc1, m.acc2, hid, gact, put_in, put_dn, lambda: gather_steps(ff, c + 3))
         reduce_steps(red, c)
+
+        @pl.when(guest & (c == 2))
+        def _():
+            pl.semaphore_wait(m.freed, 1)
+            sized(True, lambda n: lent_q(n).start())
+
 
     @pl.loop(0, tiles)
     def _(t):
@@ -945,50 +1001,43 @@
     lo = local(m.back.at[0], outputs, m.l_sem.at[0])
     m.sums[...] = jnp.zeros_like(m.sums)
     second_norm_back(rows, m.lnp, m.resid, cot, m.acc2, m.resid, n2, m.sums)
-    branch_back(rows, n2, w_o, m.gmixed)
-    head_sums(m.gmixed, mixed, m.inner)
-
-    @pl.when(guest)
-    def _():
-        lent[2]().start()
-        for p in range(pairs):
-            lent_pair(p).start()
-
+    d_o = flat(m.cot)
 
     @pl.loop(0, width // tile)
     def _(t):
         r = rows_at(t * tile, tile)
-        w_o[r, :] = bf(tn(mixed[:, pl.ds(pl.multiple_of(t * tile, tile), tile)], n2[...]))
-
+        d_o[r, :] = bf(tn(mixed[:, pl.ds(pl.multiple_of(t * tile, tile), tile)], n2[...]))
+
+    gmixed = n2
+    branch_back(rows, n2, w_o, gmixed)
+    head_sums(gmixed, mixed, m.inner)
+
+    @pl.when(guest)
+    def _():
+        for c in lent_rows():
+            c.start()
+
+    sized(True, lambda n: lent_run(0, n).start())
     lo.wait()
 
     @pl.when((f < last) & jnp.logical_not(host))
     def _():
         pl.semaphore_signal(m.ready, inc=1, device_id=(pc.r, f + 1), device_id_type=MESH)
 
-    for t in range(tiles):
-
-        @pl.when((f < last) & (t * tile >= next_start))
-        def _():
-            for c in window(t):
-                c.wait_send()
-
-    @pl.when(guest)
-    def _():
-        lent[0]().wait_send()
+    sized(True, lambda n: lent_q(n).wait_send())
 
     transpose_all(n1, tr)
-    mid, end = half + (pairs // 2 - 1) * BLOCK, width
+    mid, end = half + (pairs // 2 - GROUP) * BLOCK, width
     wide = 2 * (mid - half)
-    rest = lambda ref: (ref.at[..., pl.ds(0, wide)], ref.at[..., pl.ds(wide, 2 * BLOCK)])
-    narrow = lambda refs, i: [ref.at[..., pl.ds(0, wide // 2) if i == 0 else pl.ds(wide // 2, BLOCK)] for ref in refs]
-    buf1, buf2 = rest(m.cot)
+    rest = lambda ref: (ref.at[..., pl.ds(0, wide)], ref.at[..., pl.ds(wide, width - wide)])
+    narrow = lambda refs, i: [ref.at[..., pl.ds(0, wide // 2) if i == 0 else pl.ds(wide // 2, half - wide // 2)] for ref in refs]
+    buf1, buf2 = rest(m.b_o)
     res1, res2 = rest(rs_k)
     stat = [
         Reduce(pc, b, *scr, res, m.rs_send.at[i], m.rs_recv.at[i], xf)
         for i, (b, scr, res, xf) in enumerate(
             (
-                (m.b_o, m.r_o, rs_o, True), (m.mixed, m.r_q, rs_q, False), (m.g_v, m.r_v, rs_v, True),
+                (m.cot, m.r_o, rs_o, True), (m.mixed, m.r_q, rs_q, False), (m.g_v, m.r_v, rs_v, True),
                 (buf1, narrow(m.r_k, 0), res1, True), (buf2, narrow(m.r_k, 1), res2, False),
             )
         )
@@ -996,7 +1045,7 @@
     red_o, red_0, red_v, red_1, red_2 = stat
 
     def early(t, p):
-        r, cols = pl.ds(t * tile, tile), pair_cols(p)
+        r, cols = pl.ds(t * tile, tile), run_cols(p)
         prev = (pc.r, f - 1)
         return [
             pltpu.make_async_remote_copy(
@@ -1008,20 +1057,21 @@
 
     dk, dv = m.acc1, m.acc2
 
-    def complete(p):
-        cols = pl.ds(p * BLOCK, BLOCK)
+    def complete(g):
+        cols = pl.ds(g * size, size)
+        fresh = min(size, max(0, half - g * size))
         for t in range(tiles):
             r = pl.ds(t * tile, tile)
 
             @pl.when((f < last) & jnp.logical_not(host) & (t * tile >= next_start))
             def _():
                 for j, own in enumerate((dk, dv)):
-                    drain(m.back.at[j, r, cols], m.e_recv.at[j, p, t])
+                    drain(m.back.at[j, r, cols], m.e_recv.at[j, g, t])
                     own[r, cols] += f32(m.back[j, r, cols])
 
             k[r, cols] = bf(dk[r, cols])
-            if p < pairs // 2:
-                v[r, cols] = bf(dv[r, cols])
+            if fresh:
+                v[r, g * size:g * size + fresh] = bf(dv[r, g * size:g * size + fresh])
 
     def weight_grad(dst, at, grad, lo, hi):
         @pl.loop(0, width // tile)
@@ -1029,11 +1079,11 @@
             r = rows_at(t * tile, tile)
             dst[r, at:at + hi - lo] = bf(mm(tr[r, :], grad[pl.ds(0, rows), lo:hi]))
 
-    d_0, d_v, d_1 = flat(m.mixed), flat(m.g_v), flat(m.cot)
+    d_0, d_v, d_1 = flat(m.mixed), flat(m.g_v), w_o
 
     def run_0():
-        for p in range(pairs // 2):
-            complete(p)
+        complete(0)
+        complete(1)
         weight_grad(d_0, 0, q, 0, half)
         weight_grad(d_0, half, k, 0, half)
         red_0.p1()
@@ -1041,65 +1091,94 @@
         weight_grad(d_v, 0, v, 0, half)
         red_v.p1()
 
-    @pl.loop(0, pairs)
-    def _(p):
-        cols = pair_cols(p)
-        attend_back_pair(span, p, q, k, v, m.gmixed, m.bias, m.lse, m.inner, m.turned, m.dk_acc, m.dv_acc, q, guest)
-        dk[:, cols] = m.dk_acc[rows:, :]
-        dv[:, cols] = m.dv_acc[rows:, :]
-
-        @pl.when((p == 0) & (f > 0) & jnp.logical_not(guest))
-        def _():
-            pl.semaphore_wait(m.ready, 1)
-
-        for t in range(tiles):
-
-            @pl.when((f > 0) & jnp.logical_not(guest) & (t * tile >= span.start))
+    @pl.loop(0, 2 * groups)
+    def _(s):
+        p, part = s // 2, lax.rem(s, 2)
+        cols = run_cols(p)
+        middle = span.blocks // 2
+
+        @pl.when(part == 0)
+        def _():
+            clear_rows(span, m.dk_acc, m.dv_acc)
+
+        attend_back_group(
+            span, p, part * middle, jnp.where(part == 0, middle, span.blocks), q, k, v, gmixed, m.bias, m.lse, m.inner, m.dk_acc, m.dv_acc, q, lent_keys
+        )
+
+        reduce_steps(red, n_ff + s)
+
+        @pl.when((part == 0) & (p < groups - 1))
+        def _():
+            sized(True, lambda n: lent_run(p + 1, n).start())
+
+        @pl.when(s == 1)
+        def _():
+            @pl.when((f > 0) & jnp.logical_not(guest))
             def _():
-                r = pl.ds(t * tile, tile)
-                x[r, cols] = bf(m.dk_acc[r, :])
-                x[pl.ds(rows + t * tile, tile), cols] = bf(m.dv_acc[r, :])
-                for c in early(t, p):
-                    c.start()
-
-        reduce_steps(red, n_ff + p)
-
-        @pl.when(host)
+                pl.semaphore_wait(m.ready, 1)
+
+        @pl.when(part == 1)
+        def _():
+            dk[:, cols] = m.dk_acc[rows:, :]
+            dv[:, cols] = m.dv_acc[rows:, :]
+            for t in range(tiles):
+
+                @pl.when((f > 0) & jnp.logical_not(guest) & (t * tile >= span.start))
+                def _():
+                    r = pl.ds(t * tile, tile)
+                    x[r, cols] = bf(m.dk_acc[r, :])
+                    x[pl.ds(rows + t * tile, tile), cols] = bf(m.dv_acc[r, :])
+                    for c in early(t, p):
+                        c.start()
+
+        @pl.when(host & (part == 1))
         def _():
             @pl.when(p == 0)
             def _():
-                for c in lent:
-                    c().wait_recv()
-
-            lent_pair(p).wait_recv()
-            borrowed_back(span, p, gq, gg, k, v, m.bias, m.g_lse, m.g_inner, dk, dv)
-
-        for s in range(5):
-
-            @pl.when(p == REDUCE_AT[s])
+                sized(False, lambda n: lent_q(n).wait_recv())
+                for c in lent_rows():
+                    c.wait_recv()
+
+            sized(False, lambda n: lent_run(p, n).wait_recv())
+            for j in range(GROUP):
+                at = (span, p * GROUP + j, group_cols(p, j, GROUP))
+                rest = (gq, gg, k, v, m.bias, m.g_lse, m.g_inner, dk, dv)
+                trunk = ((0, 256, None), (256, 256, None))
+
+                @pl.when(next_kind == 6)
+                def _():
+                    borrowed_back(*at, 0, (*trunk, (512, 256, 0)), *rest)
+
+                @pl.when(next_kind == 4)
+                def _():
+                    @pl.loop(0, 2)
+                    def _(n):
+                        borrowed_back(*at, 2 * n, trunk, *rest)
+
+        for i in range(4):
+
+            @pl.when(s == REDUCE_AT[i])
             def _():
-                Reduce.STAGES[s](red_o)
-
-        @pl.when(p == pairs - 2)
+                Reduce.STAGES[i](red_o)
+
+        @pl.when(s == 2 * groups - 2)
         def _():
             run_0()
 
-        @pl.when(p == pairs - 1)
+        @pl.when(s == 2 * groups - 1)
         def _():
             red_0.p2()
             red_v.p2()
 
-    for p in range(pairs // 2, pairs - 1):
-        complete(p)
     weight_grad(d_1, 0, q, half, mid)
     weight_grad(d_1, mid - half, k, half, mid)
     red_1.p1()
     weight_grad(d_1, wide, q, mid, end)
     red_0.p3()
     red_v.p3()
-    red_o.p6()
-    complete(pairs - 1)
-    weight_grad(d_1, wide + BLOCK, k, mid, end)
+    red_o.p5()
+    complete(groups - 1)
+    weight_grad(d_1, wide + end - mid, k, mid, end)
     red_2.p1()
     gf = local(dv.at[:, pl.ds(half, half)], gfirst, m.l_sem.at[1])
     lx = local(inputs, n1, m.l_sem.at[2])
@@ -1116,7 +1195,7 @@
     red_2.p3()
     red_1.p3()
     reduce_steps(red, n_ff + pairs)
-    red_o.p7()
+    red_o.p6()
     lx.wait()
 
     @pl.loop(0, tiles)
@@ -1150,6 +1229,7 @@
         exchange(cur, m.s_z.at[f], 4, pc.zdev(o))
     red_2.p6()
     red_1.p6()
+    red_o.p7()
     for u in range(n_ff + pairs + 1, n_ff + REDUCE_AT[-1]):
         reduce_steps(red, u)
     red_2.p7()
@@ -1169,7 +1249,7 @@
             g.p8()
             g.finish()
 
-    @pl.loop(0, pairs)
+    @pl.loop(0, groups)
     def _(p):
         for t in range(tiles):
 
@@ -1178,13 +1258,13 @@
                 for c in early(t, p):
                     c.wait_send()
 
-    @pl.when(guest)
-    def _():
-        for c in lent[1:]:
-            c().wait_send()
-        for p in range(pairs):
-            lent_pair(p).wait_send()
-
+    def sent(n):
+        for c in lent_rows():
+            c.wait_send()
+        for p in range(groups):
+            lent_run(p, n).wait_send()
+
+    sized(True, sent)
     gf.wait()
     gi.wait()
 
@@ -1206,14 +1286,13 @@
         ("b_q", buf(mq, width)), ("b_k", buf(mq, width)), ("b_v", buf(mq, wide_v)), ("b_o", buf(mq, width)),
         ("b_in", buf(mq, chunk, (n_ff,))), ("b_dn", buf(md, width, (n_ff,))), ("g_v", buf(mq, wide_v)),
         ("mixed", buf(mq, width)), ("cot", buf(mq, width)), ("x", (2 * rows, width)), ("k", (2 * rows, width)), ("v", (2 * rows, width)),
-        ("q", (rows, width)), ("n1", (rows, width)), ("n2", (rows, width)), ("tr", (width, rows)), ("gmixed", (rows, width)), ("back", (2, rows, width)),
-        ("turned", (2 * HEAD, 2 * rows)),
+        ("q", (rows, width)), ("n1", (rows, width)), ("n2", (rows, width)), ("tr", (width, rows)), ("back", (2, rows, width)),
     ):
         sc.add(name, V(shape, low))
     for name, shape in (
         ("vec", (fsdp, 8, width)), ("lnp", (8, width)), ("sums", (8, width)), ("s_pair", (3, 8, width)), ("s_z", (fsdp, 8, width)),
         ("resid", (rows, width)), ("acc1", (rows, width)), ("acc2", (rows, width)), ("bias", (blocks + 2, 3 * BLOCK, BLOCK)), ("inner", (pairs, 8, 2 * BLOCK)), ("g_inner", (pairs, 8, 2 * BLOCK)), ("g_lse", (pairs, -(-blocks // 8) * 8, 2 * BLOCK)),
-        ("dk_acc", (2 * rows, 2 * HEAD)), ("dv_acc", (2 * rows, 2 * HEAD)), ("lse", (pairs, -(-blocks // 8) * 8, 2 * BLOCK)),
+        ("dk_acc", (2 * rows, GROUP * 2 * HEAD)), ("dv_acc", (2 * rows, GROUP * 2 * HEAD)), ("lse", (pairs, -(-blocks // 8) * 8, 2 * BLOCK)),
     ):
         sc.add(name, V(shape, full))
     for name, shape in (
@@ -1221,10 +1300,11 @@
         ("w_send", (2, rows // row_tiles(rows))), ("w_recv", (2, rows // row_tiles(rows))),
         ("gi_send", (n_ff, 5)), ("gi_recv", (n_ff, 5)), ("gd_send", (n_ff, 5)), ("gd_recv", (n_ff, 5)),
         ("ri_send", (n_ff, 8)), ("ri_recv", (n_ff, 8)), ("rd_send", (n_ff, 8)), ("rd_recv", (n_ff, 8)), ("rs_send", (5, 8)), ("rs_recv", (5, 8)),
-        ("b_send", (3 + pairs,)), ("b_recv", (3 + pairs,)), ("e_send", (2, pairs, rows // row_tiles(rows))), ("e_recv", (2, pairs, rows // row_tiles(rows))),
+        ("b_send", (3 + pairs,)), ("b_recv", (3 + pairs,)), ("e_send", (2, pairs // GROUP, rows // row_tiles(rows))), ("e_recv", (2, pairs // GROUP, rows // row_tiles(rows))),
     ):
         sc.add(name, D(shape))
     sc.add("ready", pltpu.SemaphoreType.REGULAR)
+    sc.add("freed", pltpu.SemaphoreType.REGULAR)
     groups = (("r_in", buf(mq, chunk), n_ff), ("r_dn", buf(md, width), n_ff), ("r_o", buf(mq, width), 0), ("r_q", buf(mq, width), 0), ("r_k", buf(mq, width), 0), ("r_v", buf(mq, wide_v), 0))
     for name, shape, lead in groups:
         for i, sub in enumerate(red_shapes(shape)):
@@ -1248,7 +1328,7 @@
 
     any_ = pl.BlockSpec(memory_space=pl.ANY)
     return pl.pallas_call(
-        body, out_shape=outs, in_specs=[any_] * 9 + [VM] * 2 + [SM] * 2, out_specs=[any_] * 3 + [VM] * 7, scratch_shapes=sc.shapes,
+        body, out_shape=outs, in_specs=[any_] * 9 + [VM] * 2 + [SM, VM], out_specs=[any_] * 3 + [VM] * 7, scratch_shapes=sc.shapes,
         compiler_params=pltpu.CompilerParams(collective_id=3, has_side_effects=True, vmem_limit_bytes=63 << 20),
     )(inputs, first, cot, split(w_query), split(w_key), split(w_value), split(w_out), split(w_in), w_down.reshape(n_ff, 2, 2, md, width), norms, segs, trees, table)
 
@@ -1288,12 +1368,13 @@
     done(1, d_dn)
     loads[2].wait()
     loads[3].wait()
-    rest = half - BLOCK
+    rest = half - GROUP * BLOCK
+    tail = half - rest
     for i, mid in ((2, d_q), (3, d_k)):
         s = i - 2
         mid[:, :half] = f32(l_0[:, s * half:(s + 1) * half])
         mid[:, half:half + rest] = f32(l_1[:, s * rest:(s + 1) * rest])
-        mid[:, half + rest:] = f32(l_1[:, 2 * rest + s * BLOCK:2 * rest + (s + 1) * BLOCK])
+        mid[:, half + rest:] = f32(l_1[:, 2 * rest + s * tail:2 * rest + (s + 1) * tail])
         done(i, mid)
     loads[4].wait()
     d_o[...] = f32(l_o[...])

time: 231 us -> 224 us (0.970)
  Pallas kernels: 226 us -> 219 us
    pallas_call x1, Pallas kernels: 218 us -> 211 us  [layer_call(): pl.pallas_call(body, out_shape=outs, in_specs=[any_] * 9 + [VM] * 2 + [SM...]
where the time goes in v5:
time: 224 us; the launch traced here: 223 us
  Pallas kernels  219 us (98%)
  local copies, waits for them, and re-layouts  3.48 us (2%)
    pallas_call x1, Pallas kernels, layer_call(): pl.pallas_call(body, out_shape=outs, in_specs=[any_] * 9 + [VM] * 2 + [SM...  211 us
    pallas_call x1, Pallas kernels, finish_call(): pl.pallas_call(finish_kernel, out_shape=(s(outputs.shape, outputs.dtype),...  7.68 us

profile of v5, /device:TPU:0, one launch (start us, length us, event | category | flops | bytes accessed | tf_op | source)
XLA Modules:
  0.0 223.5 jit_solution(6617118144947655399)
XLA Ops:
  0.6 0.8 pad_maximum_fusion
  1.4 0.7 reshape.74.refs_9_
  2.1 1.4 copy.29.refs_12_
  3.5 210.8 %shard_map.255 = (bf16[768,768]{1,0:T(8,128)(2,1)}, f32[768,768]{1,0:T(8,128)}, f32[768,384]{1,0:T(8,128)}, bf16[2,2,48,768]{3,2,1,0:T(8,128)(2,1)}, bf16[2,2,48...) custom-call(bf16[768,768]{1,0:T(8,128)(2,1)} %refs_0_.1, ...), custom_call_target="tpu_custom_call" | custom-call | tf_op jit(solution)/shard_map/pallas_call | solution.py:1330
  214.3 7.7 %shard_map.256 = (bf16[768,768]{1,0:T(8,128)(2,1)}, f32[768,768]{1,0:T(8,128)}, f32[768,384]{1,0:T(8,128)}, f32[192,3072]{1,0:T(8,128)}, f32[768,768]{1,0:T(8,12...) custom-call(bf16[768,768]{1,0:T(8,128)(2,1)} %get-tuple-element.33.o, ...), custom_call_target="tpu_custom_call" | custom-call | tf_op jit(solution)/shard_map/pallas_call | solution.py:1399
  222.0 1.4 fusion

commit v6 on v5

--- a/solution.py
+++ b/solution.py
@@ -716,7 +716,7 @@
                 stage(g)
 
 
-REDUCE_AT = (0, 1, 3, 4, 6, 7, 8)
+REDUCE_AT = (0, 1, 3, 5, 7, 8, 9)
 
 
 def reduce_steps(items, u):

time: 224 us -> 219 us (0.978)
  Pallas kernels: 219 us -> 213 us
    pallas_call x1, Pallas kernels: 211 us -> 205 us  [layer_call(): pl.pallas_call(body, out_shape=outs, in_specs=[any_] * 9 + [VM] * 2 + [SM...]
where the time goes in v6:
time: 219 us; the launch traced here: 218 us
  Pallas kernels  213 us (97%)
  local copies, waits for them, and re-layouts  3.48 us (2%)
    pallas_call x1, Pallas kernels, layer_call(): pl.pallas_call(body, out_shape=outs, in_specs=[any_] * 9 + [VM] * 2 + [SM...  205 us
    pallas_call x1, Pallas kernels, finish_call(): pl.pallas_call(finish_kernel, out_shape=(s(outputs.shape, outputs.dtype),...  7.68 us

profile of v6, /device:TPU:0, one launch (start us, length us, event | category | flops | bytes accessed | tf_op | source)
XLA Modules:
  0.0 218.0 jit_solution(7418309921958140132)
XLA Ops:
  0.6 0.8 pad_maximum_fusion
  1.4 0.7 reshape.74.refs_9_
  2.1 1.4 copy.29.refs_12_
  3.5 205.3 %shard_map.255 = (bf16[768,768]{1,0:T(8,128)(2,1)}, f32[768,768]{1,0:T(8,128)}, f32[768,384]{1,0:T(8,128)}, bf16[2,2,48,768]{3,2,1,0:T(8,128)(2,1)}, bf16[2,2,48...) custom-call(bf16[768,768]{1,0:T(8,128)(2,1)} %refs_0_.1, ...), custom_call_target="tpu_custom_call" | custom-call | tf_op jit(solution)/shard_map/pallas_call | solution.py:1330
  208.8 7.7 %shard_map.256 = (bf16[768,768]{1,0:T(8,128)(2,1)}, f32[768,768]{1,0:T(8,128)}, f32[768,384]{1,0:T(8,128)}, f32[192,3072]{1,0:T(8,128)}, f32[768,768]{1,0:T(8,12...) custom-call(bf16[768,768]{1,0:T(8,128)(2,1)} %get-tuple-element.33.o, ...), custom_call_target="tpu_custom_call" | custom-call | tf_op jit(solution)/shard_map/pallas_call | solution.py:1399
  216.5 1.4 fusion
